TPU v7x, 32 devices: a whole 2x2x4 slice. The times are simulated.
32 devices in a mesh: dp: 8 (over y, x, core), seq: 4 (over z).
Axes of the slice: x: 2, y: 2, z: 4, core: 2. Of those that a mesh axis runs over, the one named last changes fastest.
Arguments:
- layer_input: bfloat16 [16, 512, 768], P('dp', 'seq'), may hold values from -6 to 6
- segment_ids: int32 [16, 512], P('dp', 'seq'), may hold values from 0 to 2, as said below
- w_query: bfloat16 [768, 768], replicated, may hold values from -0.21875 to 0.21875
- b_query: float32 [768], replicated, may hold values from -1.5 to 1.5
- w_key: bfloat16 [768, 768], replicated, may hold values from -0.21875 to 0.21875
- w_value: bfloat16 [768, 768], replicated, may hold values from -0.21875 to 0.21875
- b_value: float32 [768], replicated, may hold values from -1.5 to 1.5
- w_out: bfloat16 [768, 768], replicated, may hold values from -1.75 to 1.75
- b_out: float32 [768], replicated, may hold values from -1.5 to 1.5
- gain_one: float32 [768], replicated, may hold values from 0.5 to 1.5
- shift_one: float32 [768], replicated, may hold values from -1.5 to 1.5
- w_inner: bfloat16 [768, 3072], replicated, may hold values from -0.21875 to 0.21875
- b_inner: float32 [3072], replicated, may hold values from -1.5 to 1.5
- w_outer: bfloat16 [3072, 768], replicated, may hold values from -0.109375 to 0.109375
- b_outer: float32 [768], replicated, may hold values from -1.5 to 1.5
- gain_two: float32 [768], replicated, may hold values from 0.5 to 1.5
- shift_two: float32 [768], replicated, may hold values from -1.5 to 1.5
- cotangent: bfloat16 [16, 512, 768], P('dp', 'seq'), may hold values from -6 to 6
Outputs:
- output: bfloat16 [16, 512, 768], P('dp', 'seq')
- d_input: bfloat16 [16, 512, 768], P('dp', 'seq')
- d_w_query: float32 [768, 768], replicated
- d_b_query: float32 [768], replicated
- d_w_key: float32 [768, 768], replicated
- d_w_value: float32 [768, 768], replicated
- d_b_value: float32 [768], replicated
- d_w_out: float32 [768, 768], replicated
- d_b_out: float32 [768], replicated
- d_gain_one: float32 [768], replicated
- d_shift_one: float32 [768], replicated
- d_w_inner: float32 [768, 3072], replicated
- d_b_inner: float32 [3072], replicated
- d_w_outer: float32 [3072, 768], replicated
- d_b_outer: float32 [768], replicated
- d_gain_two: float32 [768], replicated
- d_shift_two: float32 [768], replicated
Inputs may be any that keep to these rules, and one draw needn't show every extreme that they name: `segment_ids`: each row holds either one pair (ids 1, then 0 for padding at its end) of more than 256 tokens, or two pairs packed in halves of 256 positions (ids 1 in the first half, 2 in the second, each followed by padding 0 in its half), each of 128 tokens or more. Some row is a single pair without padding, some row is packed with padding.
All inputs are finite; a program needn't handle non-finite values.
Results may differ from a plain program's by a relative error of at most 0.015.
Values may be sent and summed in bfloat16 or wider, within the bound.
A program may use at most 192 MiB of HBM per device.

v0:
```python
import math

import jax
import jax.numpy as jnp
from jax import lax
from jax.sharding import PartitionSpec as P

HD = 64


EPSILON = 1e-12
MASKED = -1000000000.0
INV_ROOT_TWO = 0.7071067811865476
DENSITY = 0.3989422804014327


def product(left, right):
    return jnp.dot(left, right, preferred_element_type=jnp.float32)


def product_tn(left, right):
    return lax.dot_general(
        left, right, (((0,), (0,)), ((), ())), preferred_element_type=jnp.float32
    )


def product_nt(left, right):
    return lax.dot_general(
        left, right, (((1,), (1,)), ((), ())), preferred_element_type=jnp.float32
    )


def layer_norm(values, scale_gain, offset):
    centre = values - jnp.mean(values, axis=-1, keepdims=True)
    inverse_std = lax.rsqrt(jnp.mean(centre * centre, axis=-1, keepdims=True) + EPSILON)
    normed = centre * inverse_std
    return (normed * scale_gain + offset, normed, inverse_std)


def norm_back(grad_out, normed, inverse_std, scale_gain):
    scaled = grad_out * scale_gain
    return inverse_std * (
        scaled
        - jnp.mean(scaled, axis=-1, keepdims=True)
        - normed * jnp.mean(scaled * normed, axis=-1, keepdims=True)
    )


def split_heads(tensor):
    return tensor.reshape(tensor.shape[0], tensor.shape[1], tensor.shape[2] // HD, HD)


def grouped(tensor, group):
    return tensor.reshape((tensor.shape[0] // group, group) + tensor.shape[1:])


def ungrouped(tensor):
    return tensor.reshape((tensor.shape[0] * tensor.shape[1],) + tensor.shape[2:])


def masked_scores(query_rows, key_rows, query_segs, key_segs):
    scores = (
        jnp.einsum(
            "rqhd,rkhd->rhqk",
            split_heads(query_rows),
            split_heads(key_rows),
            preferred_element_type=jnp.float32,
        )
        * 0.125
    )
    same_pair = query_segs[:, None, :, None] == key_segs[:, None, None, :]
    return jnp.where(same_pair, scores, MASKED)


def attend(packed_item):
    query_rows, key_rows, value_rows, query_segs, key_segs = packed_item
    scores = masked_scores(query_rows, key_rows, query_segs, key_segs)
    row_max = jnp.max(scores, axis=-1, keepdims=True)
    powers = jnp.exp(scores - row_max)
    totals = jnp.sum(powers, axis=-1, keepdims=True)
    soft_probs = (powers / totals).astype(jnp.bfloat16)
    attended = jnp.einsum(
        "rhqk,rkhd->rqhd", soft_probs, split_heads(value_rows), preferred_element_type=jnp.float32
    )
    return (attended.reshape(query_rows.shape), (row_max + jnp.log(totals))[..., 0])


def attend_back(packed_item):
    query_rows, key_rows, value_rows, query_segs, key_segs, log_total, grad_attn, attended = (
        packed_item
    )
    scores = masked_scores(query_rows, key_rows, query_segs, key_segs)
    probs = jnp.exp(scores - log_total[..., None])
    grad_heads = split_heads(grad_attn)
    delta = jnp.sum(grad_heads.astype(jnp.float32) * split_heads(attended), axis=-1)
    delta = jnp.swapaxes(delta, 1, 2)[..., None]
    grad_prob = jnp.einsum(
        "rqhd,rkhd->rhqk", grad_heads, split_heads(value_rows), preferred_element_type=jnp.float32
    )
    grad_scores = (probs * (grad_prob - delta)).astype(jnp.bfloat16)
    grad_query = (
        jnp.einsum(
            "rhqk,rkhd->rqhd",
            grad_scores,
            split_heads(key_rows),
            preferred_element_type=jnp.float32,
        )
        * 0.125
    )
    grad_keys = (
        jnp.einsum(
            "rhqk,rqhd->rkhd",
            grad_scores,
            split_heads(query_rows),
            preferred_element_type=jnp.float32,
        )
        * 0.125
    )
    grad_values = jnp.einsum(
        "rhqk,rqhd->rkhd",
        probs.astype(jnp.bfloat16),
        grad_heads,
        preferred_element_type=jnp.float32,
    )
    return (
        grad_query.reshape(query_rows.shape),
        grad_keys.reshape(key_rows.shape),
        grad_values.reshape(key_rows.shape),
    )


def on_device(
    layer_input,
    segment_ids,
    w_query,
    b_query,
    w_key,
    w_value,
    b_value,
    w_out,
    b_out,
    gain_one,
    shift_one,
    w_inner,
    b_inner,
    w_outer,
    b_outer,
    gain_two,
    shift_two,
    cotangent,
):
    row_count, shard_len, model_dim = layer_input.shape
    tok_count = row_count * shard_len
    tokens = layer_input.reshape(tok_count, model_dim)
    query_flat = (product(tokens, w_query) + b_query).astype(jnp.bfloat16)
    key_flat = product(tokens, w_key).astype(jnp.bfloat16)
    value_flat = (product(tokens, w_value) + b_value).astype(jnp.bfloat16)
    stacked = jnp.stack([key_flat, value_flat]).reshape(2, row_count, shard_len, model_dim)
    context, seg_context = (
        lax.all_gather(stacked, "seq", axis=2, tiled=True),
        lax.all_gather(segment_ids, "seq", axis=1, tiled=True),
    )
    group = math.gcd(row_count, max(1, 512 // shard_len))
    query_grid = grouped(query_flat.reshape(row_count, shard_len, model_dim), group)
    query_segs = grouped(segment_ids, group)
    key_segs = grouped(seg_context, group)
    attn_grid, log_total = lax.map(
        attend,
        (query_grid, grouped(context[0], group), grouped(context[1], group), query_segs, key_segs),
    )
    attn_low = ungrouped(attn_grid).reshape(tok_count, model_dim).astype(jnp.bfloat16)
    branch = product(attn_low, w_out) + b_out
    hidden_one, normed_one, inverse_one = layer_norm(
        tokens.astype(jnp.float32) + branch, gain_one, shift_one
    )
    hidden_low = hidden_one.astype(jnp.bfloat16)
    inner_pre = product(hidden_low, w_inner) + b_inner
    cdf_part = 0.5 * (1.0 + lax.erf(inner_pre * INV_ROOT_TWO))
    active_low = (inner_pre * cdf_part).astype(jnp.bfloat16)
    outer_out = product(active_low, w_outer) + b_outer
    result, normed_two, inverse_two = layer_norm(hidden_one + outer_out, gain_two, shift_two)
    grad_out = cotangent.reshape(tok_count, model_dim).astype(jnp.float32)
    grad_gain_two = jnp.sum(grad_out * normed_two, axis=0)
    grad_shift_two = jnp.sum(grad_out, axis=0)
    grad_two = norm_back(grad_out, normed_two, inverse_two, gain_two)
    grad_outer = grad_two.astype(jnp.bfloat16)
    grad_w_outer = product_tn(active_low, grad_outer)
    grad_b_outer = jnp.sum(grad_outer.astype(jnp.float32), axis=0)
    grad_active = product_nt(grad_outer, w_outer)
    slope = cdf_part + inner_pre * DENSITY * jnp.exp(-0.5 * inner_pre * inner_pre)
    grad_inner = (grad_active * slope).astype(jnp.bfloat16)
    grad_w_inner = product_tn(hidden_low, grad_inner)
    grad_b_inner = jnp.sum(grad_inner.astype(jnp.float32), axis=0)
    grad_hidden = grad_two + product_nt(grad_inner, w_inner)
    grad_gain_one = jnp.sum(grad_hidden * normed_one, axis=0)
    grad_shift_one = jnp.sum(grad_hidden, axis=0)
    grad_one = norm_back(grad_hidden, normed_one, inverse_one, gain_one)
    grad_branch = grad_one.astype(jnp.bfloat16)
    grad_w_out = product_tn(attn_low, grad_branch)
    grad_b_out = jnp.sum(grad_branch.astype(jnp.float32), axis=0)
    grad_attn = product_nt(grad_branch, w_out).astype(jnp.bfloat16)
    grad_attn_grid = grouped(grad_attn.reshape(row_count, shard_len, model_dim), group)
    query_part, key_part, value_part = lax.map(
        attend_back,
        (
            query_grid,
            grouped(context[0], group),
            grouped(context[1], group),
            query_segs,
            key_segs,
            log_total,
            grad_attn_grid,
            attn_grid,
        ),
    )
    key_home, value_home = (
        lax.psum_scatter(
            ungrouped(key_part).astype(jnp.bfloat16), "seq", scatter_dimension=1, tiled=True
        ).astype(jnp.float32),
        lax.psum_scatter(
            ungrouped(value_part).astype(jnp.bfloat16), "seq", scatter_dimension=1, tiled=True
        ).astype(jnp.float32),
    )
    grad_query = ungrouped(query_part).reshape(tok_count, model_dim).astype(jnp.bfloat16)
    grad_key = key_home.reshape(tok_count, model_dim).astype(jnp.bfloat16)
    grad_value = value_home.reshape(tok_count, model_dim).astype(jnp.bfloat16)
    grad_w_query = product_tn(tokens, grad_query)
    grad_b_query = jnp.sum(grad_query.astype(jnp.float32), axis=0)
    grad_w_key = product_tn(tokens, grad_key)
    grad_w_value = product_tn(tokens, grad_value)
    grad_b_value = jnp.sum(grad_value.astype(jnp.float32), axis=0)
    grad_input = (
        grad_one
        + product_nt(grad_query, w_query)
        + product_nt(grad_key, w_key)
        + product_nt(grad_value, w_value)
    )
    summed = lax.psum(
        (
            grad_w_query,
            grad_b_query,
            grad_w_key,
            grad_w_value,
            grad_b_value,
            grad_w_out,
            grad_b_out,
            grad_w_outer,
            grad_b_outer,
            grad_gain_two,
            grad_shift_two,
            grad_w_inner,
            grad_b_inner,
            grad_gain_one,
            grad_shift_one,
        ),
        ("dp", "seq"),
    )
    return (
        result.reshape(row_count, shard_len, model_dim).astype(jnp.bfloat16),
        grad_input.reshape(row_count, shard_len, model_dim).astype(jnp.bfloat16),
        summed[0],
        summed[1],
        summed[2],
        summed[3],
        summed[4],
        summed[5],
        summed[6],
        summed[13],
        summed[14],
        summed[11],
        summed[12],
        summed[7],
        summed[8],
        summed[9],
        summed[10],
    )


def solution(mesh):
    return jax.shard_map(
        on_device,
        mesh=mesh,
        in_specs=(
            P("dp", "seq", None),
            P("dp", "seq"),
            P(),
            P(),
            P(),
            P(),
            P(),
            P(),
            P(),
            P(),
            P(),
            P(),
            P(),
            P(),
            P(),
            P(),
            P(),
            P("dp", "seq", None),
        ),
        out_specs=(
            P("dp", "seq", None),
            P("dp", "seq", None),
            P(),
            P(),
            P(),
            P(),
            P(),
            P(),
            P(),
            P(),
            P(),
            P(),
            P(),
            P(),
            P(),
            P(),
            P(),
        ),
        check_vma=False,
    )
```

profile of v0, /device:TPU:0, one launch (start us, length us, event | category | flops | bytes accessed | tf_op | source)
XLA Modules:
  0.0 666.1 jit_solution(12733375049098746954)
XLA Ops:
  7.3 2.0 convolution_convert_fusion.1
  9.3 1.8 fusion.20
  14.2 12.6 %all_gather.7 = s32[2,512]{1,0:T(2,128)S(1)} all-gather(s32[2,128]{1,0:T(2,128)S(1)} %copy-done.40), channel_id=1, replica_groups=mesh['dp'=8,'seq'=4] {'seq'}, dimensions={1}, use_global_device_ids=true | all-gather | bytes 5120 | tf_op jit(solution)/shard_map/all_gather | solution.py:161
  28.3 50.1 %all-gather.2.cloned.1.call-done = bf16[2,2,512,768]{3,2,1,0:T(8,128)(2,1)} async-done(((bf16[2,2,128,768]{3,2,1,0:T(8,128)(2,1)}), bf16[2,2,512,768]{3,2,1,0:T(8,128)(2,1)}) %all-gather.2.cloned.1.call-update) | async-done | bytes 3145744 | tf_op jit(solution)/shard_map/all_gather | solution.py:160
  78.4 3.7 fusion.60
  83.9 2.6 copy.42
  86.5 2.3 fusion.3
  91.5 3.1 fusion.61
  96.0 1.8 multiply_convert_fusion.2
  102.4 3.0 convert_reduce_fusion
  105.4 2.2 multiply_reduce_fusion
  112.3 4.6 multiply_convert_fusion
  120.3 2.6 copy.52
  123.0 5.5 fusion.14
  128.5 2.6 copy.54
  131.2 3.2 convert_reduce_fusion.5
  134.8 1.9 convolution_bitcast_fusion.2
  136.7 1.9 fusion.35
  138.6 5.2 fusion.49
  143.8 5.3 fusion.56
  149.2 7.9 %reduce-scatter.3.cloned.1.call-done = bf16[2,128,768]{2,1,0:T(8,128)(2,1)} async-done(((bf16[2,512,768]{2,1,0:T(8,128)(2,1)}), bf16[2,128,768]{2,1,0:T(8,128)(2,1)}) %reduce-scatter.3.cloned.1.call-update) | async-done | bytes 393232 | tf_op jit(solution)/shard_map/reduce_scatter | solution.py:217
  157.0 2.9 convolution_bitcast_fusion.1
  160.0 34.3 %reduce-scatter.5.cloned.1.call-done = bf16[2,128,768]{2,1,0:T(8,128)(2,1)} async-done(((bf16[2,512,768]{2,1,0:T(8,128)(2,1)}), bf16[2,128,768]{2,1,0:T(8,128)(2,1)}) %reduce-scatter.5.cloned.1.call-update) | async-done | bytes 393232 | tf_op jit(solution)/shard_map/reduce_scatter | solution.py:220
  194.2 2.9 convolution_bitcast_fusion
  197.9 1.8 convolution_add_fusion.3
  199.8 42.9 %all-reduce = (f32[768]{0:T(1024)}, f32[768]{0:T(1024)}, f32[768]{0:T(1024)}, f32[768]{0:T(1024)}, f32[768]{0:T(1024)}, /*index=5*/f32[3072]{0:T(1024)}, f32[768]{0:T(1024)}, f32[768]{0:T(1024)}, f32[768]{0:T(1024)}) all-reduce(f32[768]{0:T(1024)S(1)} %copy-done.36, ...), channel_id=1, replica_groups=mesh['dp'=8,'seq'=4] {'dp','seq'}, use_global_device_ids=true, to_apply=%region_15.16 | all-reduce | flops 9216 | bytes 73728 | tf_op jit(solution)/shard_map/psum | solution.py:238
  245.6 391.2 %all-reduce.4.cloned.1.call-done = (f32[768,768]{0,1:T(8,128)}, f32[768,768]{0,1:T(8,128)}, f32[768,768]{0,1:T(8,128)}, f32[768,768]{1,0:T(8,128)}, f32[768,3072]{1,0:T(8,128)}, /*index=5*/f32[3072,768]{1,0:T(8,128)}) async-done(((f32[768,768]{0,1:T(8,128)}, f32[768,768]{0,1:T(8,128)}, f32[768,768]{0,1:T(8,128)}, f32[768,768]{1,0:T(8,128)}, f32[768,3072]{1,0:T(8,128)}, /*index=5*/f32[3072,768]{1,0:T(8,128)}), ...) | async-done | bytes 28311568 | tf_op jit(solution)/shard_map/psum | solution.py:238
  636.7 3.2 copy.57
  639.9 1.9 copy.58
  641.9 3.2 copy.59
  646.5 9.3 %copy.100 = f32[768,3072]{1,0:T(8,128)} copy(f32[768,3072]{1,0:T(8,128)} %get-tuple-element.169) | data formatting | bytes 18874368
  655.8 3.7 copy.101
  (150 shorter events, 28.4 us)
Async XLA Ops:
  7.2 87.9 %copy-start = (bf16[768,768]{1,0:T(8,128)(2,1)S(1)}, bf16[768,768]{1,0:T(8,128)(2,1)}, u32[]{:S(2)}) copy-start(bf16[768,768]{1,0:T(8,128)(2,1)} %param.25) | copy-start | bytes 3538948
  7.2 71.2 %all-gather.2.cloned.1.call-start = ((), (), s32[]{:S(2)}) async-start(), calls=%async_computation.2 | async-start | bytes 3932160 | tf_op jit(solution)/shard_map/all_gather | solution.py:160
  7.3 4.9 copy-start.6
  7.3 4.9 copy-start.42
  11.1 3.1 copy-start.40
  11.1 15.7 %copy-start.11 = (bf16[2,128,768]{2,1,0:T(8,128)(2,1)S(1)}, bf16[2,128,768]{2,1,0:T(8,128)(2,1)}, u32[]{:S(2)}) copy-start(bf16[2,128,768]{2,1,0:T(8,128)(2,1)} %param.35) | copy-start | bytes 1179652
  11.1 15.7 %copy-start.30 = (f32[768]{0:T(1024)S(1)}, f32[768]{0:T(1024)}, u32[]{:S(2)}) copy-start(f32[768]{0:T(1024)} %param.33) | copy-start | bytes 9220
  12.1 144.9 %reduce-scatter.3.cloned.1.call-start = ((), (), s32[]{:S(2)}) async-start(), calls=%async_computation.3 | async-start | bytes 1966080 | tf_op jit(solution)/shard_map/reduce_scatter | solution.py:217
  14.2 72.3 %copy-start.9 = (bf16[2,128,12,64]{1,0,3,2:T(2,128)(2,1)}, bf16[2,128,12,64]{1,0,3,2:T(2,128)(2,1)S(1)}, u32[]{:S(2)}) copy-start(bf16[2,128,12,64]{1,0,3,2:T(2,128)(2,1)S(1)} %reshape.206) | copy-start | bytes 1179652
  91.4 4.5 slice-start.5
  91.5 3.6 copy-start.43
  91.5 4.5 slice-start.6
  95.7 11.9 %copy-start.4 = (f32[256,768]{1,0:T(8,128)}, f32[256,768]{1,0:T(8,128)S(1)}, u32[]{:S(2)}) copy-start(f32[256,768]{1,0:T(8,128)S(1)} %get-tuple-element.146) | copy-start | bytes 2359300
  95.7 11.9 %copy-start.31 = (f32[256]{0:T(256)}, f32[256]{0:T(256)S(1)}, u32[]{:S(2)}) copy-start(f32[256]{0:T(256)S(1)} %broadcast_multiply_fusion.4) | copy-start | bytes 3076
  96.0 11.6 %copy-start.37 = (f32[256]{0:T(256)}, f32[256]{0:T(256)S(1)}, u32[]{:S(2)}) copy-start(f32[256]{0:T(256)S(1)} %add_rsqrt_fusion.1) | copy-start | bytes 3076
  112.3 6.3 copy-start.10
  122.9 71.3 %reduce-scatter.5.cloned.1.call-start = ((), (), s32[]{:S(2)}) async-start(), calls=%async_computation.4 | async-start | bytes 1966080 | tf_op jit(solution)/shard_map/reduce_scatter | solution.py:220
  131.1 3.7 copy-start.7
  131.1 505.6 %all-reduce.4.cloned.1.call-start = ((), (), s32[]{:S(2)}) async-start(), calls=%async_computation.5 | async-start | bytes 56623104 | tf_op jit(solution)/shard_map/psum | solution.py:238
  134.8 3.8 copy-start.15
  134.8 3.8 copy-start.17
  138.6 5.2 copy-start.5
  138.6 5.2 copy-start.24
  138.6 5.2 copy-start.32
  138.6 5.2 copy-start.38
  197.2 45.5 %copy-start.8 = (bf16[768,768]{1,0:T(8,128)(2,1)S(1)}, bf16[768,768]{1,0:T(8,128)(2,1)}, u32[]{:S(2)}) copy-start(bf16[768,768]{1,0:T(8,128)(2,1)} %param.22) | copy-start | bytes 3538948
  636.7 3.2 copy-start.19
  641.9 3.2 copy-start.18
  645.1 10.7 %slice-start = ((s8[9437184]{0:T(1024)(128)(4,1)}), s8[4194304]{0:T(1024)(128)(4,1)S(1)}, s32[]{:S(2)}) async-start(s8[9437184]{0:T(1024)(128)(4,1)} %bitcast.106), calls=%async_computation.6 | async-start | bytes 8388608
  646.5 9.3 %slice-start.1 = ((s8[9437184]{0:T(1024)(128)(4,1)}), s8[4194304]{0:T(1024)(128)(4,1)S(1)}, s32[]{:S(2)}) async-start(s8[9437184]{0:T(1024)(128)(4,1)} %bitcast.106), calls=%async_computation.7 | async-start | bytes 8388608
  646.5 9.3 %slice-start.2 = ((s8[9437184]{0:T(1024)(128)(4,1)}), s8[1048576]{0:T(1024)(128)(4,1)S(1)}, s32[]{:S(2)}) async-start(s8[9437184]{0:T(1024)(128)(4,1)} %bitcast.106), calls=%async_computation.8 | async-start | bytes 2097152
  655.8 3.8 copy-start.1
  (24 other events, 51.4 us)
Sparse Core Ops, SparseCore 0:
  12.2 66.1 all-gather.1
  123.0 33.9 reduce-scatter.2
  159.9 34.2 reduce-scatter.4
  201.6 435.0 all-reduce.3
where the time goes:
time: 667 us; the launch traced here: 666 us
  waiting for transfers between devices  483 us (72%)
  matrix products  61.2 us (9%)
  blocking collectives  55.5 us (8%)
  local copies, waits for them, and re-layouts  41 us (6%)
  between operations  14.4 us (2%)
  other arithmetic  10.4 us (2%)
    psum x1, waiting for transfers between devices, on_device(): lax.psum((grad_w_query, grad_b_query, grad_w_key, grad_w_value, grad_b_va...  391 us
    all_gather x1, waiting for transfers between devices, on_device(): lax.all_gather(stacked, 'seq', axis=2, tiled=True)  50.1 us
    psum x1, blocking collectives, on_device(): lax.psum((grad_w_query, grad_b_query, grad_w_key, grad_w_value, grad_b_va...  42.9 us
    reduce_scatter x1, waiting for transfers between devices, on_device(): lax.psum_scatter(ungrouped(value_part).astype(jnp.bfloat16), 'seq', scatt...  34.3 us
    unnamed x110, local copies, waits for them, and re-layouts  24.8 us
    dot_general x6, matrix products, product_tn(): lax.dot_general(left, right, (((0,), (0,)), ((), ())), preferred_element_...  20.1 us
  transfers between devices with their start and end apart: 4, of which 4 were waited for; matrix products, arithmetic and copies ran while one was open for 6% of the time, Pallas kernels for 0%

commit v1 on v0

v1 whole, which is shorter than its diff:
```python
import functools

import jax
import jax.numpy as jnp
from jax import lax
from jax.experimental import pallas as pl
from jax.experimental.pallas import tpu as pltpu
from jax.sharding import PartitionSpec as P

HD = 64
EPSILON = 1e-12
MASKED = -1000000000.0
INV_ROOT_TWO = 0.7071067811865476
DENSITY = 0.3989422804014327
MESH = pl.DeviceIdType.MESH
BF16 = jnp.bfloat16
F32 = jnp.float32


def product(left, right):
    return jnp.dot(left, right, preferred_element_type=F32)


def product_tn(left, right):
    return lax.dot_general(left, right, (((0,), (0,)), ((), ())), preferred_element_type=F32)


def product_nt(left, right):
    return lax.dot_general(left, right, (((1,), (1,)), ((), ())), preferred_element_type=F32)


def place(seq_size):
    dp, sq = lax.axis_index("dp"), lax.axis_index("seq")
    side = dp % 2
    return dp, sq, side, dp - side


def gather_kernel(seq_size, x_ref, cot_ref, seg_ref, xf_ref, ct_ref, sg_ref, ss, rs, ls):
    rows, length = x_ref.shape[0], x_ref.shape[1]
    spread = seq_size // 2
    dp, sq, side, pair = place(seq_size)
    half, spot = sq // spread, sq % spread
    own = side * spread * length
    sibling = (dp + 1 - 2 * side, sq)

    def x_copy(r, b, tgt, row0):
        return pltpu.make_async_remote_copy(
            x_ref.at[r], xf_ref.at[pl.ds(row0, length)], ss.at[0, r], rs.at[0, b], tgt, MESH
        )

    def c_copy(r, b, tgt):
        return pltpu.make_async_remote_copy(
            cot_ref.at[r], ct_ref.at[pl.ds(pl.multiple_of(b * length, length), length)],
            ss.at[1, r], rs.at[1, b], tgt, MESH,
        )

    def s_copy(r, c, at, tgt):
        return pltpu.make_async_remote_copy(
            seg_ref.at[r], sg_ref.at[at], ss.at[2 + c, r], rs.at[2, at], tgt, MESH
        )

    def forward(b):
        row0 = pl.multiple_of(own + b * length, length)
        return pltpu.make_async_remote_copy(
            xf_ref.at[pl.ds(row0, length)], xf_ref.at[pl.ds(row0, length)],
            ss.at[4, b], rs.at[3, b], sibling, MESH,
        )

    for r in range(rows):
        to_seq = rows * side + r
        local = jnp.logical_and(half == side, sq == to_seq)
        row0 = pl.multiple_of((half * spread + spot) * length, length)

        @pl.when(local)
        def _():
            pltpu.make_async_copy(x_ref.at[r], xf_ref.at[pl.ds(row0, length)], ls.at[0, r]).start()
            pltpu.make_async_copy(
                cot_ref.at[r], ct_ref.at[pl.ds(pl.multiple_of(spot * length, length), length)], ls.at[1, r]
            ).start()

        @pl.when(jnp.logical_not(local))
        def _():
            x_copy(r, spot, (pair + half, to_seq), row0).start()

        for c in range(2):
            mine = jnp.logical_and(side == c, sq == to_seq)

            @pl.when(mine)
            def _():
                pltpu.make_async_copy(seg_ref.at[r], sg_ref.at[sq], ls.at[2, r]).start()

            @pl.when(jnp.logical_not(mine))
            def _():
                s_copy(r, c, sq, (pair + c, to_seq)).start()

    for r in range(rows):
        to_seq = rows * side + r
        local = jnp.logical_and(half == side, sq == to_seq)

        @pl.when(jnp.logical_not(local))
        def _():
            c_copy(r, spot, (pair + half, to_seq)).start()

    for b in range(spread):
        local = jnp.logical_and(sq // rows == side, side * spread + b == sq)

        @pl.when(local)
        def _():
            row0 = pl.multiple_of(own + b * length, length)
            pltpu.make_async_copy(x_ref.at[b], xf_ref.at[pl.ds(row0, length)], ls.at[0, sq % rows]).wait()

        @pl.when(jnp.logical_not(local))
        def _():
            x_copy(0, b, sibling, pl.multiple_of(own + b * length, length)).wait_recv()

        forward(b).start()

    for b in range(spread):
        local = jnp.logical_and(sq // rows == side, side * spread + b == sq)

        @pl.when(local)
        def _():
            pltpu.make_async_copy(
                cot_ref.at[b], ct_ref.at[pl.ds(pl.multiple_of(b * length, length), length)], ls.at[1, sq % rows]
            ).wait()

        @pl.when(jnp.logical_not(local))
        def _():
            c_copy(0, b, sibling).wait_recv()

        other = pl.multiple_of((1 - side) * spread * length + b * length, length)
        pltpu.make_async_remote_copy(
            xf_ref.at[pl.ds(other, length)], xf_ref.at[pl.ds(other, length)], ss.at[4, b], rs.at[3, b], sibling, MESH
        ).wait_recv()
        forward(b).wait_send()

    for p in range(seq_size):
        mine = jnp.logical_and(sq // rows == side, p == sq)

        @pl.when(mine)
        def _():
            pltpu.make_async_copy(seg_ref.at[0], sg_ref.at[sq], ls.at[2, sq % rows]).wait()

        @pl.when(jnp.logical_not(mine))
        def _():
            s_copy(0, 0, p, sibling).wait_recv()

    for r in range(rows):
        to_seq = rows * side + r
        local = jnp.logical_and(half == side, sq == to_seq)

        @pl.when(jnp.logical_not(local))
        def _():
            x_copy(r, spot, sibling, 0).wait_send()
            c_copy(r, spot, sibling).wait_send()

        for c in range(2):

            @pl.when(jnp.logical_not(jnp.logical_and(side == c, sq == to_seq)))
            def _():
                s_copy(r, c, sq, sibling).wait_send()


def gather_rows(layer_input, cotangent, segment_ids, seq_size):
    rows, length, width = layer_input.shape
    tokens = seq_size * length
    seg = jnp.broadcast_to(segment_ids[:, None, :], (rows, 8, length))
    vmem = pl.BlockSpec(memory_space=pltpu.VMEM)
    return pl.pallas_call(
        functools.partial(gather_kernel, seq_size),
        out_shape=(
            jax.ShapeDtypeStruct((tokens, width), BF16),
            jax.ShapeDtypeStruct((tokens // 2, width), BF16),
            jax.ShapeDtypeStruct((seq_size, 8, length), jnp.int32),
        ),
        in_specs=[vmem] * 3,
        out_specs=(vmem,) * 3,
        scratch_shapes=[
            pltpu.SemaphoreType.DMA((5, 2)),
            pltpu.SemaphoreType.DMA((4, seq_size)),
            pltpu.SemaphoreType.DMA((3, 2)),
        ],
        compiler_params=pltpu.CompilerParams(has_side_effects=True),
        name="gather_rows",
    )(layer_input, cotangent, seg)


GROUP = 3072
PIECE = 1024
ORDERS = (("x", "y", "z"), ("y", "z", "x"), ("z", "x", "y"))
SUBS = 2


class Exchange:
    def __init__(self, dp_size, seq_size, groups):
        self.dp_size, self.seq_size, self.groups = dp_size, seq_size, groups
        self.extra = []
        bit = 8
        while bit < dp_size:
            self.extra.append(bit)
            bit *= 2
        self.sems = 0
        self.slots = 0
        self.pieces = []
        for g in range(groups):
            for cls in range(3):
                self.pieces.append(self.plan(g * GROUP + cls * PIECE, ORDERS[cls]))

    def sem(self):
        self.sems += 1
        return self.sems - 1

    def slot(self, rows):
        self.slots += rows
        return self.slots - rows

    def plan(self, base, order):
        stages, rows, ends = [], PIECE, False
        for axis in ("c",) + order:
            half = rows // 2
            st = dict(axis=axis, rows=half, ends=ends)
            if axis == "z":
                n = half // SUBS
                st["down"] = [dict(rs=self.sem(), ag=self.sem(), slot=self.slot(n), rows=n, at=i * n) for i in range(SUBS)]
                st["up"] = [dict(rs=self.sem(), ag=self.sem(), slot=self.slot(n), rows=n, at=i * n) for i in range(SUBS)]
                ends = True
            else:
                st.update(rs=self.sem(), ag=self.sem(), slot=self.slot(half))
            stages.append(st)
            rows = half
        more = [dict(bit=b, rs=self.sem(), slot=self.slot(rows)) for b in self.extra]
        return dict(base=base, stages=stages, more=more, rows=rows)

    def bind(self, total, slots, final, send_sem, recv_sem):
        self.total, self.landing, self.final = total, slots, final
        self.ss, self.rs = send_sem, recv_sem
        dp, sq = lax.axis_index("dp"), lax.axis_index("seq")
        self.dp, self.sq = dp, sq
        self.bits = {"c": (1, dp % 2), "x": (2, (dp // 2) % 2), "y": (4, (dp // 4) % 2)}
        self.last = self.seq_size - 1
        self.edge = jnp.logical_or(sq == 0, sq == self.last)
        self.side = sq // self.last
        self.sent = []
        for p in self.pieces:
            off = p["base"]
            for st in p["stages"]:
                half = st["rows"]
                st["off"] = off
                value = self.side if st["axis"] == "z" else self.bits[st["axis"]][1]
                st["keep"] = off + value * half
                st["give"] = off + (1 - value) * half
                off = st["keep"]
            p["own"] = off

    def view(self, off, rows):
        return self.total.at[pl.ds(pl.multiple_of(off, 16), rows)]

    def partner(self, axis):
        bit, value = self.bits[axis]
        return (self.dp + bit * (1 - 2 * value), self.sq)

    def copy(self, src, dst, sem, tgt):
        return pltpu.make_async_remote_copy(src, dst, self.ss.at[sem], self.rs.at[sem], tgt, MESH)

    def send(self, make, when):
        self.sent.append((make, when))
        make().start()

    def gated(self, when, f):
        if when is None:
            f()
        else:
            pl.when(when)(f)

    def done(self, off, rows):
        return self.final.at[pl.ds(pl.multiple_of(off, 16), rows)]

    def add(self, off, slot, rows, into=None):
        into = self.total if into is None else into
        step = 32 if rows % 32 == 0 else 16

        def body(i, _):
            at = pl.multiple_of(off + i * step, 16)
            frm = pl.multiple_of(slot + i * step, 16)
            into[pl.ds(at, step)] = self.total[pl.ds(at, step)] + self.landing[pl.ds(frm, step)]
            return 0

        lax.fori_loop(0, rows // step, body, 0)


    def rs_start(self, p, i):
        st = p["stages"][i]
        if st["axis"] == "z":
            for way, at, to, base in (("down", self.last, -1, 0), ("up", 0, 1, st["rows"])):
                when = self.sq == at

                def f(way=way, to=to, base=base, when=when):
                    for s in st[way]:
                        self.send(lambda s=s: self.rs_copy(st, s, base, to), when)
                self.gated(when, f)
        else:
            when = self.edge if st["ends"] else None

            def f():
                self.send(
                    lambda: self.copy(
                        self.view(st["give"], st["rows"]), self.landing.at[pl.ds(st["slot"], st["rows"])],
                        st["rs"], self.partner(st["axis"]),
                    ),
                    when,
                )
            self.gated(when, f)

    def rs_hyper(self, p, i):
        st = p["stages"][i]

        def f():
            self.copy(
                self.view(st["give"], st["rows"]), self.landing.at[pl.ds(st["slot"], st["rows"])],
                st["rs"], self.partner(st["axis"]),
            ).wait_recv()
            self.add(st["keep"], st["slot"], st["rows"], self.final if i + 1 == len(p["stages"]) else None)
        self.gated(self.edge if st["ends"] else None, f)

    def rs_hop(self, p, i, hop):
        st = p["stages"][i]
        for way, at, to, base in (("down", self.last - hop, -1, 0), ("up", hop, 1, st["rows"])):
            when = self.sq == at

            def f(way=way, to=to, base=base, when=when):
                for s in st[way]:
                    self.rs_copy(st, s, base, -to).wait_recv()
                    ended = hop == self.last and i + 1 == len(p["stages"])
                    self.add(st["off"] + base + s["at"], s["slot"], s["rows"], self.final if ended else None)
                    if hop < self.last:
                        self.send(lambda s=s: self.rs_copy(st, s, base, to), when)
            self.gated(when, f)

    def rs_copy(self, st, s, base, to):
        return self.copy(
            self.view(st["off"] + base + s["at"], s["rows"]), self.landing.at[pl.ds(s["slot"], s["rows"])],
            s["rs"], (self.dp, self.sq + to),
        )

    def more(self, p):
        for m in p["more"]:
            bit = m["bit"]
            value = (self.dp // bit) % 2
            tgt = (self.dp + bit * (1 - 2 * value), self.sq)

            def f():
                c = self.copy(
                    self.done(p["own"], p["rows"]), self.landing.at[pl.ds(m["slot"], p["rows"])], m["rs"], tgt
                )
                c.start()
                c.wait()
                part = pl.ds(pl.multiple_of(p["own"], 16), p["rows"])
                self.final[part] = self.final[part] + self.landing[pl.ds(m["slot"], p["rows"])]
            self.gated(self.edge, f)


    def ag_start(self, p, i):
        st = p["stages"][i]
        if st["axis"] == "z":
            for way, at, to, base in (("down", self.last, -1, st["rows"]), ("up", 0, 1, 0)):
                when = self.sq == at

                def f(way=way, to=to, base=base, when=when):
                    for s in st[way]:
                        self.send(lambda s=s: self.ag_copy(st, s, base, to), when)
                self.gated(when, f)
        else:
            when = self.edge if st["ends"] else None

            def f():
                self.send(
                    lambda: self.copy(
                        self.done(st["keep"], st["rows"]), self.done(st["keep"], st["rows"]),
                        st["ag"], self.partner(st["axis"]),
                    ),
                    when,
                )
            self.gated(when, f)

    def ag_copy(self, st, s, base, to):
        part = self.done(st["off"] + base + s["at"], s["rows"])
        return self.copy(part, part, s["ag"], (self.dp, self.sq + to))

    def ag_hyper(self, p, i):
        st = p["stages"][i]

        def f():
            part = self.done(st["give"], st["rows"])
            self.copy(part, part, st["ag"], self.partner(st["axis"])).wait_recv()
        self.gated(self.edge if st["ends"] else None, f)

    def ag_hop(self, p, i, hop):
        st = p["stages"][i]
        for way, at, to, base in (("down", self.last - hop, -1, st["rows"]), ("up", hop, 1, 0)):
            when = self.sq == at

            def f(way=way, to=to, base=base, when=when):
                for s in st[way]:
                    self.ag_copy(st, s, base, -to).wait_recv()
                    if hop < self.last:
                        self.send(lambda s=s: self.ag_copy(st, s, base, to), when)
            self.gated(when, f)

    def script(self, p):
        steps, n = [], len(p["stages"])
        for i, st in enumerate(p["stages"]):
            after = (lambda i=i: self.rs_start(p, i + 1)) if i + 1 < n else (lambda: (self.more(p), self.ag_start(p, n - 1)))
            if st["axis"] == "z":
                for hop in range(1, self.last + 1):
                    def step(i=i, hop=hop, after=after):
                        self.rs_hop(p, i, hop)
                        if hop == self.last:
                            after()
                    steps.append((f"rz{hop}", step))
            else:
                def step(i=i, after=after):
                    self.rs_hyper(p, i)
                    after()
                steps.append(("r" + st["axis"], step))
        for i in reversed(range(n)):
            st = p["stages"][i]
            after = (lambda i=i: self.ag_start(p, i - 1)) if i > 0 else (lambda: None)
            if st["axis"] == "z":
                for hop in range(1, self.last + 1):
                    def step(i=i, hop=hop, after=after):
                        self.ag_hop(p, i, hop)
                        if hop == self.last:
                            after()
                    steps.append((f"gz{hop}", step))
            else:
                def step(i=i, after=after):
                    self.ag_hyper(p, i)
                    after()
                steps.append(("g" + st["axis"], step))
        return steps

    def finish(self):
        for make, when in self.sent:
            self.gated(when, lambda make=make: make().wait_send())


def small_bits(dp_size, seq_size):
    out, bit = [], 1
    while bit < dp_size:
        out.append(("dp", bit))
        bit *= 2
    bit = 1
    while bit < seq_size:
        out.append(("seq", bit))
        bit *= 2
    return out


def blocks_of(refs, g):
    outer, inner, proj = refs
    out = []
    for i in range(GROUP // 256):
        at = i * 256
        block, row = at // 768, at % 768
        if g == 0:
            view = outer.at[pl.ds(at, 256)]
        elif g == 1:
            view = inner.at[pl.ds(row, 256), pl.ds(block * 768, 768)]
        else:
            view = proj[block].at[pl.ds(row, 256)]
        out.append((g * GROUP + at, view))
    return out


def sums_kernel(
    plan, seq_size,
    outer_in, inner_in, o_in, q_in, k_in, v_in, small_in, y_in, dx_in, dxs_in,
    outer_out, inner_out, o_out, q_out, k_out, v_out, small_out, y_out, dx_out,
    total, landing, final, small, dx_far, dx_near, ss, rs, ls, ms, mr, ys, yr, xs,
):
    plan.bind(total, landing, final, ss, rs)
    dp, sq, side, pair = place(seq_size)
    sibling = (dp + 1 - 2 * side, sq)
    rows, length = y_out.shape[0], y_out.shape[1]
    spread = seq_size // 2

    loads = []
    for g in range(plan.groups):
        part = []
        for i, (at, view) in enumerate(blocks_of((outer_in, inner_in, (o_in, q_in, k_in, v_in)), g)):
            c = pltpu.make_async_copy(view, total.at[pl.ds(at, 256)], ls.at[g, i])
            c.start()
            part.append(c)
        loads.append(part)

    dx_send = pltpu.make_async_remote_copy(dxs_in, dx_far, xs.at[0], xs.at[1], sibling, MESH)
    dx_send.start()

    def back(src, dst, b, lane, tgt):
        return pltpu.make_async_remote_copy(
            src.at[pl.ds(b * length, length)], dst.at[tgt[2]], ys.at[lane, b], yr.at[lane, tgt[2]], tgt[:2], MESH
        )

    def each_back(src, dst, lane, remote, local):
        for b in range(spread):
            home = (pair + sq // rows, side * spread + b, sq % rows)
            mine = jnp.logical_and(home[0] == dp, home[1] == sq)

            @pl.when(mine)
            def _():
                local(pltpu.make_async_copy(src.at[pl.ds(b * length, length)], dst.at[home[2]], xs.at[2 + lane]))

            @pl.when(jnp.logical_not(mine))
            def _():
                remote(back(src, dst, b, lane, home))

    def all_arrived(src, dst, lane):
        for r in range(rows):
            mine = jnp.logical_and(sq // spread == side, sq == rows * side + r)

            @pl.when(jnp.logical_not(mine))
            def _():
                back(src, dst, 0, lane, (sibling[0], sibling[1], r)).wait_recv()

    each_back(y_in, y_out, 0, lambda c: c.start(), lambda c: c.start())

    steps = [plan.script(p) for p in plan.pieces]
    for g in range(plan.groups):
        for c in loads[g]:
            c.wait()
        for p in plan.pieces[3 * g : 3 * g + 3]:
            plan.rs_start(p, 0)

    small[0] = small_in[...]
    bits = small_bits(plan.dp_size, seq_size)

    def small_copy(i):
        axis, bit = bits[i]
        if axis == "dp":
            tgt = (dp + bit * (1 - 2 * ((dp // bit) % 2)), sq)
        else:
            tgt = (dp, sq + bit * (1 - 2 * ((sq // bit) % 2)))
        return pltpu.make_async_remote_copy(small.at[i], small.at[len(bits) + 1 + i], ms.at[i], mr.at[i], tgt, MESH)

    small_copy(0).start()

    dx_send.wait_recv()

    def dx_body(i, _):
        at = pl.ds(pl.multiple_of(i * 32, 32), 32)
        dx_near[at] = (dx_in[at] + dx_far[at].astype(F32)).astype(BF16)
        return 0

    lax.fori_loop(0, dx_in.shape[0] // 32, dx_body, 0)
    each_back(dx_near, dx_out, 1, lambda c: c.start(), lambda c: c.start())

    stores = []
    for t in range(len(steps[0])):
        for g in range(plan.groups):
            for cls in range(3):
                steps[3 * g + cls][t][1]()
        if t < len(bits):
            small_copy(t).wait_recv()
            small[t + 1] = small[t] + small[len(bits) + 1 + t]
            if t + 1 < len(bits):
                small_copy(t + 1).start()
    for g in range(plan.groups):
        for i, (at, view) in enumerate(blocks_of((outer_out, inner_out, (o_out, q_out, k_out, v_out)), g)):
            c = pltpu.make_async_copy(final.at[pl.ds(at, 256)], view, ls.at[g, i])
            c.start()
            stores.append(c)
    small_out[...] = small[len(bits)]
    for i in range(len(bits)):
        small_copy(i).wait_send()
    dx_send.wait_send()
    each_back(y_in, y_out, 0, lambda c: c.wait_send(), lambda c: c.wait())
    each_back(dx_near, dx_out, 1, lambda c: c.wait_send(), lambda c: c.wait())
    all_arrived(y_in, y_out, 0)
    all_arrived(dx_near, dx_out, 1)
    plan.finish()
    for c in stores:
        c.wait()


def all_sums(outer, inner, w_o, w_q, w_k, w_v, small, y, dx, dx_far, dp_size, seq_size, rows):
    plan = Exchange(dp_size, seq_size, 3)
    tokens, width = dx.shape
    length = 2 * tokens // seq_size
    vmem, anyw = pl.BlockSpec(memory_space=pltpu.VMEM), pl.BlockSpec(memory_space=pl.ANY)
    nbits = len(small_bits(dp_size, seq_size))
    back = jax.ShapeDtypeStruct((rows, length, width), BF16)
    like = lambda a: jax.ShapeDtypeStruct(a.shape, a.dtype)
    return pl.pallas_call(
        functools.partial(sums_kernel, plan, seq_size),
        out_shape=(like(outer), like(inner), like(w_o), like(w_q), like(w_k), like(w_v), like(small), back, back),
        in_specs=[anyw] * 6 + [vmem, anyw, vmem, anyw],
        out_specs=(anyw,) * 6 + (vmem, anyw, anyw),
        scratch_shapes=[
            pltpu.VMEM((3 * GROUP, width), BF16),
            pltpu.VMEM((plan.slots, width), BF16),
            pltpu.VMEM((3 * GROUP, width), BF16),
            pltpu.VMEM((2 * nbits + 1,) + small.shape, F32),
            pltpu.VMEM((tokens, width), BF16),
            pltpu.VMEM((tokens, width), BF16),
            pltpu.SemaphoreType.DMA((plan.sems,)),
            pltpu.SemaphoreType.DMA((plan.sems,)),
            pltpu.SemaphoreType.DMA((3, GROUP // 256)),
            pltpu.SemaphoreType.DMA((nbits,)),
            pltpu.SemaphoreType.DMA((nbits,)),
            pltpu.SemaphoreType.DMA((2, 2)),
            pltpu.SemaphoreType.DMA((2, 2)),
            pltpu.SemaphoreType.DMA((4,)),
        ],
        compiler_params=pltpu.CompilerParams(has_side_effects=True, vmem_limit_bytes=56 << 20),
        name="all_sums",
    )(outer, inner, w_o, w_q, w_k, w_v, small, y, dx, dx_far)


def layer_norm(values, scale_gain, offset):
    centre = values - jnp.mean(values, axis=-1, keepdims=True)
    inverse_std = lax.rsqrt(jnp.mean(centre * centre, axis=-1, keepdims=True) + EPSILON)
    normed = centre * inverse_std
    return (normed * scale_gain + offset, normed, inverse_std)


def norm_back(grad_out, normed, inverse_std, scale_gain):
    scaled = grad_out * scale_gain
    return inverse_std * (
        scaled
        - jnp.mean(scaled, axis=-1, keepdims=True)
        - normed * jnp.mean(scaled * normed, axis=-1, keepdims=True)
    )


def heads(t):
    return t.reshape(t.shape[0], t.shape[1] // HD, HD)


def local_layer(x_full, cot, segs, side, w):
    (w_query, b_query, w_key, w_value, b_value, w_out, b_out, gain_one, shift_one,
     w_inner, b_inner, w_outer, b_outer, gain_two, shift_two) = w
    tokens = cot.shape[0]
    x_own = lax.dynamic_slice_in_dim(x_full, side * tokens, tokens, 0)
    seg_own = lax.dynamic_slice_in_dim(segs, side * tokens, tokens, 0)
    query = (product(x_own, w_query) + b_query).astype(BF16)
    key = product(x_full, w_key).astype(BF16)
    value = (product(x_full, w_value) + b_value).astype(BF16)
    scores = jnp.einsum("qhd,khd->hqk", heads(query), heads(key), preferred_element_type=F32) * 0.125
    scores = jnp.where(seg_own[None, :, None] == segs[None, None, :], scores, MASKED)
    row_max = jnp.max(scores, axis=-1, keepdims=True)
    powers = jnp.exp(scores - row_max)
    totals = jnp.sum(powers, axis=-1, keepdims=True)
    probs = powers / totals
    probs_low = probs.astype(BF16)
    attended = jnp.einsum("hqk,khd->qhd", probs_low, heads(value), preferred_element_type=F32)
    attn_low = attended.reshape(tokens, -1).astype(BF16)
    hidden_one, normed_one, inverse_one = layer_norm(
        x_own.astype(F32) + product(attn_low, w_out) + b_out, gain_one, shift_one
    )
    hidden_low = hidden_one.astype(BF16)
    inner = product(hidden_low, w_inner) + b_inner
    cdf = 0.5 * (1.0 + lax.erf(inner * INV_ROOT_TWO))
    active = (inner * cdf).astype(BF16)
    result, normed_two, inverse_two = layer_norm(hidden_one + product(active, w_outer) + b_outer, gain_two, shift_two)
    g = cot.astype(F32)
    d_gain_two, d_shift_two = jnp.sum(g * normed_two, 0), jnp.sum(g, 0)
    grad_two = norm_back(g, normed_two, inverse_two, gain_two)
    grad_outer = grad_two.astype(BF16)
    d_outer = product_tn(active, grad_outer).astype(BF16)
    d_b_outer = jnp.sum(grad_outer.astype(F32), 0)
    slope = cdf + inner * DENSITY * jnp.exp(-0.5 * inner * inner)
    grad_inner = (product_nt(grad_outer, w_outer) * slope).astype(BF16)
    d_inner = product_tn(hidden_low, grad_inner).astype(BF16)
    d_b_inner = jnp.sum(grad_inner.astype(F32), 0)
    grad_hidden = grad_two + product_nt(grad_inner, w_inner)
    d_gain_one, d_shift_one = jnp.sum(grad_hidden * normed_one, 0), jnp.sum(grad_hidden, 0)
    grad_one = norm_back(grad_hidden, normed_one, inverse_one, gain_one)
    grad_branch = grad_one.astype(BF16)
    d_out = product_tn(attn_low, grad_branch).astype(BF16)
    d_b_out = jnp.sum(grad_branch.astype(F32), 0)
    grad_attn = product_nt(grad_branch, w_out).astype(BF16)
    delta = jnp.sum(heads(grad_attn).astype(F32) * heads(attended.reshape(tokens, -1)), -1)
    grad_prob = jnp.einsum("qhd,khd->hqk", heads(grad_attn), heads(value), preferred_element_type=F32)
    grad_scores = (probs * (grad_prob - delta.T[:, :, None])).astype(BF16)
    grad_query = (jnp.einsum("hqk,khd->qhd", grad_scores, heads(key), preferred_element_type=F32) * 0.125)
    grad_query = grad_query.reshape(tokens, -1).astype(BF16)
    grad_key = (jnp.einsum("hqk,qhd->khd", grad_scores, heads(query), preferred_element_type=F32) * 0.125)
    grad_key = grad_key.reshape(2 * tokens, -1).astype(BF16)
    grad_value = jnp.einsum("hqk,qhd->khd", probs_low, heads(grad_attn), preferred_element_type=F32)
    grad_value = grad_value.reshape(2 * tokens, -1).astype(BF16)
    d_query = product_tn(x_own, grad_query).astype(BF16)
    d_key = product_tn(x_full, grad_key).astype(BF16)
    d_value = product_tn(x_full, grad_value).astype(BF16)
    d_b_query = jnp.sum(grad_query.astype(F32), 0)
    d_b_value = jnp.sum(grad_value.astype(F32), 0)
    both = product_nt(grad_key, w_key) + product_nt(grad_value, w_value)
    dx = grad_one + product_nt(grad_query, w_query) + lax.dynamic_slice_in_dim(both, side * tokens, tokens, 0)
    dx_far = lax.dynamic_slice_in_dim(both, (1 - side) * tokens, tokens, 0).astype(BF16)
    small = jnp.concatenate(
        [
            jnp.stack([d_b_query, d_b_value, d_b_out, d_gain_one, d_shift_one, d_b_outer, d_gain_two, d_shift_two]),
            d_b_inner.reshape(-1, 768),
            jnp.zeros((4, 768), F32),
        ]
    )
    return result.astype(BF16), dx, dx_far, d_outer, d_inner, d_out, d_query, d_key, d_value, small


def on_device(
    dp_size, seq_size, layer_input, segment_ids, w_query, b_query, w_key, w_value, b_value, w_out, b_out, gain_one,
    shift_one, w_inner, b_inner, w_outer, b_outer, gain_two, shift_two, cotangent,
):
    rows = layer_input.shape[0]
    x_full, cot, sg = gather_rows(layer_input, cotangent, segment_ids, seq_size)
    side = lax.axis_index("dp") % 2
    y, dx, dx_far, d_outer, d_inner, d_out, d_query, d_key, d_value, small = local_layer(
        x_full, cot, sg[:, 0, :].reshape(-1), side,
        (w_query, b_query, w_key, w_value, b_value, w_out, b_out, gain_one, shift_one, w_inner, b_inner, w_outer,
         b_outer, gain_two, shift_two),
    )
    d_outer, d_inner, d_out, d_query, d_key, d_value, small, y, dx = all_sums(
        d_outer, d_inner, d_out, d_query, d_key, d_value, small, y, dx, dx_far, dp_size, seq_size, rows
    )
    up = lambda a: a.astype(F32)
    return (
        y, dx, up(d_query), small[0], up(d_key), up(d_value), small[1], up(d_out), small[2], small[3], small[4],
        up(d_inner), small[8:12].reshape(-1), up(d_outer), small[5], small[6], small[7],
    )


def solution(mesh):
    sizes = (mesh.shape["dp"], mesh.shape["seq"])
    tokens = P("dp", "seq", None)
    return jax.shard_map(
        functools.partial(on_device, *sizes),
        mesh=mesh,
        in_specs=(tokens, P("dp", "seq")) + (P(),) * 15 + (tokens,),
        out_specs=(tokens, tokens) + (P(),) * 15,
        check_vma=False,
    )
```

time: 667 us -> 295 us (0.44)
  waiting for transfers between devices: 483 us -> 0 us
  Pallas kernels: 0 us -> 200 us
  blocking collectives: 55.5 us -> 0 us
  local copies, waits for them, and re-layouts: 41 us -> 12.8 us
  other arithmetic: 10.4 us -> 27.2 us
  between operations: 14.4 us -> 1.48 us
  matrix products: 61.2 us -> 52.7 us
    psum x1 -> x0, waiting for transfers between devices: 391 us -> none  [on_device(): lax.psum((grad_w_query, grad_b_query, grad_w_key, grad_w_value, grad_b_va...]
    pallas_call x0 -> x2, Pallas kernels: none -> 200 us  [the longest x1 178 us: all_sums(): pl.pallas_call(functools.partial(sums_kernel, plan, seq_size), out_shape=...]
    all_gather x1 -> x0, waiting for transfers between devices: 50.1 us -> none  [on_device(): lax.all_gather(stacked, 'seq', axis=2, tiled=True)]
    psum x1 -> x0, blocking collectives: 42.9 us -> none  [on_device(): lax.psum((grad_w_query, grad_b_query, grad_w_key, grad_w_value, grad_b_va...]
    reduce_scatter x2 -> x0, waiting for transfers between devices: 42.1 us -> none  [the longest x1 34.3 us: on_device(): lax.psum_scatter(ungrouped(value_part).astype(jnp.bfloat16), 'seq', scatt...]
    convert_element_type x0 -> x7, other arithmetic: none -> 22.9 us  [the longest x6 18.3 us: on_device(): up = lambda a: a.astype(F32)]
    unnamed x110 -> x128, local copies, waits for them, and re-layouts: 24.8 us -> 2.75 us
    all_gather x1 -> x0, blocking collectives: 12.6 us -> none  [on_device(): lax.all_gather(segment_ids, 'seq', axis=1, tiled=True)]
  transfers between devices with their start and end apart: 4 -> 0, of which waited for: 4 -> 0; matrix products, arithmetic and copies ran while one was open for 6% -> 0% of each run, Pallas kernels for 0% -> 0%
where the time goes in v1:
time: 295 us; the launch traced here: 294 us
  Pallas kernels  200 us (68%)
  matrix products  52.7 us (18%)
  other arithmetic  27.2 us (9%)
  local copies, waits for them, and re-layouts  12.8 us (4%)
    pallas_call x1, Pallas kernels, all_sums(): pl.pallas_call(functools.partial(sums_kernel, plan, seq_size), out_shape=...  178 us
    pallas_call x1, Pallas kernels, gather_rows(): pl.pallas_call(functools.partial(gather_kernel, seq_size), out_shape=(jax...  21.6 us
    convert_element_type x6, other arithmetic, on_device(): up = lambda a: a.astype(F32)  18.3 us
    dot_general x6, matrix products, product_tn(): lax.dot_general(left, right, (((0,), (0,)), ((), ())), preferred_element_...  15.3 us
    dot_general x6, matrix products, product(): return jnp.dot(left, right, preferred_element_type=F32)  10.2 us
    dot_general x6, matrix products, product_nt(): lax.dot_general(left, right, (((1,), (1,)), ((), ())), preferred_element_...  9.58 us

profile of v1, /device:TPU:0, one launch (start us, length us, event | category | flops | bytes accessed | tf_op | source)
XLA Modules:
  0.0 294.0 jit_solution(12578211526673296803)
XLA Ops:
  0.7 1.4 broadcast_in_dim.16.seg_ref
  2.1 21.6 %gather_rows.1 = (bf16[512,768]{1,0:T(8,128)(2,1)}, bf16[256,768]{1,0:T(8,128)(2,1)}, s32[4,8,128]{2,1,0:T(8,128)}) custom-call(bf16[2,128,768]{2,1,0:T(8,128)(2,1)} %x_ref.1, bf16[2,128,768]{2,1,0:T(8,128)(2,1)} %cot_ref.1, s32[2,8,128]{2,1,0:T(8,128)} %broadcast_in_dim.16.seg_ref), custom_call_target="tpu_custom_call" | custom-call | tf_op jit(solution)/shard_map/gather_rows/pallas_call | solution.py:169
  24.7 1.8 fusion.13
  27.8 5.0 %fusion.38 = (f32[12,256]{1,0:T(8,128)S(1)}, f32[12,256,512]{2,1,0:T(8,128)}) fusion(pred[256,512]{1,0:T(8,128)(4,1)S(1)} %broadcast_compare_fusion, bf16[256,12,64]{0,2,1:T(8,128)(2,1)S(1)} %bitcast.73, bf16[512,12,64]{0,2,1:T(8,128)(2,1)S(1)} %bitcast.71), kind=kOutput, calls=%fused_computation.99 | convolution fusion | flops 207618560 | bytes 7614464 | tf_op jit(solution)/shard_map/sub | solution.py:651
  32.8 4.6 %fusion.9 = bf16[12,256,512]{2,1,0:T(8,128)(2,1)} fusion(f32[12,256,512]{2,1,0:T(8,128)} %get-tuple-element.63, f32[12,256]{1,0:T(8,128)S(1)} %get-tuple-element.62), kind=kLoop, calls=%fused_computation.21 | loop fusion | flops 3145728 | bytes 9449472 | tf_op jit(solution)/shard_map/convert_element_type | solution.py:654
  37.5 1.7 add_convert_fusion
  39.1 1.5 copy.42
  40.7 4.1 %fusion.39 = (bf16[256,12,64]{0,2,1:T(8,128)(2,1)S(1)}, f32[256,12,64]{0,2,1:T(8,128)}) fusion(bf16[512,12,64]{0,2,1:T(8,128)(2,1)S(1)} %bitcast.67, bf16[12,256,512]{2,1,0:T(8,128)(2,1)} %fusion.9), kind=kOutput, calls=%fused_computation.100 | convolution fusion | flops 201523200 | bytes 5111808 | tf_op jit(solution)/shard_map/hqk,khd->qhd/dot_general | solution.py:655
  45.8 3.8 %multiply_convert_fusion.1 = (bf16[256,3072]{1,0:T(8,128)(2,1)S(1)}, f32[256,3072]{1,0:T(8,128)S(1)}) fusion(f32[3072]{0:T(1024)S(1)} %copy-done.56, bf16[768,3072]{1,0:T(8,128)(2,1)} %param.29, f32[256,768]{1,0:T(8,128)S(1)} %get-tuple-element.67, f32[768]{0:T(1024)S(1)} %copy-done.38, f32[768]{0:T(1024)S(1)} %copy-done.37, f32[256]{0:T(256)S(1)} %add_rsqrt_fusion.1, ...), kind=kOutput, calls=%fused_computation.15 | convolution fusion | flops 1213661184 | bytes 10244096 | tf_op jit(solution)/shard_map/dot_general | solution.py:21
  49.6 1.5 fusion.41
  51.4 1.8 fusion.21
  54.1 3.0 %convert_reduce_fusion = (f32[3072]{0:T(1024)}, bf16[256,3072]{1,0:T(8,128)(2,1)S(1)}) fusion(f32[256,3072]{1,0:T(8,128)S(1)} %get-tuple-element.69, bf16[3072,768]{1,0:T(8,128)(2,1)S(1)} %bitcast.81, f32[256,768]{1,0:T(8,128)S(1)} %get-tuple-element.58), kind=kOutput, calls=%fused_computation.14 | convolution fusion | flops 1217590272 | bytes 10235904 | tf_op jit(solution)/shard_map/dot_general | solution.py:29
  57.1 2.2 multiply_reduce_fusion
  60.2 1.3 convolution_convert_fusion.8
  62.7 2.7 convert_reduce_fusion.1
  65.6 3.9 %multiply_convert_fusion = bf16[12,256,512]{2,1,0:T(8,128)(2,1)S(1)} fusion(f32[12,256]{1,0:T(8,128)S(1)} %bitcast.77, bf16[256,12,64]{0,2,1:T(8,128)(2,1)S(1)} %bitcast.66, bf16[512,12,64]{0,2,1:T(8,128)(2,1)S(1)} %bitcast.68, f32[12,256,512]{2,1,0:T(8,128)} %get-tuple-element.63, f32[12,256]{1,0:T(8,128)S(1)} %copy-done.43), kind=kOutput, calls=%fused_computation.1 | convolution fusion | flops 207618048 | bytes 10641408 | tf_op jit(solution)/shard_map/qhd,khd->hqk/dot_general | solution.py:683
  74.1 1.5 fusion.10.dx_in
  75.6 1.9 dynamic-slice_convert_fusion.dxs_in
  77.8 1.3 concatenate.3.small_in
  79.1 3.1 %convolution_convert_fusion.2.v_in = bf16[768,768]{1,0:T(8,128)(2,1)} fusion(bf16[512,768]{1,0:T(8,128)(2,1)} %get-tuple-element.29, bf16[512,768]{0,1:T(8,128)(2,1)S(1)} %bitcast.70), kind=kOutput, calls=%fused_computation.25 | convolution fusion | flops 604569600 | bytes 2752512 | tf_op jit(solution)/shard_map/dot_general | solution.py:25
  82.2 1.9 convolution_convert_fusion.3.k_in
  84.0 1.5 convolution_convert_fusion.4.q_in
  85.6 1.5 convolution_convert_fusion.5.o_in
  87.1 3.8 %convolution_convert_fusion.inner_in = bf16[768,3072]{1,0:T(8,128)(2,1)} fusion(bf16[256,3072]{1,0:T(8,128)(2,1)S(1)} %copy-done.21, f32[256,768]{1,0:T(8,128)S(1)} %get-tuple-element.67, f32[768]{0:T(1024)S(1)} %copy-done.38, f32[768]{0:T(1024)S(1)} %copy-done.37, f32[256]{0:T(256)S(1)} %copy-done.50, f32[256]{0:T(256)S(1)} %copy-done.41), kind=kOutput, calls=%fused_computation.4 | convolution fusion | flops 1211301888 | bytes 7086080 | tf_op jit(solution)/shard_map/dot_general | solution.py:25
  90.8 3.6 %convolution_convert_fusion.1.outer_in = bf16[3072,768]{1,0:T(8,128)(2,1)} fusion(bf16[256,3072]{1,0:T(8,128)(2,1)S(1)} %copy-done.7, f32[256,768]{1,0:T(8,128)S(1)} %copy-done.12), kind=kOutput, calls=%fused_computation.5 | convolution fusion | flops 1210515456 | bytes 7077888 | tf_op jit(solution)/shard_map/dot_general | solution.py:25
  94.5 178.3 %all_sums.1 = (bf16[3072,768]{1,0:T(8,128)(2,1)}, bf16[768,3072]{1,0:T(8,128)(2,1)}, bf16[768,768]{1,0:T(8,128)(2,1)}, bf16[768,768]{1,0:T(8,128)(2,1)}, bf16[76...) custom-call(bf16[3072,768]{1,0:T(8,128)(2,1)} %convolution_convert_f, ...), custom_call_target="tpu_custom_call" | custom-call | tf_op jit(solution)/shard_map/all_sums/pallas_call | solution.py:593
  272.8 7.5 %convert_element_type.182 = f32[768,3072]{1,0:T(8,128)} convert(bf16[768,3072]{1,0:T(8,128)(2,1)} %get-tuple-element.39) | non-fusion elementwise | flops 2359296 | bytes 14155776 | tf_op jit(solution)/shard_map/convert_element_type | solution.py:724
  280.4 4.5 %convert_element_type.183 = f32[3072,768]{1,0:T(8,128)} convert(bf16[3072,768]{1,0:T(8,128)(2,1)S(1)} %copy-done.3) | non-fusion elementwise | flops 2359296 | bytes 14155776 | tf_op jit(solution)/shard_map/convert_element_type | solution.py:724
  284.8 1.6 convert_element_type.178
  286.5 1.6 convert_element_type.179
  288.1 1.6 convert_element_type.180
  289.7 1.6 convert_element_type.181
  (167 shorter events, 14.0 us)
Async XLA Ops:
  0.7 26.1 %copy-start = (bf16[768,768]{1,0:T(8,128)(2,1)S(1)}, bf16[768,768]{1,0:T(8,128)(2,1)}, u32[]{:S(2)}) copy-start(bf16[768,768]{1,0:T(8,128)(2,1)} %param.22) | copy-start | bytes 3538948
  26.7 6.1 %copy-start.17 = (bf16[256,768]{0,1:T(8,128)(2,1)}, bf16[256,768]{0,1:T(8,128)(2,1)S(1)}, u32[]{:S(2)}) copy-start(bf16[256,768]{0,1:T(8,128)(2,1)S(1)} %copy.43) | copy-start | bytes 1179652
  27.8 5.0 %copy-start.15 = (bf16[512,768]{0,1:T(8,128)(2,1)}, bf16[512,768]{0,1:T(8,128)(2,1)S(1)}, u32[]{:S(2)}) copy-start(bf16[512,768]{0,1:T(8,128)(2,1)S(1)} %copy.44) | copy-start | bytes 2359300
  32.8 4.6 %copy-start.42 = (f32[12,256]{1,0:T(8,128)}, f32[12,256]{1,0:T(8,128)S(1)}, u32[]{:S(2)}) copy-start(f32[12,256]{1,0:T(8,128)S(1)} %get-tuple-element.62) | copy-start | bytes 36868
  32.8 4.6 %copy-start.22 = (bf16[768,768]{1,0:T(8,128)(2,1)S(1)}, bf16[768,768]{1,0:T(8,128)(2,1)}, u32[]{:S(2)}) copy-start(bf16[768,768]{1,0:T(8,128)(2,1)} %param.23) | copy-start | bytes 3538948
  32.8 4.6 %copy-start.30 = (bf16[512,768]{1,0:T(8,128)(2,1)S(1)}, bf16[512,768]{1,0:T(8,128)(2,1)}, u32[]{:S(2)}) copy-start(bf16[512,768]{1,0:T(8,128)(2,1)} %get-tuple-element.29) | copy-start | bytes 2359300
  32.8 4.6 %copy-start.57 = (f32[768]{0:T(1024)S(1)}, f32[768]{0:T(1024)}, u32[]{:S(2)}) copy-start(f32[768]{0:T(1024)} %param.24) | copy-start | bytes 9220
  39.1 5.7 %copy-start.4 = (bf16[768,768]{1,0:T(8,128)(2,1)S(1)}, bf16[768,768]{1,0:T(8,128)(2,1)}, u32[]{:S(2)}) copy-start(bf16[768,768]{1,0:T(8,128)(2,1)} %param.25) | copy-start | bytes 3538948
  39.1 5.7 %copy-start.52 = (f32[768]{0:T(1024)S(1)}, f32[768]{0:T(1024)}, u32[]{:S(2)}) copy-start(f32[768]{0:T(1024)} %param.26) | copy-start | bytes 9220
  40.6 4.2 %copy-start.31 = (bf16[512,768]{1,0:T(8,128)(2,1)S(1)}, bf16[512,768]{1,0:T(8,128)(2,1)}, u32[]{:S(2)}) copy-start(bf16[512,768]{1,0:T(8,128)(2,1)} %get-tuple-element.29) | copy-start | bytes 2359300
  40.7 5.1 %copy-start.37 = (f32[768]{0:T(1024)S(1)}, f32[768]{0:T(1024)}, u32[]{:S(2)}) copy-start(f32[768]{0:T(1024)} %param.27) | copy-start | bytes 9220
  40.7 5.1 %copy-start.38 = (f32[768]{0:T(1024)S(1)}, f32[768]{0:T(1024)}, u32[]{:S(2)}) copy-start(f32[768]{0:T(1024)} %param.28) | copy-start | bytes 9220
  40.7 5.1 %copy-start.56 = (f32[3072]{0:T(1024)S(1)}, f32[3072]{0:T(1024)}, u32[]{:S(2)}) copy-start(f32[3072]{0:T(1024)} %param.30) | copy-start | bytes 36868
  45.5 13.9 %copy-start.40 = (f32[256]{0:T(256)}, f32[256]{0:T(256)S(1)}, u32[]{:S(2)}) copy-start(f32[256]{0:T(256)S(1)} %broadcast_multiply_fusion.5) | copy-start | bytes 3076
  45.7 13.6 %copy-start.49 = (f32[256]{0:T(256)}, f32[256]{0:T(256)S(1)}, u32[]{:S(2)}) copy-start(f32[256]{0:T(256)S(1)} %add_rsqrt_fusion.1) | copy-start | bytes 3076
  65.4 5.7 %copy-start.13 = (bf16[12,64,512]{2,1,0:T(8,128)(2,1)}, bf16[12,64,512]{2,1,0:T(8,128)(2,1)S(1)}, u32[]{:S(2)}) copy-start(bf16[12,64,512]{2,1,0:T(8,128)(2,1)S(1)} %get-tuple-element.76) | copy-start | bytes 2359300
  73.4 4.2 %copy-start.48 = (f32[768]{0:T(1024)S(1)}, f32[768]{0:T(1024)}, u32[]{:S(2)}) copy-start(f32[768]{0:T(1024)} %get-tuple-element.59) | copy-start | bytes 9220
  73.4 4.2 %copy-start.55 = (f32[768]{0:T(1024)S(1)}, f32[768]{0:T(1024)}, u32[]{:S(2)}) copy-start(f32[768]{0:T(1024)} %get-tuple-element.41) | copy-start | bytes 9220
  73.4 4.2 %copy-start.54 = (f32[768]{0:T(1024)S(1)}, f32[768]{0:T(1024)}, u32[]{:S(2)}) copy-start(f32[768]{0:T(1024)} %get-tuple-element.46) | copy-start | bytes 9220
  73.4 4.3 %copy-start.51 = (f32[3072]{0:T(1024)S(1)}, f32[3072]{0:T(1024)}, u32[]{:S(2)}) copy-start(f32[3072]{0:T(1024)} %get-tuple-element.77) | copy-start | bytes 36868
  73.5 4.3 %copy-start.47 = (f32[768]{0:T(1024)S(1)}, f32[768]{0:T(1024)}, u32[]{:S(2)}) copy-start(f32[768]{0:T(1024)} %get-tuple-element.57) | copy-start | bytes 9220
  73.5 4.3 %copy-start.46 = (f32[768]{0:T(1024)S(1)}, f32[768]{0:T(1024)}, u32[]{:S(2)}) copy-start(f32[768]{0:T(1024)} %get-tuple-element.43) | copy-start | bytes 9220
  73.5 4.3 %copy-start.45 = (f32[768]{0:T(1024)S(1)}, f32[768]{0:T(1024)}, u32[]{:S(2)}) copy-start(f32[768]{0:T(1024)} %get-tuple-element.48) | copy-start | bytes 9220
  73.5 5.6 %copy-start.14 = (bf16[12,64,512]{2,1,0:T(8,128)(2,1)S(1)}, bf16[12,64,512]{2,1,0:T(8,128)(2,1)}, u32[]{:S(2)}) copy-start(bf16[12,64,512]{2,1,0:T(8,128)(2,1)} %copy-done.13) | copy-start | bytes 2359300
  82.2 4.9 %copy-start.21 = (bf16[256,3072]{1,0:T(8,128)(2,1)S(1)}, bf16[256,3072]{1,0:T(8,128)(2,1)}, u32[]{:S(2)}) copy-start(bf16[256,3072]{1,0:T(8,128)(2,1)} %copy-done.20) | copy-start | bytes 4718596
  82.2 4.9 %copy-start.41 = (f32[256]{0:T(256)S(1)}, f32[256]{0:T(256)}, u32[]{:S(2)}) copy-start(f32[256]{0:T(256)} %copy-done.40) | copy-start | bytes 3076
  82.2 4.9 %copy-start.50 = (f32[256]{0:T(256)S(1)}, f32[256]{0:T(256)}, u32[]{:S(2)}) copy-start(f32[256]{0:T(256)} %copy-done.49) | copy-start | bytes 3076
  272.8 7.5 %copy-start.3 = (bf16[3072,768]{1,0:T(8,128)(2,1)S(1)}, bf16[3072,768]{1,0:T(8,128)(2,1)}, u32[]{:S(2)}) copy-start(bf16[3072,768]{1,0:T(8,128)(2,1)} %get-tuple-element.40) | copy-start | bytes 14155780
  280.4 4.5 %copy-start.27 = (bf16[768,768]{1,0:T(8,128)(2,1)S(1)}, bf16[768,768]{1,0:T(8,128)(2,1)}, u32[]{:S(2)}) copy-start(bf16[768,768]{1,0:T(8,128)(2,1)} %get-tuple-element.34) | copy-start | bytes 3538948
  288.1 4.5 %copy-start.36 = (bf16[2,128,768]{2,1,0:T(8,128)(2,1)S(1)}, bf16[2,128,768]{2,1,0:T(8,128)(2,1)}, u32[]{:S(2)}) copy-start(bf16[2,128,768]{2,1,0:T(8,128)(2,1)} %get-tuple-element.98) | copy-start | bytes 1179652
  288.1 5.2 %copy-start.35 = (bf16[2,128,768]{2,1,0:T(8,128)(2,1)S(1)}, bf16[2,128,768]{2,1,0:T(8,128)(2,1)}, u32[]{:S(2)}) copy-start(bf16[2,128,768]{2,1,0:T(8,128)(2,1)} %get-tuple-element.99) | copy-start | bytes 1179652
  288.1 5.9 %copy-start.1 = (bf16[768,768]{1,0:T(8,128)(2,1)S(1)}, bf16[768,768]{1,0:T(8,128)(2,1)}, u32[]{:S(2)}) copy-start(bf16[768,768]{1,0:T(8,128)(2,1)} %param.22) | copy-start | bytes 3538948
  (31 other events, 86.3 us)

commit v2 on v1

v2 whole, which is shorter than its diff:
```python
import functools

import jax
import jax.numpy as jnp
from jax import lax
from jax.experimental import pallas as pl
from jax.experimental.pallas import tpu as pltpu
from jax.sharding import PartitionSpec as P

HD = 64
EPSILON = 1e-12
MASKED = -1000000000.0
INV_ROOT_TWO = 0.7071067811865476
DENSITY = 0.3989422804014327
MESH = pl.DeviceIdType.MESH
BF16 = jnp.bfloat16
F32 = jnp.float32


def product(left, right):
    return jnp.dot(left, right, preferred_element_type=F32)


def product_tn(left, right):
    return lax.dot_general(left, right, (((0,), (0,)), ((), ())), preferred_element_type=F32)


def product_nt(left, right):
    return lax.dot_general(left, right, (((1,), (1,)), ((), ())), preferred_element_type=F32)


def place(seq_size):
    dp, sq = lax.axis_index("dp"), lax.axis_index("seq")
    side = dp % 2
    return dp, sq, side, dp - side


GROUP = 1536
PIECE = 512
ORDERS = (("x", "y", "z"), ("y", "z", "x"), ("z", "x", "y"))
SUBS = 1


class Exchange:
    def __init__(self, dp_size, seq_size, groups):
        self.dp_size, self.seq_size, self.groups = dp_size, seq_size, groups
        self.extra = []
        bit = 8
        while bit < dp_size:
            self.extra.append(bit)
            bit *= 2
        self.sems = 0
        self.slots = 0
        self.pieces = []
        for g in range(groups):
            for cls in range(3):
                self.pieces.append(self.plan(g * GROUP + cls * PIECE, ORDERS[cls]))

    def sem(self):
        self.sems += 1
        return self.sems - 1

    def slot(self, rows):
        self.slots += rows
        return self.slots - rows

    def plan(self, base, order):
        stages, rows, ends = [], PIECE, False
        for axis in ("c",) + order:
            half = rows // 2
            st = dict(axis=axis, rows=half, ends=ends)
            if axis == "z":
                n = half // SUBS
                st["down"] = [dict(rs=self.sem(), ag=self.sem(), slot=self.slot(n), rows=n, at=i * n) for i in range(SUBS)]
                st["up"] = [dict(rs=self.sem(), ag=self.sem(), slot=self.slot(n), rows=n, at=i * n) for i in range(SUBS)]
                ends = True
            else:
                st.update(rs=self.sem(), ag=self.sem(), slot=None if axis == "c" else self.slot(half))
            stages.append(st)
            rows = half
        more = [dict(bit=b, rs=self.sem(), slot=self.slot(rows)) for b in self.extra]
        return dict(base=base, stages=stages, more=more, rows=rows)

    def bind(self, total, slots, final, send_sem, recv_sem):
        self.total, self.landing, self.final = total, slots, final
        self.ss, self.rs = send_sem, recv_sem
        dp, sq = lax.axis_index("dp"), lax.axis_index("seq")
        self.dp, self.sq = dp, sq
        self.bits = {"c": (1, dp % 2), "x": (2, (dp // 2) % 2), "y": (4, (dp // 4) % 2)}
        self.last = self.seq_size - 1
        self.edge = jnp.logical_or(sq == 0, sq == self.last)
        self.side = sq // self.last
        self.sent = []
        for p in self.pieces:
            off = p["base"]
            for st in p["stages"]:
                half = st["rows"]
                st["off"] = off
                value = self.side if st["axis"] == "z" else self.bits[st["axis"]][1]
                st["keep"] = off + value * half
                st["give"] = off + (1 - value) * half
                off = st["keep"]
            p["own"] = off

    def view(self, off, rows):
        return self.total.at[pl.ds(pl.multiple_of(off, 16), rows)]

    def partner(self, axis):
        bit, value = self.bits[axis]
        return (self.dp + bit * (1 - 2 * value), self.sq)

    def copy(self, src, dst, sem, tgt):
        return pltpu.make_async_remote_copy(src, dst, self.ss.at[sem], self.rs.at[sem], tgt, MESH)

    def send(self, make, when):
        self.sent.append((make, when))
        make().start()

    def gated(self, when, f):
        if when is None:
            f()
        else:
            pl.when(when)(f)

    def done(self, off, rows):
        return self.final.at[pl.ds(pl.multiple_of(off, 16), rows)]

    def landed(self, st):
        if st["slot"] is None:
            return self.done(st["give"], st["rows"])
        return self.landing.at[pl.ds(st["slot"], st["rows"])]

    def add(self, off, slot, rows, into=None):
        into = self.total if into is None else into
        source = self.final if slot is None else self.landing
        slot = off if slot is None else slot
        step = 32 if rows % 32 == 0 else 16

        def body(i, _):
            at = pl.multiple_of(off + i * step, 16)
            frm = pl.multiple_of(slot + i * step, 16)
            into[pl.ds(at, step)] = self.total[pl.ds(at, step)] + source[pl.ds(frm, step)]
            return 0

        lax.fori_loop(0, rows // step, body, 0)


    def rs_start(self, p, i):
        st = p["stages"][i]
        if st["axis"] == "z":
            for way, at, to, base in (("down", self.last, -1, 0), ("up", 0, 1, st["rows"])):
                when = self.sq == at

                def f(way=way, to=to, base=base, when=when):
                    for s in st[way]:
                        self.send(lambda s=s: self.rs_copy(st, s, base, to), when)
                self.gated(when, f)
        else:
            when = self.edge if st["ends"] else None

            def f():
                self.send(
                    lambda: self.copy(
                        self.view(st["give"], st["rows"]), self.landed(st), st["rs"], self.partner(st["axis"]),
                    ),
                    when,
                )
            self.gated(when, f)

    def rs_hyper(self, p, i):
        st = p["stages"][i]

        def f():
            self.copy(
                self.view(st["give"], st["rows"]), self.landed(st), st["rs"], self.partner(st["axis"]),
            ).wait_recv()
            self.add(st["keep"], st["slot"], st["rows"], self.final if i + 1 == len(p["stages"]) else None)
        self.gated(self.edge if st["ends"] else None, f)

    def rs_hop(self, p, i, hop):
        st = p["stages"][i]
        for way, at, to, base in (("down", self.last - hop, -1, 0), ("up", hop, 1, st["rows"])):
            when = self.sq == at

            def f(way=way, to=to, base=base, when=when):
                for s in st[way]:
                    self.rs_copy(st, s, base, -to).wait_recv()
                    ended = hop == self.last and i + 1 == len(p["stages"])
                    self.add(st["off"] + base + s["at"], s["slot"], s["rows"], self.final if ended else None)
                    if hop < self.last:
                        self.send(lambda s=s: self.rs_copy(st, s, base, to), when)
            self.gated(when, f)

    def rs_copy(self, st, s, base, to):
        return self.copy(
            self.view(st["off"] + base + s["at"], s["rows"]), self.landing.at[pl.ds(s["slot"], s["rows"])],
            s["rs"], (self.dp, self.sq + to),
        )

    def more(self, p):
        for m in p["more"]:
            bit = m["bit"]
            value = (self.dp // bit) % 2
            tgt = (self.dp + bit * (1 - 2 * value), self.sq)

            def f():
                c = self.copy(
                    self.done(p["own"], p["rows"]), self.landing.at[pl.ds(m["slot"], p["rows"])], m["rs"], tgt
                )
                c.start()
                c.wait()
                part = pl.ds(pl.multiple_of(p["own"], 16), p["rows"])
                self.final[part] = self.final[part] + self.landing[pl.ds(m["slot"], p["rows"])]
            self.gated(self.edge, f)


    def ag_start(self, p, i):
        st = p["stages"][i]
        if st["axis"] == "z":
            for way, at, to, base in (("down", self.last, -1, st["rows"]), ("up", 0, 1, 0)):
                when = self.sq == at

                def f(way=way, to=to, base=base, when=when):
                    for s in st[way]:
                        self.send(lambda s=s: self.ag_copy(st, s, base, to), when)
                self.gated(when, f)
        else:
            when = self.edge if st["ends"] else None

            def f():
                self.send(
                    lambda: self.copy(
                        self.done(st["keep"], st["rows"]), self.done(st["keep"], st["rows"]),
                        st["ag"], self.partner(st["axis"]),
                    ),
                    when,
                )
            self.gated(when, f)

    def ag_copy(self, st, s, base, to):
        part = self.done(st["off"] + base + s["at"], s["rows"])
        return self.copy(part, part, s["ag"], (self.dp, self.sq + to))

    def ag_hyper(self, p, i):
        st = p["stages"][i]

        def f():
            part = self.done(st["give"], st["rows"])
            self.copy(part, part, st["ag"], self.partner(st["axis"])).wait_recv()
        self.gated(self.edge if st["ends"] else None, f)

    def ag_hop(self, p, i, hop):
        st = p["stages"][i]
        for way, at, to, base in (("down", self.last - hop, -1, st["rows"]), ("up", hop, 1, 0)):
            when = self.sq == at

            def f(way=way, to=to, base=base, when=when):
                for s in st[way]:
                    self.ag_copy(st, s, base, -to).wait_recv()
                    if hop < self.last:
                        self.send(lambda s=s: self.ag_copy(st, s, base, to), when)
            self.gated(when, f)

    def script(self, p):
        steps, n = [], len(p["stages"])
        for i, st in enumerate(p["stages"]):
            after = (lambda i=i: self.rs_start(p, i + 1)) if i + 1 < n else (lambda: (self.more(p), self.ag_start(p, n - 1)))
            if st["axis"] == "z":
                for hop in range(1, self.last + 1):
                    def step(i=i, hop=hop, after=after):
                        self.rs_hop(p, i, hop)
                        if hop == self.last:
                            after()
                    steps.append((f"rz{hop}", step))
            else:
                def step(i=i, after=after):
                    self.rs_hyper(p, i)
                    after()
                steps.append(("r" + st["axis"], step))
        for i in reversed(range(n)):
            st = p["stages"][i]
            after = (lambda i=i: self.ag_start(p, i - 1)) if i > 0 else (lambda: None)
            if st["axis"] == "z":
                for hop in range(1, self.last + 1):
                    def step(i=i, hop=hop, after=after):
                        self.ag_hop(p, i, hop)
                        if hop == self.last:
                            after()
                    steps.append((f"gz{hop}", step))
            else:
                def step(i=i, after=after):
                    self.ag_hyper(p, i)
                    after()
                steps.append(("g" + st["axis"], step))
        return steps

    def finish(self):
        for make, when in self.sent:
            self.gated(when, lambda make=make: make().wait_send())


def small_bits(dp_size, seq_size):
    out, bit = [], 1
    while bit < dp_size:
        out.append(("dp", bit))
        bit *= 2
    bit = 1
    while bit < seq_size:
        out.append(("seq", bit))
        bit *= 2
    return out


D = 768
FF = 3072
OUTER, INNER, PROJ = 0, 3072, 6144
ORDER = (
    -1, -2, -3, 0, 1, 2, 3, 4, -4, 5, -5, 0, 6, 1, 2, 7, 8, -6, 3, 4, 5, -7, 9, 0,
    1, 10, 2, 6, 11, -8, 7, 8, 5, -9, 3, 4, 9, 1, 0, 2, 10, 8, -10, 11, 5, 2, 6, 4,
    7, 0, 1, 9, 3, 2, -11, 10, 5, 6, 8, 1, 9, 2, 4, 11, 0, -12, 7, 5, -13, 3, 8, 0,
    12, 1, 13, 5, 10, 14, 11, 6, 15, 2, 9, 16, 8, 4, 7, 0, 17, 3, 1, -14, -15, 10, 12, 13,
    6, 1, 9, 14, 5, 0, 11, 16, 1, -16, 8, 2, 14, 12, 15, 4, 0, 17, 7, 11, 3, 2, -17, 10,
    14, 13, 8, 6, 1, 9, 17, 1, 3, 15, 2, -18, 0, 11, 13, 2, 7, 5, 0, 6, 10, 9, 17, 16,
    -19, 14, 3, 12, 11, 13, 14, 4, 5, 6, 17, 9, 3, -20, 16, 13, 14, 12, 8, 6, 15, 4, 5, 17,
    7, 3, 5, 16, 9, 13, 12, 17, 3, 10, 8, 14, 15, 4, 7, 11, 6, 10, 8, 13, 16, 15, 6, 4,
    12, 8, 7, 4, 11, 9, 10, 14, 13, 9, 15, 17, 12, 16, 7, 11, 7, 14, 11, 13, 15, 17, 12, 10,
    16, 10, 14, 13, 15, 17, 14, 12, 13, 16, 15, 17, 12, 17, 16, 12, 15, 15, 16, 16,
)


SMALL_PARTS = 5


def fold(values):
    return jnp.sum(values.reshape(values.shape[0] // 8, 8, values.shape[1]), axis=0)


def layer_kernel(
    plan, seq_size,
    x_ref, cot_ref, seg_ref, wq_hbm, wk_hbm, wv_hbm, wo_hbm, win_hbm, wout_hbm,
    bq, bv, bo, g1, s1, bi, b2, g2, s2,
    final, small_out, y_out, dx_out,
    total, landing, wproj, xf, qs, key, val, probs, attn, normed, inv1, hid, hid_t, active, slope, cot, ybuf, gout, acc,
    mask, sg, dx_far, small,
    ss, rs, gs_, gr, gl, ws, ms, mr, ys, yr, xs,
):
    plan.bind(total, landing, final, ss, rs)
    dp, sq, side, pair = place(seq_size)
    sibling = (dp + 1 - 2 * side, sq)
    rows, length = x_ref.shape[0], x_ref.shape[1]
    spread = seq_size // 2
    tokens = spread * length
    own, far = side * tokens, (1 - side) * tokens

    loads = {}

    def load(name, src, dst, i):
        loads.setdefault(name, []).append(pltpu.make_async_copy(src, dst, ws.at[i]))
        loads[name][-1].start()

    for i, (name, src) in enumerate((("q", wq_hbm), ("k", wk_hbm), ("v", wv_hbm), ("o", wo_hbm))):
        load(name, src, wproj.at[i], i)
    for j in range(4):
        load("in", win_hbm.at[:, pl.ds(j * D, D)], total.at[pl.ds(INNER + j * D, D)], 4 + j)
    load("out", wout_hbm, total.at[pl.ds(PROJ, FF)], 8)

    def loaded(name):
        for c in loads[name]:
            c.wait()

    half, spot = sq // spread, sq % spread

    def block(i):
        return pl.ds(pl.multiple_of(i * length, length), length)

    def x_copy(r, b, tgt, at):
        return pltpu.make_async_remote_copy(x_ref.at[r], xf.at[block(at)], gs_.at[0, r], gr.at[0, b], tgt, MESH)

    def c_copy(r, b, tgt):
        return pltpu.make_async_remote_copy(cot_ref.at[r], cot.at[block(b)], gs_.at[1, r], gr.at[1, b], tgt, MESH)

    def s_copy(r, c, at, tgt):
        return pltpu.make_async_remote_copy(seg_ref.at[r], sg.at[at], gs_.at[2 + c, r], gr.at[2, at], tgt, MESH)

    def forward(b, base):
        part = xf.at[block(base + b)]
        return pltpu.make_async_remote_copy(part, part, gs_.at[4, b], gr.at[3, b], sibling, MESH)

    def split(local, near, remote):
        pl.when(local)(near)
        pl.when(jnp.logical_not(local))(remote)

    stays = [jnp.logical_and(half == side, sq == rows * side + r) for r in range(rows)]
    comes = [jnp.logical_and(sq // rows == side, side * spread + b == sq) for b in range(spread)]

    def x_local(r, at):
        return pltpu.make_async_copy(x_ref.at[r], xf.at[block(at)], gl.at[0])

    def c_local(r, at):
        return pltpu.make_async_copy(cot_ref.at[r], cot.at[block(at)], gl.at[1])

    def s_local(r):
        return pltpu.make_async_copy(seg_ref.at[r], sg.at[sq], gl.at[2])

    for r in range(rows):
        at = half * spread + spot
        split(
            stays[r],
            lambda r=r, at=at: x_local(r, at).start(),
            lambda r=r, at=at: x_copy(r, spot, (pair + half, rows * side + r), at).start(),
        )
    mine = [[jnp.logical_and(side == c, sq == rows * side + r) for c in range(2)] for r in range(rows)]
    for r in range(rows):
        for c in range(2):
            split(
                mine[r][c],
                lambda r=r: s_local(r).start(),
                lambda r=r, c=c: s_copy(r, c, sq, (pair + c, rows * side + r)).start(),
            )
    for r in range(rows):
        split(
            stays[r],
            lambda r=r: c_local(r, spot).start(),
            lambda r=r: c_copy(r, spot, (pair + half, rows * side + r)).start(),
        )

    for b in range(spread):
        split(
            comes[b],
            lambda b=b: x_local(b, side * spread + b).wait(),
            lambda b=b: x_copy(0, b, sibling, side * spread + b).wait_recv(),
        )
        forward(b, side * spread).start()

    def token_block(which):
        return pl.ds(pl.multiple_of(which, tokens), tokens)

    def cols(i, n=256):
        return pl.ds(pl.multiple_of(i * n, 128), n)

    loaded("q")
    loaded("k")
    loaded("v")

    def project(which, also_query):
        def body(i, _):
            xb = xf[token_block(which)]
            c = cols(i)
            if also_query:
                qs[:, c] = (product(xb, wproj[0, :, c]) + bq[:, c]).astype(BF16) * BF16(0.125)
            key[token_block(which), c] = product(xb, wproj[1, :, c]).astype(BF16)
            val[token_block(which), c] = (product(xb, wproj[2, :, c]) + bv[:, c]).astype(BF16)
            return 0

        lax.fori_loop(0, D // 256, body, 0)

    project(own, True)

    for p in range(seq_size):
        split(
            jnp.logical_and(sq // rows == side, p == sq),
            lambda: s_local(0).wait(),
            lambda p=p: s_copy(0, 0, p, sibling).wait_recv(),
        )
    diagonal = lax.broadcasted_iota(jnp.int32, (length, length), 0) == lax.broadcasted_iota(
        jnp.int32, (length, length), 1
    )
    for b in range(spread):
        mine_seg = jnp.broadcast_to(sg[side * spread + b], (length, length))
        column = jnp.sum(jnp.where(diagonal, mine_seg, 0), axis=1, keepdims=True)
        for p in range(seq_size):
            seen = jnp.broadcast_to(column, (length, length)) == jnp.broadcast_to(sg[p], (length, length))
            mask[b * length : (b + 1) * length, p * length : (p + 1) * length] = jnp.where(seen, 0.0, MASKED)

    for b in range(spread):
        forward(b, (1 - side) * spread).wait_recv()
    project(far, False)

    lane = lax.broadcasted_iota(jnp.int32, (1, 128), 1)
    first = (lane < HD).astype(BF16)
    picks = (first, BF16(1.0) - first)
    low_lanes = lane < HD

    def attend(i, _):
        c = cols(i, 128)
        qp, kp, vp = qs[:, c], key[:, c], val[:, c]
        outs = []
        for n in range(2):
            s = product_nt(qp * picks[n], kp) + mask[...]
            e = jnp.exp(s - jnp.max(s, axis=-1, keepdims=True))
            p = (e * (1.0 / jnp.sum(e, axis=-1, keepdims=True))).astype(BF16)
            probs[2 * i + n] = p
            outs.append(product(p, vp))
        attn[:, c] = jnp.where(low_lanes, outs[0], outs[1]).astype(BF16)
        return 0

    lax.fori_loop(0, D // 128, attend, 0)

    loaded("o")

    def branch(i, _):
        c = cols(i)
        acc[:, c] = product(attn[...], wproj[3, :, c]) + bo[:, c] + xf[token_block(own), c].astype(F32)
        return 0

    lax.fori_loop(0, D // 256, branch, 0)
    step = 32

    def chunk(i):
        return pl.ds(pl.multiple_of(i * step, step), step)

    def norm_one(i, _):
        r = chunk(i)
        v = acc[r]
        centre = v - jnp.mean(v, axis=-1, keepdims=True)
        inv = lax.rsqrt(jnp.mean(centre * centre, axis=-1, keepdims=True) + EPSILON)
        n = centre * inv
        normed[r] = n
        inv1[r] = jnp.broadcast_to(inv, (step, 128))
        hid[r] = (n * g1[...] + s1[...]).astype(BF16)
        return 0

    lax.fori_loop(0, tokens // step, norm_one, 0)

    loaded("in")
    loaded("out")

    def inner_cols(j, i):
        return total.at[pl.ds(INNER + j * D, D), cols(i)]

    for j in range(4):

        def expand(i, _, j=j):
            c = cols(j * 3 + i)
            v = product(hid[...], inner_cols(j, i)[...]) + bi[:, c]
            cdf = 0.5 * (1.0 + lax.erf(v * INV_ROOT_TWO))
            active[:, c] = (v * cdf).astype(BF16)
            slope[:, c] = cdf + v * DENSITY * jnp.exp(-0.5 * v * v)
            return 0

        lax.fori_loop(0, 3, expand, 0)

    def contract(i, _):
        c = cols(i)
        acc[:, c] = product(active[...], total[pl.ds(PROJ, FF), c]) + b2[:, c]
        return 0

    lax.fori_loop(0, D // 256, contract, 0)
    for b in range(spread):
        split(comes[b], lambda b=b: c_local(b, b).wait(), lambda b=b: c_copy(0, b, sibling).wait_recv())

    small[0] = jnp.zeros((16, D), F32)

    def norm_two(i, carry):
        d_gain, d_shift, d_bias = carry
        r = chunk(i)
        v = normed[r] * g1[...] + s1[...] + acc[r]
        centre = v - jnp.mean(v, axis=-1, keepdims=True)
        inv = lax.rsqrt(jnp.mean(centre * centre, axis=-1, keepdims=True) + EPSILON)
        n = centre * inv
        ybuf[r] = (n * g2[...] + s2[...]).astype(BF16)
        g = cot[r].astype(F32)
        scaled = g * g2[...]
        grad = inv * (
            scaled - jnp.mean(scaled, axis=-1, keepdims=True) - n * jnp.mean(scaled * n, axis=-1, keepdims=True)
        )
        grad_low = grad.astype(BF16)
        gout[r] = grad_low
        acc[r] = grad
        return d_gain + fold(g * n), d_shift + fold(g), d_bias + fold(grad_low.astype(F32))

    zero = jnp.zeros((8, D), F32)
    sums = lax.fori_loop(0, tokens // step, norm_two, (zero, zero, zero))
    for at, v in zip((6, 7, 5), sums):
        small[0, at : at + 1] = jnp.sum(v, axis=0, keepdims=True)

    homes = [(pair + sq // rows, side * spread + b) for b in range(spread)]
    at_home = [jnp.logical_and(h[0] == dp, h[1] == sq) for h in homes]

    def back(src, dst, b, lane_, to, slot):
        return pltpu.make_async_remote_copy(
            src.at[pl.ds(b * length, length)], dst.at[slot], ys.at[lane_, b], yr.at[lane_, slot], to, MESH
        )

    def home_local(src, dst, b, lane_):
        return pltpu.make_async_copy(src.at[pl.ds(b * length, length)], dst.at[sq % rows], xs.at[2 + lane_])

    def send_home(src, dst, lane_):
        for b in range(spread):
            split(
                at_home[b],
                lambda b=b: home_local(src, dst, b, lane_).start(),
                lambda b=b: back(src, dst, b, lane_, homes[b], sq % rows).start(),
            )

    def sent_home(src, dst, lane_):
        for b in range(spread):
            split(
                at_home[b],
                lambda b=b: home_local(src, dst, b, lane_).wait(),
                lambda b=b: back(src, dst, b, lane_, homes[b], sq % rows).wait_send(),
            )
        for r in range(rows):
            pl.when(jnp.logical_not(jnp.logical_and(half == side, sq == rows * side + r)))(
                lambda r=r: back(src, dst, 0, lane_, sibling, r).wait_recv()
            )

    send_home(ybuf, y_out, 0)


    def outer_part(n):
        def body(i, _):
            t = n * 6 + i
            total[pl.ds(pl.multiple_of(OUTER + t * 256, 256), 256)] = product(
                active[:, cols(t)].T, gout[...]
            ).astype(BF16)
            return 0

        lax.fori_loop(0, 6, body, 0)

    def inner_part(j):
        if j == 0:
            for i in range(3):
                hid_t[i * 256 : (i + 1) * 256] = hid[:, i * 256 : (i + 1) * 256].T

        def body(i, _):
            t = j * 3 + i
            up = product_nt(gout[...], total[pl.ds(pl.multiple_of(PROJ + t * 256, 256), 256)])
            gi = (up * slope[:, cols(t)]).astype(BF16)
            small[0, 8 + j : 9 + j, cols(i)] = jnp.sum(fold(gi.astype(F32)), axis=0, keepdims=True)
            view = inner_cols(j, i)
            acc[...] += product_nt(gi, view[...])
            view[...] = product(hid_t[...], gi).astype(BF16)
            return 0

        lax.fori_loop(0, 3, body, 0)

    def norm_one_part():
        def body(i, carry):
            d_gain, d_shift, d_bias = carry
            r = chunk(i)
            g, n = acc[r], normed[r]
            scaled = g * g1[...]
            grad = inv1[r][:, :1] * (
                scaled - jnp.mean(scaled, axis=-1, keepdims=True) - n * jnp.mean(scaled * n, axis=-1, keepdims=True)
            )
            grad_low = grad.astype(BF16)
            gout[r] = grad_low
            acc[r] = grad
            return d_gain + fold(g * n), d_shift + fold(g), d_bias + fold(grad_low.astype(F32))

        out = lax.fori_loop(0, tokens // step, body, (zero, zero, zero))
        for at, v in zip((3, 4, 2), out):
            small[0, at : at + 1] = jnp.sum(v, axis=0, keepdims=True)

    def branch_part():
        def body(i, _):
            total[pl.ds(pl.multiple_of(PROJ + i * 256, 256), 256)] = product(attn[:, cols(i)].T, gout[...]).astype(BF16)
            cot[:, cols(i)] = product_nt(gout[...], wproj[3, pl.ds(pl.multiple_of(i * 256, 256), 256)]).astype(BF16)
            return 0

        lax.fori_loop(0, D // 256, body, 0)

    def attention_part(n):
        def body(m, _):
            i = n * 2 + m
            c = cols(i, 128)
            qp, kp, vp, gp = qs[:, c], key[:, c], val[:, c], cot[:, c]
            dq, dk, dv = [], [], []
            for h in range(2):
                p = probs[2 * i + h]
                pf = p.astype(F32)
                weighted = pf * product_nt(gp * picks[h], vp)
                delta = jnp.sum(weighted, axis=-1, keepdims=True)
                gs = (weighted - pf * delta).astype(BF16)
                dq.append(product(gs, kp))
                dk.append(product_tn(gs, qp))
                dv.append(product_tn(p, gp))
            gq = (jnp.where(low_lanes, dq[0], dq[1]) * 0.125).astype(BF16)
            gk = jnp.where(low_lanes, dk[0], dk[1]).astype(BF16)
            gv = jnp.where(low_lanes, dv[0], dv[1]).astype(BF16)
            qs[:, c] = gq
            small[0, 0:1, c] = jnp.sum(fold(gq.astype(F32)), axis=0, keepdims=True)
            small[0, 1:2, c] = jnp.sum(fold(gv.astype(F32)), axis=0, keepdims=True)
            for b in range(2):
                active[:, cols(b * 6 + i, 128)] = gk[b * tokens : (b + 1) * tokens]
                active[:, cols(12 + b * 6 + i, 128)] = gv[b * tokens : (b + 1) * tokens]
            return 0

        lax.fori_loop(0, 2, body, 0)

    def query_part():
        def body(i, _):
            total[pl.ds(pl.multiple_of(PROJ + D + i * 256, 256), 256)] = product(
                xf[token_block(own), cols(i)].T, qs[...]
            ).astype(BF16)
            return 0

        lax.fori_loop(0, D // 256, body, 0)

    def key_part():
        def body(i, _):
            left = xf[pl.ds(0, tokens), cols(i)].T
            right = xf[pl.ds(tokens, tokens), cols(i)].T
            for n in range(2):
                base = n * 2 * D
                total[pl.ds(pl.multiple_of(PROJ + (2 + n) * D + i * 256, 256), 256)] = (
                    product(left, active[:, base : base + D]) + product(right, active[:, base + D : base + 2 * D])
                ).astype(BF16)
            return 0

        lax.fori_loop(0, D // 256, body, 0)

    dx_send = pltpu.make_async_remote_copy(hid, dx_far, xs.at[0], xs.at[1], sibling, MESH)

    def input_part():
        def both(s, w):
            return product_nt(active[:, pl.ds(pl.multiple_of(s * D, 128), D)], wproj[1, w]) + product_nt(
                active[:, pl.ds(pl.multiple_of((2 + s) * D, 128), D)], wproj[2, w]
            )

        def body(i, _):
            w = pl.ds(pl.multiple_of(i * 256, 256), 256)
            hid[:, cols(i)] = both(1 - side, w).astype(BF16)
            acc[:, cols(i)] += product_nt(qs[...], wproj[0, w]) + both(side, w)
            return 0

        lax.fori_loop(0, D // 256, body, 0)
        dx_send.start()

    bits = small_bits(plan.dp_size, seq_size)

    def small_copy(i):
        axis, bit = bits[i]
        if axis == "dp":
            tgt = (dp + bit * (1 - 2 * ((dp // bit) % 2)), sq)
        else:
            tgt = (dp, sq + bit * (1 - 2 * ((sq // bit) % 2)))
        return pltpu.make_async_remote_copy(small.at[i], small.at[len(bits) + 1 + i], ms.at[i], mr.at[i], tgt, MESH)

    def input_end():
        dx_send.wait_recv()

        def body(i, _):
            r = chunk(i)
            gout[r] = (acc[r] + dx_far[r].astype(F32)).astype(BF16)
            return 0

        lax.fori_loop(0, tokens // step, body, 0)
        send_home(gout, dx_out, 1)
        small_copy(0).start()

    def small_part(n):
        for i in range(n, n + 1 if n < SMALL_PARTS - 1 else len(bits)):
            small_copy(i).wait_recv()
            small[i + 1] = small[i] + small[len(bits) + 1 + i]
            if i + 1 < len(bits):
                small_copy(i + 1).start()

    parts = (
        [functools.partial(outer_part, n) for n in range(2)]
        + [functools.partial(inner_part, j) for j in range(4)]
        + [norm_one_part, branch_part]
        + [functools.partial(attention_part, n) for n in range(3)]
        + [query_part, key_part, input_part, input_end]
        + [functools.partial(small_part, n) for n in range(SMALL_PARTS)]
    )
    ready = {0: (0,), 1: (1,), 3: (2,), 5: (3,), 11: (4,), 12: (5,)}
    scripts = [iter(plan.script(p)) for p in plan.pieces]
    for entry in ORDER:
        if entry >= 0:
            next(scripts[entry])[1]()
            continue
        parts[-entry - 1]()
        for g in ready.get(-entry - 1, ()):
            for p in plan.pieces[3 * g : 3 * g + 3]:
                plan.rs_start(p, 0)
    small_out[...] = small[len(bits)]
    for i in range(len(bits)):
        small_copy(i).wait_send()
    dx_send.wait_send()
    sent_home(ybuf, y_out, 0)
    sent_home(gout, dx_out, 1)
    for r in range(rows):
        for c in range(2):
            pl.when(jnp.logical_not(mine[r][c]))(lambda r=r, c=c: s_copy(r, c, sq, sibling).wait_send())
        pl.when(jnp.logical_not(stays[r]))(lambda r=r: x_copy(r, spot, sibling, 0).wait_send())
        pl.when(jnp.logical_not(stays[r]))(lambda r=r: c_copy(r, spot, sibling).wait_send())
    for b in range(spread):
        forward(b, side * spread).wait_send()
    plan.finish()


def whole_layer(args, dp_size, seq_size):
    (layer_input, segment_ids, w_query, b_query, w_key, w_value, b_value, w_out, b_out, gain_one, shift_one,
     w_inner, b_inner, w_outer, b_outer, gain_two, shift_two, cotangent) = args
    plan = Exchange(dp_size, seq_size, 6)
    rows, length, width = layer_input.shape
    tokens = seq_size * length // 2
    vmem, anyw = pl.BlockSpec(memory_space=pltpu.VMEM), pl.BlockSpec(memory_space=pl.ANY)
    nbits = len(small_bits(dp_size, seq_size))
    back = jax.ShapeDtypeStruct((rows, length, width), BF16)
    vector = lambda v: v.reshape(1, -1)
    dma = pltpu.SemaphoreType.DMA
    return pl.pallas_call(
        functools.partial(layer_kernel, plan, seq_size),
        out_shape=(pltpu.VMEM((3 * FF, D), BF16), jax.ShapeDtypeStruct((16, D), F32), back, back),
        in_specs=[anyw] * 9 + [vmem] * 9,
        out_specs=(vmem, vmem, anyw, anyw),
        scratch_shapes=[
            pltpu.VMEM((3 * FF, D), BF16),
            pltpu.VMEM((plan.slots, D), BF16),
            pltpu.VMEM((4, D, D), BF16),
            pltpu.VMEM((2 * tokens, D), BF16),
            pltpu.VMEM((tokens, D), BF16),
            pltpu.VMEM((2 * tokens, D), BF16),
            pltpu.VMEM((2 * tokens, D), BF16),
            pltpu.VMEM((D // HD, tokens, 2 * tokens), BF16),
            pltpu.VMEM((tokens, D), BF16),
            pltpu.VMEM((tokens, D), F32),
            pltpu.VMEM((tokens, 128), F32),
            pltpu.VMEM((tokens, D), BF16),
            pltpu.VMEM((D, tokens), BF16),
            pltpu.VMEM((tokens, FF), BF16),
            pltpu.VMEM((tokens, FF), F32),
            pltpu.VMEM((tokens, D), BF16),
            pltpu.VMEM((tokens, D), BF16),
            pltpu.VMEM((tokens, D), BF16),
            pltpu.VMEM((tokens, D), F32),
            pltpu.VMEM((tokens, 2 * tokens), F32),
            pltpu.VMEM((seq_size, 1, length), jnp.int32),
            pltpu.VMEM((tokens, D), BF16),
            pltpu.VMEM((2 * nbits + 1, 16, D), F32),
            dma((plan.sems,)), dma((plan.sems,)),
            dma((5, 2)), dma((4, seq_size)), dma((3,)), dma((9,)),
            dma((nbits,)), dma((nbits,)), dma((2, 2)), dma((2, 2)), dma((4,)),
        ],
        compiler_params=pltpu.CompilerParams(has_side_effects=True, vmem_limit_bytes=VMEM_LIMIT),
        name="layer",
    )(
        layer_input, cotangent, segment_ids.reshape(rows, 1, length), w_query, w_key, w_value, w_out, w_inner, w_outer,
        vector(b_query), vector(b_value), vector(b_out), vector(gain_one), vector(shift_one), vector(b_inner),
        vector(b_outer), vector(gain_two), vector(shift_two),
    )


VMEM_LIMIT = 48 << 20


def on_device(dp_size, seq_size, *args):
    sums, small, y, dx = whole_layer(args, dp_size, seq_size)
    up = sums.astype(F32)
    d_inner = jnp.concatenate([up[INNER + j * D : INNER + (j + 1) * D] for j in range(4)], axis=1)
    d_out, d_query, d_key, d_value = (up[PROJ + j * D : PROJ + (j + 1) * D] for j in range(4))
    return (
        y, dx, d_query, small[0], d_key, d_value, small[1], d_out, small[2], small[3], small[4],
        d_inner, small[8:12].reshape(-1), up[:FF], small[5], small[6], small[7],
    )


def solution(mesh):
    sizes = (mesh.shape["dp"], mesh.shape["seq"])
    tokens = P("dp", "seq", None)
    return jax.shard_map(
        functools.partial(on_device, *sizes),
        mesh=mesh,
        in_specs=(tokens, P("dp", "seq")) + (P(),) * 15 + (tokens,),
        out_specs=(tokens, tokens) + (P(),) * 15,
        check_vma=False,
    )
```

time: 295 us -> 226 us (0.77)
  matrix products: 52.7 us -> 0 us
  other arithmetic: 27.2 us -> 4.12 us
  local copies, waits for them, and re-layouts: 12.8 us -> 33.5 us
  Pallas kernels: 200 us -> 187 us
    dot_general x23 -> x0, matrix products: 47.7 us -> none  [the longest x6 15.3 us: product_tn(): lax.dot_general(left, right, (((0,), (0,)), ((), ())), preferred_element_...]
    convert_element_type x7 -> x0, other arithmetic: 22.9 us -> none  [the longest x6 18.3 us: on_device(): up = lambda a: a.astype(F32)]
    pallas_call x2 -> x1, Pallas kernels: 200 us -> 187 us  [whole_layer(): pl.pallas_call(functools.partial(layer_kernel, plan, seq_size), out_shape...]
    slice x1 -> x2, local copies, waits for them, and re-layouts: 0.79 us -> 11.9 us  [the longest x1 8.01 us: on_device(): up[:FF]]
    reshape x1 -> x8, local copies, waits for them, and re-layouts: 0.01 us -> 10.1 us  [whole_layer(): vector = lambda v: v.reshape(1, -1)]
    unnamed x128 -> x10, local copies, waits for them, and re-layouts: 2.75 us -> 8.38 us
    convert_element_type x5 -> x0, local copies, waits for them, and re-layouts: 5.04 us -> none  [the longest x1 1.92 us: local_layer(): lax.dynamic_slice_in_dim(both, (1 - side) * tokens, tokens, 0).astype(BF16)]
    sub x1 -> x0, matrix products: 4.97 us -> none  [local_layer(): powers = jnp.exp(scores - row_max)]
where the time goes in v2:
time: 226 us; the launch traced here: 225 us
  Pallas kernels  187 us (83%)
  local copies, waits for them, and re-layouts  33.5 us (15%)
  other arithmetic  4.12 us (2%)
    pallas_call x1, Pallas kernels, whole_layer(): pl.pallas_call(functools.partial(layer_kernel, plan, seq_size), out_shape...  187 us
    reshape x8, local copies, waits for them, and re-layouts, whole_layer(): vector = lambda v: v.reshape(1, -1)  10.1 us
    unnamed x10, local copies, waits for them, and re-layouts  8.38 us
    slice x1, local copies, waits for them, and re-layouts, on_device(): up[:FF]  8.01 us

profile of v2, /device:TPU:0, one launch (start us, length us, event | category | flops | bytes accessed | tf_op | source)
XLA Modules:
  0.0 225.4 jit_solution(4975019968089203744)
XLA Ops:
  0.7 1.3 reshape.68.bq
  1.9 1.3 reshape.69.bv
  3.2 1.3 reshape.70.bo
  4.5 1.3 reshape.71.g1
  5.7 1.3 reshape.72.s1
  7.0 1.3 reshape.74.b2
  8.3 1.3 reshape.75.g2
  9.5 1.3 reshape.76.s2
  10.8 187.1 %layer.1 = (bf16[9216,768]{1,0:T(8,128)(2,1)S(1)}, f32[16,768]{1,0:T(8,128)}, bf16[2,128,768]{2,1,0:T(8,128)(2,1)}, bf16[2,128,768]{2,1,0:T(8,128)(2,1)}) custom-call(bf16[2,128,768]{2,1,0:T(8,128)(2,1)} %x_ref.1, bf16[2,128,768]{2,1,0:T(8,128)(2,1)} %cot_ref.1, s32[2,1,128]{2,1,0:T(1,128)} %bitcast.3, bf16[768,768]{1,0:T(8,128)(2,1)} %wq_hbm.1, ...), custom_call_target="tpu_custom_call" | custom-call | tf_op jit(solution)/shard_map/layer/pallas_call | solution.py:805
  197.9 0.0 copy-start
  197.9 5.0 %copy-done = bf16[9216,768]{1,0:T(8,128)(2,1)} copy-done((bf16[9216,768]{1,0:T(8,128)(2,1)}, bf16[9216,768]{1,0:T(8,128)(2,1)S(1)}, u32[]{:S(2)}) %copy-start) | copy-done | bytes 14155800
  203.0 0.7 slice.67
  203.7 1.7 slice_reduce_fusion
  205.4 0.6 reshape.77
  206.0 0.0 copy-start.1
  206.0 8.0 %slice.80 = f32[3072,768]{1,0:T(8,128)} slice(bf16[9216,768]{1,0:T(8,128)(2,1)} %copy-done), slice={[0:3072], [0:768]} | slice | bytes 18874368 | tf_op jit(solution)/shard_map/slice | solution.py:857
  214.1 1.8 copy-done.1
  215.9 3.9 %fusion = (f32[768,768]{1,0:T(8,128)S(1)}, f32[768,768]{1,0:T(8,128)S(1)}, f32[768,768]{1,0:T(8,128)S(1)}, f32[768,768]{1,0:T(8,128)S(1)}, f32[768,768]{1,0:T(8,...) fusion(bf16[9216,768]{1,0:T(8,128)(2,1)S(1)} %copy-done.1), kind=kLoop, calls=%fused_computation.9 | loop fusion | bytes 37748736 | tf_op jit(solution)/shard_map/slice | solution.py:853
  219.8 0.0 copy-start.3
  219.8 0.0 copy-start.2
  219.8 4.1 %pad_maximum_fusion = f32[768,3072]{1,0:T(8,128)} fusion(f32[768,768]{1,0:T(8,128)S(1)} %get-tuple-element.36, f32[768,768]{1,0:T(8,128)S(1)} %get-tuple-element.35, f32[768,768]{1,0:T(8,128)S(1)} %get-tuple-element.34, f32[768,768]{1,0:T(8,128)S(1)} %get-tuple-element.33), kind=kLoop, calls=%fused_computation | loop fusion | flops 7077888 | bytes 18874368 | tf_op jit(solution)/shard_map/concatenate | solution.py:853
  223.9 0.0 copy-done.3
  223.9 0.7 copy.37
  224.7 0.0 copy-done.2
  224.7 0.7 copy.38
Async XLA Ops:
  197.9 5.1 %copy-start = (bf16[9216,768]{1,0:T(8,128)(2,1)}, bf16[9216,768]{1,0:T(8,128)(2,1)S(1)}, u32[]{:S(2)}) copy-start(bf16[9216,768]{1,0:T(8,128)(2,1)S(1)} %get-tuple-element.23) | copy-start | bytes 42467332
  206.0 9.8 %copy-start.1 = (bf16[9216,768]{1,0:T(8,128)(2,1)S(1)}, bf16[9216,768]{1,0:T(8,128)(2,1)}, u32[]{:S(2)}) copy-start(bf16[9216,768]{1,0:T(8,128)(2,1)} %copy-done) | copy-start | bytes 42467332
  219.8 4.1 %copy-start.3 = (bf16[2,128,768]{2,1,0:T(8,128)(2,1)S(1)}, bf16[2,128,768]{2,1,0:T(8,128)(2,1)}, u32[]{:S(2)}) copy-start(bf16[2,128,768]{2,1,0:T(8,128)(2,1)} %get-tuple-element.58) | copy-start | bytes 1179652
  219.8 4.9 %copy-start.2 = (bf16[2,128,768]{2,1,0:T(8,128)(2,1)S(1)}, bf16[2,128,768]{2,1,0:T(8,128)(2,1)}, u32[]{:S(2)}) copy-start(bf16[2,128,768]{2,1,0:T(8,128)(2,1)} %get-tuple-element.59) | copy-start | bytes 1179652

commit v3 on v2

--- a/solution.py
+++ b/solution.py
@@ -37,7 +37,7 @@
 
 GROUP = 1536
 PIECE = 512
-ORDERS = (("x", "y", "z"), ("y", "z", "x"), ("z", "x", "y"))
+ORDERS = (("xyz", "yxz", "zxy"), ("xyz", "yxz", "zyx"))
 SUBS = 1
 
 
@@ -54,7 +54,7 @@
         self.pieces = []
         for g in range(groups):
             for cls in range(3):
-                self.pieces.append(self.plan(g * GROUP + cls * PIECE, ORDERS[cls]))
+                self.pieces.append(self.plan(g * GROUP + cls * PIECE, ORDERS[g % len(ORDERS)][cls]))
 
     def sem(self):
         self.sems += 1
@@ -66,7 +66,7 @@
 
     def plan(self, base, order):
         stages, rows, ends = [], PIECE, False
-        for axis in ("c",) + order:
+        for axis in "c" + order:
             half = rows // 2
             st = dict(axis=axis, rows=half, ends=ends)
             if axis == "z":
@@ -315,20 +315,28 @@
 FF = 3072
 OUTER, INNER, PROJ = 0, 3072, 6144
 ORDER = (
-    -1, -2, -3, 0, 1, 2, 3, 4, -4, 5, -5, 0, 6, 1, 2, 7, 8, -6, 3, 4, 5, -7, 9, 0,
-    1, 10, 2, 6, 11, -8, 7, 8, 5, -9, 3, 4, 9, 1, 0, 2, 10, 8, -10, 11, 5, 2, 6, 4,
-    7, 0, 1, 9, 3, 2, -11, 10, 5, 6, 8, 1, 9, 2, 4, 11, 0, -12, 7, 5, -13, 3, 8, 0,
-    12, 1, 13, 5, 10, 14, 11, 6, 15, 2, 9, 16, 8, 4, 7, 0, 17, 3, 1, -14, -15, 10, 12, 13,
-    6, 1, 9, 14, 5, 0, 11, 16, 1, -16, 8, 2, 14, 12, 15, 4, 0, 17, 7, 11, 3, 2, -17, 10,
-    14, 13, 8, 6, 1, 9, 17, 1, 3, 15, 2, -18, 0, 11, 13, 2, 7, 5, 0, 6, 10, 9, 17, 16,
-    -19, 14, 3, 12, 11, 13, 14, 4, 5, 6, 17, 9, 3, -20, 16, 13, 14, 12, 8, 6, 15, 4, 5, 17,
-    7, 3, 5, 16, 9, 13, 12, 17, 3, 10, 8, 14, 15, 4, 7, 11, 6, 10, 8, 13, 16, 15, 6, 4,
-    12, 8, 7, 4, 11, 9, 10, 14, 13, 9, 15, 17, 12, 16, 7, 11, 7, 14, 11, 13, 15, 17, 12, 10,
-    16, 10, 14, 13, 15, 17, 14, 12, 13, 16, 15, 17, 12, 17, 16, 12, 15, 15, 16, 16,
+    -1, -2, 0, -3, 1, 2, 3, 4, -4, 5, 0, -5, 6, 7, 1, 8, 2, -6, 3, -7, 4, 5, -8, 9,
+    10, 6, 0, 11, 2, -9, 8, 7, 1, 4, 0, -10, 3, 5, 2, -11, 9, 10, 11, 7, 8, 1, 3, 4,
+    0, -12, 6, 2, -13, 12, 9, 13, 10, 5, 6, 14, 7, 11, 2, 15, -14, -15, 16, 17, 8, 9, 10, 1,
+    -16, 3, 12, 4, 6, 13, 7, -17, 0, 11, 14, 5, 2, 15, -18, 8, 16, 13, 1, 5, 12, -19, 9, 3,
+    10, 4, 2, 11, -20, 6, 17, 7, 16, 0, 15, 9, 5, 13, 8, 14, 10, 11, 1, 12, 3, 5, 4, 11,
+    17, 8, 0, 13, 14, 1, 2, 11, 12, 8, 6, 3, 7, 4, 17, 14, 16, 0, 15, 13, 9, 1, 10, 2,
+    12, 17, 6, 3, 14, 7, 4, 16, 1, 0, 5, 15, 17, 9, 3, 10, 2, 14, 4, 6, 11, 2, 7, 16,
+    5, 15, 0, 1, 9, 17, 8, 10, 0, 13, 1, 12, 11, 4, 16, 3, 15, 5, 6, 4, 3, 14, 8, 5,
+    9, 13, 7, 12, 11, 17, 16, 10, 15, 11, 14, 8, 13, 6, 7, 8, 12, 16, 6, 17, 7, 15, 9, 10,
+    14, 9, 12, 13, 10, 16, 15, 17, 14, 12, 13, 14, 12, 17, 13, 15, 16, 17, 15, 16,
 )
 
 
 SMALL_PARTS = 5
+
+
+class Row:
+    def __init__(self, ref):
+        self.ref = ref
+
+    def __getitem__(self, at):
+        return (self.ref[...] if at is Ellipsis else self.ref[at[1]]).reshape(1, -1)
 
 
 def fold(values):
@@ -345,6 +353,7 @@
     ss, rs, gs_, gr, gl, ws, ms, mr, ys, yr, xs,
 ):
     plan.bind(total, landing, final, ss, rs)
+    bq, bv, bo, g1, s1, bi, b2, g2, s2 = (Row(v) for v in (bq, bv, bo, g1, s1, bi, b2, g2, s2))
     dp, sq, side, pair = place(seq_size)
     sibling = (dp + 1 - 2 * side, sq)
     rows, length = x_ref.shape[0], x_ref.shape[1]
@@ -352,6 +361,17 @@
     tokens = spread * length
     own, far = side * tokens, (1 - side) * tokens
 
+    barrier = pltpu.get_barrier_semaphore()
+    column = [(pair + c, p) for p in range(seq_size) for c in range(2)]
+    for to in column:
+        pl.when(jnp.logical_not(jnp.logical_and(to[0] == dp, to[1] == sq)))(
+            lambda to=to: pl.semaphore_signal(barrier, inc=1, device_id=to, device_id_type=MESH)
+        )
+    across = [bit for axis, bit in small_bits(plan.dp_size, seq_size) if axis == "dp" and bit > 1]
+    for bit in across:
+        to = (dp + bit * (1 - 2 * ((dp // bit) % 2)), sq)
+        pl.semaphore_signal(barrier, inc=1, device_id=to, device_id_type=MESH)
+
     loads = {}
 
     def load(name, src, dst, i):
@@ -367,6 +387,8 @@
     def loaded(name):
         for c in loads[name]:
             c.wait()
+
+    pl.semaphore_wait(barrier, len(column) - 1 + len(across))
 
     half, spot = sq // spread, sq % spread
 
@@ -799,14 +821,13 @@
     tokens = seq_size * length // 2
     vmem, anyw = pl.BlockSpec(memory_space=pltpu.VMEM), pl.BlockSpec(memory_space=pl.ANY)
     nbits = len(small_bits(dp_size, seq_size))
-    back = jax.ShapeDtypeStruct((rows, length, width), BF16)
-    vector = lambda v: v.reshape(1, -1)
+    back = pltpu.VMEM((rows, length, width), BF16)
     dma = pltpu.SemaphoreType.DMA
     return pl.pallas_call(
         functools.partial(layer_kernel, plan, seq_size),
-        out_shape=(pltpu.VMEM((3 * FF, D), BF16), jax.ShapeDtypeStruct((16, D), F32), back, back),
+        out_shape=(pltpu.VMEM((3 * FF, D), BF16), pltpu.VMEM((16, D), F32), back, back),
         in_specs=[anyw] * 9 + [vmem] * 9,
-        out_specs=(vmem, vmem, anyw, anyw),
+        out_specs=(vmem,) * 4,
         scratch_shapes=[
             pltpu.VMEM((3 * FF, D), BF16),
             pltpu.VMEM((plan.slots, D), BF16),
@@ -835,27 +856,79 @@
             dma((5, 2)), dma((4, seq_size)), dma((3,)), dma((9,)),
             dma((nbits,)), dma((nbits,)), dma((2, 2)), dma((2, 2)), dma((4,)),
         ],
-        compiler_params=pltpu.CompilerParams(has_side_effects=True, vmem_limit_bytes=VMEM_LIMIT),
+        compiler_params=pltpu.CompilerParams(collective_id=1, has_side_effects=True, vmem_limit_bytes=VMEM_LIMIT),
         name="layer",
     )(
         layer_input, cotangent, segment_ids.reshape(rows, 1, length), w_query, w_key, w_value, w_out, w_inner, w_outer,
-        vector(b_query), vector(b_value), vector(b_out), vector(gain_one), vector(shift_one), vector(b_inner),
-        vector(b_outer), vector(gain_two), vector(shift_two),
+        b_query, b_value, b_out, gain_one, shift_one, b_inner, b_outer, gain_two, shift_two,
     )
 
 
-VMEM_LIMIT = 48 << 20
+VMEM_LIMIT = 46 << 20
+
+
+def widen_kernel(sums, small, y_in, dx_in, *refs):
+    outs, (wide, sem, far) = refs[:17], refs[17:]
+    (y, dx, d_query, d_b_query, d_key, d_value, d_b_value, d_out, d_b_out, d_gain_one, d_shift_one, d_inner,
+     d_b_inner, d_outer, d_b_outer, d_gain_two, d_shift_two) = outs
+    rows = [pltpu.make_async_copy(y_in, y, far.at[0]), pltpu.make_async_copy(dx_in, dx, far.at[1])]
+    for c in rows:
+        c.start()
+    for i, o in enumerate((d_b_query, d_b_value, d_b_out, d_gain_one, d_shift_one, d_b_outer, d_gain_two, d_shift_two)):
+        o[...] = small[i]
+    for j in range(4):
+        d_b_inner[j * D : (j + 1) * D] = small[8 + j]
+    step = 384
+    copies = []
+    for n in range(3 * FF // step):
+        at = n * step
+        if at < INNER:
+            view = d_outer.at[pl.ds(at, step)]
+        elif at < PROJ:
+            j, row = (at - INNER) // D, (at - INNER) % D
+            view = d_inner.at[pl.ds(row, step), pl.ds(j * D, D)]
+        else:
+            j, row = (at - PROJ) // D, (at - PROJ) % D
+            view = (d_out, d_query, d_key, d_value)[j].at[pl.ds(row, step)]
+        slot = n % 4
+        if n >= 4:
+            copies[n - 4].wait()
+
+        def body(i, _, at=at, slot=slot):
+            wide[slot, pl.ds(pl.multiple_of(i * 32, 32), 32)] = sums[pl.ds(pl.multiple_of(at + i * 32, 32), 32)].astype(F32)
+            return 0
+
+        lax.fori_loop(0, step // 32, body, 0)
+        copies.append(pltpu.make_async_copy(wide.at[slot], view, sem.at[slot]))
+        copies[-1].start()
+    for c in copies[-4:] + rows:
+        c.wait()
+
+
+def widen(sums, small, y, dx):
+    vmem, anyw = pl.BlockSpec(memory_space=pltpu.VMEM), pl.BlockSpec(memory_space=pl.ANY)
+    back = jax.ShapeDtypeStruct(y.shape, BF16)
+    square, vector = jax.ShapeDtypeStruct((D, D), F32), jax.ShapeDtypeStruct((D,), F32)
+    shapes = (
+        back, back, square, vector, square, square, vector, square, vector, vector, vector,
+        jax.ShapeDtypeStruct((D, FF), F32), jax.ShapeDtypeStruct((FF,), F32), jax.ShapeDtypeStruct((FF, D), F32),
+        vector, vector, vector,
+    )
+    return pl.pallas_call(
+        widen_kernel,
+        out_shape=shapes,
+        in_specs=[vmem] * 4,
+        out_specs=tuple(vmem if len(o.shape) == 1 else anyw for o in shapes),
+        scratch_shapes=[
+            pltpu.VMEM((4, 384, D), F32), pltpu.SemaphoreType.DMA((4,)), pltpu.SemaphoreType.DMA((2,)),
+        ],
+        compiler_params=pltpu.CompilerParams(vmem_limit_bytes=16 << 20),
+        name="widen",
+    )(sums, small, y, dx)
 
 
 def on_device(dp_size, seq_size, *args):
-    sums, small, y, dx = whole_layer(args, dp_size, seq_size)
-    up = sums.astype(F32)
-    d_inner = jnp.concatenate([up[INNER + j * D : INNER + (j + 1) * D] for j in range(4)], axis=1)
-    d_out, d_query, d_key, d_value = (up[PROJ + j * D : PROJ + (j + 1) * D] for j in range(4))
-    return (
-        y, dx, d_query, small[0], d_key, d_value, small[1], d_out, small[2], small[3], small[4],
-        d_inner, small[8:12].reshape(-1), up[:FF], small[5], small[6], small[7],
-    )
+    return widen(*whole_layer(args, dp_size, seq_size))
 
 
 def solution(mesh):

time: 226 us -> 174 us (0.77)
  local copies, waits for them, and re-layouts: 33.5 us -> 0 us
  Pallas kernels: 187 us -> 172 us
  other arithmetic: 4.12 us -> 0 us
    pallas_call x1, Pallas kernels: 187 us -> 162 us  [whole_layer(): pl.pallas_call(functools.partial(layer_kernel, plan, seq_size), out_shape...]
    slice x4 -> x0, local copies, waits for them, and re-layouts: 14.4 us -> none  [the longest x1 8.01 us: on_device(): up[:FF]]
    reshape x9 -> x0, local copies, waits for them, and re-layouts: 10.7 us -> none  [the longest x8 10.1 us: whole_layer(): vector = lambda v: v.reshape(1, -1)]
    pallas_call x0 -> x1, Pallas kernels: none -> 10.2 us  [widen(): pl.pallas_call(widen_kernel, out_shape=shapes, in_specs=[vmem] * 4, out_s...]
    unnamed x10 -> x0, local copies, waits for them, and re-layouts: 8.38 us -> none
    concatenate x1 -> x0, other arithmetic: 4.12 us -> none  [on_device(): jnp.concatenate([up[INNER + j * D:INNER + (j + 1) * D] for j in range(4)]...]
where the time goes in v3:
time: 174 us; the launch traced here: 173 us
  Pallas kernels  172 us (99%)
    pallas_call x1, Pallas kernels, whole_layer(): pl.pallas_call(functools.partial(layer_kernel, plan, seq_size), out_shape...  162 us
    pallas_call x1, Pallas kernels, widen(): pl.pallas_call(widen_kernel, out_shape=shapes, in_specs=[vmem] * 4, out_s...  10.2 us

profile of v3, /device:TPU:0, one launch (start us, length us, event | category | flops | bytes accessed | tf_op | source)
XLA Modules:
  0.0 173.1 jit_solution(12827431062574113625)
XLA Ops:
  0.7 162.0 %layer.1 = (bf16[9216,768]{1,0:T(8,128)(2,1)S(1)}, f32[16,768]{1,0:T(8,128)S(1)}, bf16[2,128,768]{2,1,0:T(8,128)(2,1)S(1)}, bf16[2,128,768]{2,1,0:T(8,128)(2,1)S(1)}) custom-call(bf16[2,128,768]{2,1,0:T(8,128)(2,1)} %x_ref.1, bf16[2,128,768]{2,1,0:T(8,128)(2,1)} %cot_ref.1, s32[2,1,128]{2,1,0:T(1,128)} %bitcast.1, bf16[768,768]{1,0:T(8,128)(2,1)} %wq_hbm.1, ...), custom_call_target="tpu_custom_call" | custom-call | tf_op jit(solution)/shard_map/layer/pallas_call | solution.py:826
  162.7 10.2 %widen.1 = (bf16[2,128,768]{2,1,0:T(8,128)(2,1)}, bf16[2,128,768]{2,1,0:T(8,128)(2,1)}, f32[768,768]{1,0:T(8,128)}, f32[768]{0:T(1024)}, f32[768,768]{1,0:T(8,12...) custom-call(bf16[9216,768]{1,0:T(8,128)(2,1)S(1)} %get-tuple-element, ...), custom_call_target="tpu_custom_call" | custom-call | tf_op jit(solution)/shard_map/widen/pallas_call | solution.py:917

commit v4 on v3

--- a/solution.py
+++ b/solution.py
@@ -37,8 +37,9 @@
 
 GROUP = 1536
 PIECE = 512
-ORDERS = (("xyz", "yxz", "zxy"), ("xyz", "yxz", "zyx"))
+ORDERS = (("xyz", "yxz", "zxy"), ("xyz", "yxz", "zyx"), ("xyz", "yxz", "zxy"), ("xyz", "yxz", "zyx"), ("xyz", "yxz", "yzx"), ("xyz", "yxz", "xzy"))
 SUBS = 1
+LANES = "cxyz"
 
 
 class Exchange:
@@ -90,7 +91,7 @@
         self.last = self.seq_size - 1
         self.edge = jnp.logical_or(sq == 0, sq == self.last)
         self.side = sq // self.last
-        self.sent = []
+        self.rows_sent = {}
         for p in self.pieces:
             off = p["base"]
             for st in p["stages"]:
@@ -109,12 +110,16 @@
         bit, value = self.bits[axis]
         return (self.dp + bit * (1 - 2 * value), self.sq)
 
-    def copy(self, src, dst, sem, tgt):
-        return pltpu.make_async_remote_copy(src, dst, self.ss.at[sem], self.rs.at[sem], tgt, MESH)
-
-    def send(self, make, when):
-        self.sent.append((make, when))
-        make().start()
+    def copy(self, src, dst, lane, sem, tgt):
+        return pltpu.make_async_remote_copy(src, dst, self.ss.at[lane], self.rs.at[sem], tgt, MESH)
+
+    def send(self, copy, lane, rows, who):
+        copy.start()
+        for place_ in who:
+            self.rows_sent[lane, place_] = self.rows_sent.get((lane, place_), 0) + rows
+
+    def everyone(self, st):
+        return (0, self.last) if st["ends"] else range(self.seq_size)
 
     def gated(self, when, f):
         if when is None:
@@ -151,29 +156,27 @@
             for way, at, to, base in (("down", self.last, -1, 0), ("up", 0, 1, st["rows"])):
                 when = self.sq == at
 
-                def f(way=way, to=to, base=base, when=when):
+                def f(way=way, at=at, to=to, base=base):
                     for s in st[way]:
-                        self.send(lambda s=s: self.rs_copy(st, s, base, to), when)
+                        self.send(self.rs_copy(st, s, base, to), LANES.index("z"), s["rows"], (at,))
                 self.gated(when, f)
         else:
             when = self.edge if st["ends"] else None
 
             def f():
-                self.send(
-                    lambda: self.copy(
-                        self.view(st["give"], st["rows"]), self.landed(st), st["rs"], self.partner(st["axis"]),
-                    ),
-                    when,
-                )
+                self.send(self.rs_pair(st), LANES.index(st["axis"]), st["rows"], self.everyone(st))
             self.gated(when, f)
+
+    def rs_pair(self, st):
+        return self.copy(
+            self.view(st["give"], st["rows"]), self.landed(st), LANES.index(st["axis"]), st["rs"], self.partner(st["axis"])
+        )
 
     def rs_hyper(self, p, i):
         st = p["stages"][i]
 
         def f():
-            self.copy(
-                self.view(st["give"], st["rows"]), self.landed(st), st["rs"], self.partner(st["axis"]),
-            ).wait_recv()
+            self.rs_pair(st).wait_recv()
             self.add(st["keep"], st["slot"], st["rows"], self.final if i + 1 == len(p["stages"]) else None)
         self.gated(self.edge if st["ends"] else None, f)
 
@@ -182,19 +185,19 @@
         for way, at, to, base in (("down", self.last - hop, -1, 0), ("up", hop, 1, st["rows"])):
             when = self.sq == at
 
-            def f(way=way, to=to, base=base, when=when):
+            def f(way=way, at=at, to=to, base=base):
                 for s in st[way]:
                     self.rs_copy(st, s, base, -to).wait_recv()
                     ended = hop == self.last and i + 1 == len(p["stages"])
                     self.add(st["off"] + base + s["at"], s["slot"], s["rows"], self.final if ended else None)
                     if hop < self.last:
-                        self.send(lambda s=s: self.rs_copy(st, s, base, to), when)
+                        self.send(self.rs_copy(st, s, base, to), LANES.index("z"), s["rows"], (at,))
             self.gated(when, f)
 
     def rs_copy(self, st, s, base, to):
         return self.copy(
             self.view(st["off"] + base + s["at"], s["rows"]), self.landing.at[pl.ds(s["slot"], s["rows"])],
-            s["rs"], (self.dp, self.sq + to),
+            LANES.index("z"), s["rs"], (self.dp, self.sq + to),
         )
 
     def more(self, p):
@@ -205,7 +208,7 @@
 
             def f():
                 c = self.copy(
-                    self.done(p["own"], p["rows"]), self.landing.at[pl.ds(m["slot"], p["rows"])], m["rs"], tgt
+                    self.done(p["own"], p["rows"]), self.landing.at[pl.ds(m["slot"], p["rows"])], len(LANES) * 2, m["rs"], tgt
                 )
                 c.start()
                 c.wait()
@@ -220,33 +223,32 @@
             for way, at, to, base in (("down", self.last, -1, st["rows"]), ("up", 0, 1, 0)):
                 when = self.sq == at
 
-                def f(way=way, to=to, base=base, when=when):
+                def f(way=way, at=at, to=to, base=base):
                     for s in st[way]:
-                        self.send(lambda s=s: self.ag_copy(st, s, base, to), when)
+                        self.send(self.ag_copy(st, s, base, to), len(LANES) + LANES.index("z"), s["rows"], (at,))
                 self.gated(when, f)
         else:
             when = self.edge if st["ends"] else None
 
             def f():
                 self.send(
-                    lambda: self.copy(
-                        self.done(st["keep"], st["rows"]), self.done(st["keep"], st["rows"]),
-                        st["ag"], self.partner(st["axis"]),
-                    ),
-                    when,
+                    self.ag_pair(st, st["keep"]), len(LANES) + LANES.index(st["axis"]), st["rows"], self.everyone(st)
                 )
             self.gated(when, f)
 
     def ag_copy(self, st, s, base, to):
         part = self.done(st["off"] + base + s["at"], s["rows"])
-        return self.copy(part, part, s["ag"], (self.dp, self.sq + to))
+        return self.copy(part, part, len(LANES) + LANES.index("z"), s["ag"], (self.dp, self.sq + to))
+
+    def ag_pair(self, st, off):
+        part = self.done(off, st["rows"])
+        return self.copy(part, part, len(LANES) + LANES.index(st["axis"]), st["ag"], self.partner(st["axis"]))
 
     def ag_hyper(self, p, i):
         st = p["stages"][i]
 
         def f():
-            part = self.done(st["give"], st["rows"])
-            self.copy(part, part, st["ag"], self.partner(st["axis"])).wait_recv()
+            self.ag_pair(st, st["give"]).wait_recv()
         self.gated(self.edge if st["ends"] else None, f)
 
     def ag_hop(self, p, i, hop):
@@ -254,11 +256,11 @@
         for way, at, to, base in (("down", self.last - hop, -1, st["rows"]), ("up", hop, 1, 0)):
             when = self.sq == at
 
-            def f(way=way, to=to, base=base, when=when):
+            def f(way=way, at=at, to=to, base=base):
                 for s in st[way]:
                     self.ag_copy(st, s, base, -to).wait_recv()
                     if hop < self.last:
-                        self.send(lambda s=s: self.ag_copy(st, s, base, to), when)
+                        self.send(self.ag_copy(st, s, base, to), len(LANES) + LANES.index("z"), s["rows"], (at,))
             self.gated(when, f)
 
     def script(self, p):
@@ -295,8 +297,17 @@
         return steps
 
     def finish(self):
-        for make, when in self.sent:
-            self.gated(when, lambda make=make: make().wait_send())
+        for lane in range(2 * len(LANES)):
+            rows = [self.rows_sent[lane, p] for p in range(self.seq_size)]
+
+            def f(n, lane=lane):
+                self.copy(self.total.at[pl.ds(0, n)], self.total.at[pl.ds(0, n)], lane, 0, self.partner("c")).wait_send()
+
+            if min(rows) == max(rows):
+                f(rows[0])
+            else:
+                for p in range(self.seq_size):
+                    pl.when(self.sq == p)(functools.partial(f, rows[p]))
 
 
 def small_bits(dp_size, seq_size):
@@ -315,16 +326,16 @@
 FF = 3072
 OUTER, INNER, PROJ = 0, 3072, 6144
 ORDER = (
-    -1, -2, 0, -3, 1, 2, 3, 4, -4, 5, 0, -5, 6, 7, 1, 8, 2, -6, 3, -7, 4, 5, -8, 9,
-    10, 6, 0, 11, 2, -9, 8, 7, 1, 4, 0, -10, 3, 5, 2, -11, 9, 10, 11, 7, 8, 1, 3, 4,
-    0, -12, 6, 2, -13, 12, 9, 13, 10, 5, 6, 14, 7, 11, 2, 15, -14, -15, 16, 17, 8, 9, 10, 1,
-    -16, 3, 12, 4, 6, 13, 7, -17, 0, 11, 14, 5, 2, 15, -18, 8, 16, 13, 1, 5, 12, -19, 9, 3,
-    10, 4, 2, 11, -20, 6, 17, 7, 16, 0, 15, 9, 5, 13, 8, 14, 10, 11, 1, 12, 3, 5, 4, 11,
-    17, 8, 0, 13, 14, 1, 2, 11, 12, 8, 6, 3, 7, 4, 17, 14, 16, 0, 15, 13, 9, 1, 10, 2,
-    12, 17, 6, 3, 14, 7, 4, 16, 1, 0, 5, 15, 17, 9, 3, 10, 2, 14, 4, 6, 11, 2, 7, 16,
-    5, 15, 0, 1, 9, 17, 8, 10, 0, 13, 1, 12, 11, 4, 16, 3, 15, 5, 6, 4, 3, 14, 8, 5,
-    9, 13, 7, 12, 11, 17, 16, 10, 15, 11, 14, 8, 13, 6, 7, 8, 12, 16, 6, 17, 7, 15, 9, 10,
-    14, 9, 12, 13, 10, 16, 15, 17, 14, 12, 13, 14, 12, 17, 13, 15, 16, 17, 15, 16,
+    -1, -2, 0, -3, 1, 2, 3, 4, -4, 5, -5, 0, 6, 7, 1, 2, 8, -6, 3, -7, 4, 5, -8, 9,
+    10, 0, 6, -9, 1, 8, 2, 11, -10, 0, 5, 4, 1, 7, -11, 3, -12, 9, 8, 2, -13, 0, 13, 12,
+    1, 4, 14, 6, 10, 11, 15, 2, 5, 7, 16, 3, 9, -14, -15, 17, 6, 4, 7, 8, 9, 0, 12, 13,
+    1, 11, 10, 3, 14, -16, 2, 15, 0, 5, 4, 1, 10, 17, 6, 16, 14, 8, 11, 7, -17, 4, 3, 9,
+    12, 13, 0, 17, 6, 2, 5, 1, 7, 3, 10, -18, 15, 16, 12, 9, 0, 8, 13, 14, 1, 2, 6, 4,
+    10, 11, -19, 5, 7, 15, 17, 0, 16, 3, 14, 1, 8, 9, 12, 4, 11, -20, 13, 5, 6, 17, 7, 3,
+    2, 15, 12, 0, 10, 16, 13, 14, 1, 9, 6, 0, 17, 7, 8, 1, 15, 3, 5, 16, 4, 12, 2, 9,
+    11, 6, 13, 10, 14, 17, 7, 8, 5, 4, 15, 12, 2, 16, 13, 10, 4, 9, 3, 2, 14, 11, 3, 17,
+    8, 5, 6, 15, 12, 16, 13, 5, 10, 7, 6, 14, 11, 7, 12, 17, 8, 9, 15, 16, 8, 13, 9, 10,
+    14, 11, 10, 15, 17, 12, 12, 16, 13, 11, 13, 15, 11, 14, 15, 14, 17, 16, 17, 16,
 )
 
 
@@ -343,17 +354,14 @@
     return jnp.sum(values.reshape(values.shape[0] // 8, 8, values.shape[1]), axis=0)
 
 
-def layer_kernel(
-    plan, seq_size,
-    x_ref, cot_ref, seg_ref, wq_hbm, wk_hbm, wv_hbm, wo_hbm, win_hbm, wout_hbm,
-    bq, bv, bo, g1, s1, bi, b2, g2, s2,
-    final, small_out, y_out, dx_out,
-    total, landing, wproj, xf, qs, key, val, probs, attn, normed, inv1, hid, hid_t, active, slope, cot, ybuf, gout, acc,
-    mask, sg, dx_far, small,
-    ss, rs, gs_, gr, gl, ws, ms, mr, ys, yr, xs,
-):
+def layer_kernel(plan, seq_size, *refs):
+    x_ref, cot_ref, seg_ref, wq_hbm, wk_hbm, wv_hbm, wo_hbm, win_hbm, wout_hbm = refs[:9]
+    vectors_hbm, vectors = refs[9:18], refs[-9:]
+    final, small_out, y_out, dx_out = refs[18:22]
+    (total, landing, wproj, xf, qs, key, val, probs, attn, normed, inv1, hid, hid_t, active, slope, cot, ybuf, gout, acc,
+     mask, sg, dx_far, small, ss, rs, gs_, gr, gl, ws, ms, mr, ys, yr, xs) = refs[22:-9]
     plan.bind(total, landing, final, ss, rs)
-    bq, bv, bo, g1, s1, bi, b2, g2, s2 = (Row(v) for v in (bq, bv, bo, g1, s1, bi, b2, g2, s2))
+    bq, bv, bo, g1, s1, bi, b2, g2, s2 = (Row(v) for v in vectors)
     dp, sq, side, pair = place(seq_size)
     sibling = (dp + 1 - 2 * side, sq)
     rows, length = x_ref.shape[0], x_ref.shape[1]
@@ -380,6 +388,8 @@
 
     for i, (name, src) in enumerate((("q", wq_hbm), ("k", wk_hbm), ("v", wv_hbm), ("o", wo_hbm))):
         load(name, src, wproj.at[i], i)
+    for i, (src, dst) in enumerate(zip(vectors_hbm, vectors)):
+        load("vectors", src, dst, 9 + i)
     for j in range(4):
         load("in", win_hbm.at[:, pl.ds(j * D, D)], total.at[pl.ds(INNER + j * D, D)], 4 + j)
     load("out", wout_hbm, total.at[pl.ds(PROJ, FF)], 8)
@@ -424,13 +434,6 @@
     def s_local(r):
         return pltpu.make_async_copy(seg_ref.at[r], sg.at[sq], gl.at[2])
 
-    for r in range(rows):
-        at = half * spread + spot
-        split(
-            stays[r],
-            lambda r=r, at=at: x_local(r, at).start(),
-            lambda r=r, at=at: x_copy(r, spot, (pair + half, rows * side + r), at).start(),
-        )
     mine = [[jnp.logical_and(side == c, sq == rows * side + r) for c in range(2)] for r in range(rows)]
     for r in range(rows):
         for c in range(2):
@@ -440,10 +443,11 @@
                 lambda r=r, c=c: s_copy(r, c, sq, (pair + c, rows * side + r)).start(),
             )
     for r in range(rows):
+        at = half * spread + spot
         split(
             stays[r],
-            lambda r=r: c_local(r, spot).start(),
-            lambda r=r: c_copy(r, spot, (pair + half, rows * side + r)).start(),
+            lambda r=r, at=at: x_local(r, at).start(),
+            lambda r=r, at=at: x_copy(r, spot, (pair + half, rows * side + r), at).start(),
         )
 
     for b in range(spread):
@@ -453,6 +457,12 @@
             lambda b=b: x_copy(0, b, sibling, side * spread + b).wait_recv(),
         )
         forward(b, side * spread).start()
+    for r in range(rows):
+        split(
+            stays[r],
+            lambda r=r: c_local(r, spot).start(),
+            lambda r=r: c_copy(r, spot, (pair + half, rows * side + r)).start(),
+        )
 
     def token_block(which):
         return pl.ds(pl.multiple_of(which, tokens), tokens)
@@ -460,9 +470,8 @@
     def cols(i, n=256):
         return pl.ds(pl.multiple_of(i * n, 128), n)
 
-    loaded("q")
-    loaded("k")
-    loaded("v")
+    for name in ("vectors", "q", "k", "v"):
+        loaded(name)
 
     def project(which, also_query):
         def body(i, _):
@@ -487,12 +496,11 @@
     diagonal = lax.broadcasted_iota(jnp.int32, (length, length), 0) == lax.broadcasted_iota(
         jnp.int32, (length, length), 1
     )
-    for b in range(spread):
-        mine_seg = jnp.broadcast_to(sg[side * spread + b], (length, length))
-        column = jnp.sum(jnp.where(diagonal, mine_seg, 0), axis=1, keepdims=True)
-        for p in range(seq_size):
-            seen = jnp.broadcast_to(column, (length, length)) == jnp.broadcast_to(sg[p], (length, length))
-            mask[b * length : (b + 1) * length, p * length : (p + 1) * length] = jnp.where(seen, 0.0, MASKED)
+    for p in range(seq_size):
+        column = jnp.sum(jnp.where(diagonal, jnp.broadcast_to(sg[p], (length, length)), 0), axis=1, keepdims=True)
+        for b in range(spread):
+            seen = jnp.broadcast_to(column, (length, length)) == jnp.broadcast_to(sg[side * spread + b], (length, length))
+            mask[p * length : (p + 1) * length, b * length : (b + 1) * length] = jnp.where(seen, 0.0, MASKED)
 
     for b in range(spread):
         forward(b, (1 - side) * spread).wait_recv()
@@ -505,15 +513,16 @@
 
     def attend(i, _):
         c = cols(i, 128)
-        qp, kp, vp = qs[:, c], key[:, c], val[:, c]
+        qp, kp = qs[:, c], key[:, c]
+        vt = val[:, c].T
         outs = []
         for n in range(2):
-            s = product_nt(qp * picks[n], kp) + mask[...]
-            e = jnp.exp(s - jnp.max(s, axis=-1, keepdims=True))
-            p = (e * (1.0 / jnp.sum(e, axis=-1, keepdims=True))).astype(BF16)
+            s = product_nt(kp, qp * picks[n]) + mask[...]
+            e = jnp.exp(s - jnp.max(s, axis=0, keepdims=True))
+            p = (e * (1.0 / jnp.sum(e, axis=0, keepdims=True))).astype(BF16)
             probs[2 * i + n] = p
-            outs.append(product(p, vp))
-        attn[:, c] = jnp.where(low_lanes, outs[0], outs[1]).astype(BF16)
+            outs.append(product(vt[n * HD : (n + 1) * HD], p))
+        attn[:, c] = jnp.concatenate(outs, axis=0).T.astype(BF16)
         return 0
 
     lax.fori_loop(0, D // 128, attend, 0)
@@ -688,17 +697,17 @@
             i = n * 2 + m
             c = cols(i, 128)
             qp, kp, vp, gp = qs[:, c], key[:, c], val[:, c], cot[:, c]
+            kt = kp.T
             dq, dk, dv = [], [], []
             for h in range(2):
                 p = probs[2 * i + h]
                 pf = p.astype(F32)
-                weighted = pf * product_nt(gp * picks[h], vp)
-                delta = jnp.sum(weighted, axis=-1, keepdims=True)
-                gs = (weighted - pf * delta).astype(BF16)
-                dq.append(product(gs, kp))
-                dk.append(product_tn(gs, qp))
-                dv.append(product_tn(p, gp))
-            gq = (jnp.where(low_lanes, dq[0], dq[1]) * 0.125).astype(BF16)
+                weighted = pf * product_nt(vp, gp * picks[h])
+                gs = (weighted - pf * jnp.sum(weighted, axis=0, keepdims=True)).astype(BF16)
+                dq.append(product(kt[h * HD : (h + 1) * HD], gs))
+                dk.append(product(gs, qp))
+                dv.append(product(p, gp))
+            gq = (jnp.concatenate(dq, axis=0).T * 0.125).astype(BF16)
             gk = jnp.where(low_lanes, dk[0], dk[1]).astype(BF16)
             gv = jnp.where(low_lanes, dv[0], dv[1]).astype(BF16)
             qs[:, c] = gq
@@ -823,10 +832,11 @@
     nbits = len(small_bits(dp_size, seq_size))
     back = pltpu.VMEM((rows, length, width), BF16)
     dma = pltpu.SemaphoreType.DMA
+    vectors = (b_query, b_value, b_out, gain_one, shift_one, b_inner, b_outer, gain_two, shift_two)
     return pl.pallas_call(
         functools.partial(layer_kernel, plan, seq_size),
         out_shape=(pltpu.VMEM((3 * FF, D), BF16), pltpu.VMEM((16, D), F32), back, back),
-        in_specs=[anyw] * 9 + [vmem] * 9,
+        in_specs=[anyw] * 18,
         out_specs=(vmem,) * 4,
         scratch_shapes=[
             pltpu.VMEM((3 * FF, D), BF16),
@@ -836,7 +846,7 @@
             pltpu.VMEM((tokens, D), BF16),
             pltpu.VMEM((2 * tokens, D), BF16),
             pltpu.VMEM((2 * tokens, D), BF16),
-            pltpu.VMEM((D // HD, tokens, 2 * tokens), BF16),
+            pltpu.VMEM((D // HD, 2 * tokens, tokens), BF16),
             pltpu.VMEM((tokens, D), BF16),
             pltpu.VMEM((tokens, D), F32),
             pltpu.VMEM((tokens, 128), F32),
@@ -848,19 +858,20 @@
             pltpu.VMEM((tokens, D), BF16),
             pltpu.VMEM((tokens, D), BF16),
             pltpu.VMEM((tokens, D), F32),
-            pltpu.VMEM((tokens, 2 * tokens), F32),
+            pltpu.VMEM((2 * tokens, tokens), F32),
             pltpu.VMEM((seq_size, 1, length), jnp.int32),
             pltpu.VMEM((tokens, D), BF16),
             pltpu.VMEM((2 * nbits + 1, 16, D), F32),
-            dma((plan.sems,)), dma((plan.sems,)),
-            dma((5, 2)), dma((4, seq_size)), dma((3,)), dma((9,)),
+            dma((2 * len(LANES) + 1,)), dma((plan.sems,)),
+            dma((5, 2)), dma((4, seq_size)), dma((3,)), dma((18,)),
             dma((nbits,)), dma((nbits,)), dma((2, 2)), dma((2, 2)), dma((4,)),
-        ],
+        ]
+        + [pltpu.VMEM(v.shape, F32) for v in vectors],
         compiler_params=pltpu.CompilerParams(collective_id=1, has_side_effects=True, vmem_limit_bytes=VMEM_LIMIT),
         name="layer",
     )(
         layer_input, cotangent, segment_ids.reshape(rows, 1, length), w_query, w_key, w_value, w_out, w_inner, w_outer,
-        b_query, b_value, b_out, gain_one, shift_one, b_inner, b_outer, gain_two, shift_two,
+        *vectors,
     )
 
 

time: 174 us -> 169 us (0.971)
  Pallas kernels: 172 us -> 168 us
    pallas_call x1, Pallas kernels: 162 us -> 158 us  [whole_layer(): pl.pallas_call(functools.partial(layer_kernel, plan, seq_size), out_shape...]
where the time goes in v4:
time: 169 us
  Pallas kernels  168 us (99%)
    pallas_call x1, Pallas kernels, whole_layer(): pl.pallas_call(functools.partial(layer_kernel, plan, seq_size), out_shape...  158 us
    pallas_call x1, Pallas kernels, widen(): pl.pallas_call(widen_kernel, out_shape=shapes, in_specs=[vmem] * 4, out_s...  10.2 us

profile of v4, /device:TPU:0, one launch (start us, length us, event | category | flops | bytes accessed | tf_op | source)
XLA Modules:
  0.0 168.9 jit_solution(9752194529596882504)
XLA Ops:
  0.7 157.8 %layer.1 = (bf16[9216,768]{1,0:T(8,128)(2,1)S(1)}, f32[16,768]{1,0:T(8,128)S(1)}, bf16[2,128,768]{2,1,0:T(8,128)(2,1)S(1)}, bf16[2,128,768]{2,1,0:T(8,128)(2,1)S(1)}) custom-call(bf16[2,128,768]{2,1,0:T(8,128)(2,1)} %refs_0_.1, bf16[2,128,768]{2,1,0:T(8,128)(2,1)} %refs_1_.1, s32[2,1,128]{2,1,0:T(1,128)} %bitcast.1, bf16[768,768]{1,0:T(8,128)(2,1)} %refs_3_.1, ...), custom_call_target="tpu_custom_call" | custom-call | tf_op jit(solution)/shard_map/layer/pallas_call | solution.py:836
  158.5 10.2 %widen.1 = (bf16[2,128,768]{2,1,0:T(8,128)(2,1)}, bf16[2,128,768]{2,1,0:T(8,128)(2,1)}, f32[768,768]{1,0:T(8,128)}, f32[768]{0:T(1024)}, f32[768,768]{1,0:T(8,12...) custom-call(bf16[9216,768]{1,0:T(8,128)(2,1)S(1)} %get-tuple-element, ...), custom_call_target="tpu_custom_call" | custom-call | tf_op jit(solution)/shard_map/widen/pallas_call | solution.py:928

commit v5 on v4

--- a/solution.py
+++ b/solution.py
@@ -37,7 +37,7 @@
 
 GROUP = 1536
 PIECE = 512
-ORDERS = (("xyz", "yxz", "zxy"), ("xyz", "yxz", "zyx"), ("xyz", "yxz", "zxy"), ("xyz", "yxz", "zyx"), ("xyz", "yxz", "yzx"), ("xyz", "yxz", "xzy"))
+ORDERS = (("yxz", "xyz", "zyx"), ("zxy", "xyz", "yxz"), ("xyz", "yxz", "zxy"), ("zxy", "yxz", "yxz"), ("xyz", "xyz", "yzx"), ("xyz", "yxz", "yxz"))
 SUBS = 1
 LANES = "cxyz"
 
@@ -326,16 +326,16 @@
 FF = 3072
 OUTER, INNER, PROJ = 0, 3072, 6144
 ORDER = (
-    -1, -2, 0, -3, 1, 2, 3, 4, -4, 5, -5, 0, 6, 7, 1, 2, 8, -6, 3, -7, 4, 5, -8, 9,
-    10, 0, 6, -9, 1, 8, 2, 11, -10, 0, 5, 4, 1, 7, -11, 3, -12, 9, 8, 2, -13, 0, 13, 12,
-    1, 4, 14, 6, 10, 11, 15, 2, 5, 7, 16, 3, 9, -14, -15, 17, 6, 4, 7, 8, 9, 0, 12, 13,
-    1, 11, 10, 3, 14, -16, 2, 15, 0, 5, 4, 1, 10, 17, 6, 16, 14, 8, 11, 7, -17, 4, 3, 9,
-    12, 13, 0, 17, 6, 2, 5, 1, 7, 3, 10, -18, 15, 16, 12, 9, 0, 8, 13, 14, 1, 2, 6, 4,
-    10, 11, -19, 5, 7, 15, 17, 0, 16, 3, 14, 1, 8, 9, 12, 4, 11, -20, 13, 5, 6, 17, 7, 3,
-    2, 15, 12, 0, 10, 16, 13, 14, 1, 9, 6, 0, 17, 7, 8, 1, 15, 3, 5, 16, 4, 12, 2, 9,
-    11, 6, 13, 10, 14, 17, 7, 8, 5, 4, 15, 12, 2, 16, 13, 10, 4, 9, 3, 2, 14, 11, 3, 17,
-    8, 5, 6, 15, 12, 16, 13, 5, 10, 7, 6, 14, 11, 7, 12, 17, 8, 9, 15, 16, 8, 13, 9, 10,
-    14, 11, 10, 15, 17, 12, 12, 16, 13, 11, 13, 15, 11, 14, 15, 14, 17, 16, 17, 16,
+    -1, -2, -3, -4, 0, -5, 1, -6, 2, -7, 3, 5, 4, -8, 0, 6, 1, -9, 2, 7, 8, 5, -10, 0,
+    1, 3, 9, 4, -11, 10, -12, 11, 2, -13, 0, 6, 7, 12, 1, 5, 4, 8, 3, -14, 0, 2, 10, 1,
+    7, 9, -15, 5, 4, -16, 3, 0, 7, 11, 12, 8, -17, 6, 14, 0, 13, 2, 10, 1, 9, 3, -18, 15,
+    6, 11, 12, 5, 4, 7, 16, 10, 8, -19, -20, 0, 1, 17, 6, 11, 14, 10, 13, 12, 3, 9, 2, 5,
+    4, 7, 16, 15, 8, -21, 14, 17, 1, 5, 9, 4, 11, 13, 0, 2, 7, 12, 3, 6, 10, 16, 14, 15,
+    13, 1, 5, 8, 11, 6, 4, 17, -22, 12, 10, 7, 9, 16, 0, 13, 14, 15, 6, 2, 5, 11, 3, 10,
+    4, 17, 16, 1, -23, 15, 14, 8, 7, 12, 11, 9, 13, 5, 17, 6, 10, 12, 16, 2, 0, 15, 1, 11,
+    14, 0, 4, 1, 17, 12, 3, 8, -24, 13, 2, 7, 5, 16, 15, 5, 9, 6, 14, 3, 10, 12, 17, 13,
+    11, 16, 2, 15, 2, 7, 8, 14, 4, 7, 3, 17, 13, 4, 16, 3, 10, 9, 15, 6, 10, 8, 14, 6,
+    17, 11, 12, 11, 13, 9, 12, 16, 15, 8, 17, 8, 14, 9, 13, 14, 9, 13, 16, 15, 16, 15, 17, 17,
 )
 
 
@@ -483,7 +483,7 @@
             val[token_block(which), c] = (product(xb, wproj[2, :, c]) + bv[:, c]).astype(BF16)
             return 0
 
-        lax.fori_loop(0, D // 256, body, 0)
+        lax.fori_loop(0, D // 256, body, 0, unroll=3)
 
     project(own, True)
 
@@ -496,11 +496,12 @@
     diagonal = lax.broadcasted_iota(jnp.int32, (length, length), 0) == lax.broadcasted_iota(
         jnp.int32, (length, length), 1
     )
-    for p in range(seq_size):
-        column = jnp.sum(jnp.where(diagonal, jnp.broadcast_to(sg[p], (length, length)), 0), axis=1, keepdims=True)
-        for b in range(spread):
-            seen = jnp.broadcast_to(column, (length, length)) == jnp.broadcast_to(sg[side * spread + b], (length, length))
-            mask[p * length : (p + 1) * length, b * length : (b + 1) * length] = jnp.where(seen, 0.0, MASKED)
+    for b in range(spread):
+        mine_seg = jnp.broadcast_to(sg[side * spread + b], (length, length))
+        column = jnp.sum(jnp.where(diagonal, mine_seg, 0), axis=1, keepdims=True)
+        for p in range(seq_size):
+            seen = jnp.broadcast_to(column, (length, length)) == jnp.broadcast_to(sg[p], (length, length))
+            mask[b * length : (b + 1) * length, p * length : (p + 1) * length] = jnp.where(seen, 0.0, MASKED)
 
     for b in range(spread):
         forward(b, (1 - side) * spread).wait_recv()
@@ -513,19 +514,18 @@
 
     def attend(i, _):
         c = cols(i, 128)
-        qp, kp = qs[:, c], key[:, c]
-        vt = val[:, c].T
+        qp, kp, vp = qs[:, c], key[:, c], val[:, c]
         outs = []
         for n in range(2):
-            s = product_nt(kp, qp * picks[n]) + mask[...]
-            e = jnp.exp(s - jnp.max(s, axis=0, keepdims=True))
-            p = (e * (1.0 / jnp.sum(e, axis=0, keepdims=True))).astype(BF16)
+            s = product_nt(qp * picks[n], kp) + mask[...]
+            e = jnp.exp(s - jnp.max(s, axis=-1, keepdims=True))
+            p = (e * (1.0 / jnp.sum(e, axis=-1, keepdims=True))).astype(BF16)
             probs[2 * i + n] = p
-            outs.append(product(vt[n * HD : (n + 1) * HD], p))
-        attn[:, c] = jnp.concatenate(outs, axis=0).T.astype(BF16)
+            outs.append(product(p, vp))
+        attn[:, c] = jnp.where(low_lanes, outs[0], outs[1]).astype(BF16)
         return 0
 
-    lax.fori_loop(0, D // 128, attend, 0)
+    lax.fori_loop(0, D // 128, attend, 0, unroll=3)
 
     loaded("o")
 
@@ -534,7 +534,7 @@
         acc[:, c] = product(attn[...], wproj[3, :, c]) + bo[:, c] + xf[token_block(own), c].astype(F32)
         return 0
 
-    lax.fori_loop(0, D // 256, branch, 0)
+    lax.fori_loop(0, D // 256, branch, 0, unroll=3)
     step = 32
 
     def chunk(i):
@@ -551,7 +551,7 @@
         hid[r] = (n * g1[...] + s1[...]).astype(BF16)
         return 0
 
-    lax.fori_loop(0, tokens // step, norm_one, 0)
+    lax.fori_loop(0, tokens // step, norm_one, 0, unroll=2)
 
     loaded("in")
     loaded("out")
@@ -569,14 +569,14 @@
             slope[:, c] = cdf + v * DENSITY * jnp.exp(-0.5 * v * v)
             return 0
 
-        lax.fori_loop(0, 3, expand, 0)
+        lax.fori_loop(0, 3, expand, 0, unroll=3)
 
     def contract(i, _):
         c = cols(i)
         acc[:, c] = product(active[...], total[pl.ds(PROJ, FF), c]) + b2[:, c]
         return 0
 
-    lax.fori_loop(0, D // 256, contract, 0)
+    lax.fori_loop(0, D // 256, contract, 0, unroll=3)
     for b in range(spread):
         split(comes[b], lambda b=b: c_local(b, b).wait(), lambda b=b: c_copy(0, b, sibling).wait_recv())
 
@@ -601,7 +601,7 @@
         return d_gain + fold(g * n), d_shift + fold(g), d_bias + fold(grad_low.astype(F32))
 
     zero = jnp.zeros((8, D), F32)
-    sums = lax.fori_loop(0, tokens // step, norm_two, (zero, zero, zero))
+    sums = lax.fori_loop(0, tokens // step, norm_two, (zero, zero, zero), unroll=2)
     for at, v in zip((6, 7, 5), sums):
         small[0, at : at + 1] = jnp.sum(v, axis=0, keepdims=True)
 
@@ -639,15 +639,25 @@
     send_home(ybuf, y_out, 0)
 
 
+    bits = small_bits(plan.dp_size, seq_size)
+
+    def small_copy(i):
+        axis, bit = bits[i]
+        if axis == "dp":
+            tgt = (dp + bit * (1 - 2 * ((dp // bit) % 2)), sq)
+        else:
+            tgt = (dp, sq + bit * (1 - 2 * ((sq // bit) % 2)))
+        return pltpu.make_async_remote_copy(small.at[i], small.at[len(bits) + 1 + i], ms.at[i], mr.at[i], tgt, MESH)
+
     def outer_part(n):
         def body(i, _):
-            t = n * 6 + i
+            t = n * 2 + i
             total[pl.ds(pl.multiple_of(OUTER + t * 256, 256), 256)] = product(
                 active[:, cols(t)].T, gout[...]
             ).astype(BF16)
             return 0
 
-        lax.fori_loop(0, 6, body, 0)
+        lax.fori_loop(0, 2, body, 0, unroll=2)
 
     def inner_part(j):
         if j == 0:
@@ -664,7 +674,7 @@
             view[...] = product(hid_t[...], gi).astype(BF16)
             return 0
 
-        lax.fori_loop(0, 3, body, 0)
+        lax.fori_loop(0, 3, body, 0, unroll=3)
 
     def norm_one_part():
         def body(i, carry):
@@ -680,7 +690,7 @@
             acc[r] = grad
             return d_gain + fold(g * n), d_shift + fold(g), d_bias + fold(grad_low.astype(F32))
 
-        out = lax.fori_loop(0, tokens // step, body, (zero, zero, zero))
+        out = lax.fori_loop(0, tokens // step, body, (zero, zero, zero), unroll=2)
         for at, v in zip((3, 4, 2), out):
             small[0, at : at + 1] = jnp.sum(v, axis=0, keepdims=True)
 
@@ -690,24 +700,24 @@
             cot[:, cols(i)] = product_nt(gout[...], wproj[3, pl.ds(pl.multiple_of(i * 256, 256), 256)]).astype(BF16)
             return 0
 
-        lax.fori_loop(0, D // 256, body, 0)
+        lax.fori_loop(0, D // 256, body, 0, unroll=3)
 
     def attention_part(n):
         def body(m, _):
             i = n * 2 + m
             c = cols(i, 128)
             qp, kp, vp, gp = qs[:, c], key[:, c], val[:, c], cot[:, c]
-            kt = kp.T
             dq, dk, dv = [], [], []
             for h in range(2):
                 p = probs[2 * i + h]
                 pf = p.astype(F32)
-                weighted = pf * product_nt(vp, gp * picks[h])
-                gs = (weighted - pf * jnp.sum(weighted, axis=0, keepdims=True)).astype(BF16)
-                dq.append(product(kt[h * HD : (h + 1) * HD], gs))
-                dk.append(product(gs, qp))
-                dv.append(product(p, gp))
-            gq = (jnp.concatenate(dq, axis=0).T * 0.125).astype(BF16)
+                weighted = pf * product_nt(gp * picks[h], vp)
+                delta = jnp.sum(weighted, axis=-1, keepdims=True)
+                gs = (weighted - pf * delta).astype(BF16)
+                dq.append(product(gs, kp))
+                dk.append(product_tn(gs, qp))
+                dv.append(product_tn(p, gp))
+            gq = (jnp.where(low_lanes, dq[0], dq[1]) * 0.125).astype(BF16)
             gk = jnp.where(low_lanes, dk[0], dk[1]).astype(BF16)
             gv = jnp.where(low_lanes, dv[0], dv[1]).astype(BF16)
             qs[:, c] = gq
@@ -718,7 +728,9 @@
                 active[:, cols(12 + b * 6 + i, 128)] = gv[b * tokens : (b + 1) * tokens]
             return 0
 
-        lax.fori_loop(0, 2, body, 0)
+        lax.fori_loop(0, 2, body, 0, unroll=2)
+        if n == 2:
+            small_copy(0).start()
 
     def query_part():
         def body(i, _):
@@ -727,7 +739,7 @@
             ).astype(BF16)
             return 0
 
-        lax.fori_loop(0, D // 256, body, 0)
+        lax.fori_loop(0, D // 256, body, 0, unroll=3)
 
     def key_part():
         def body(i, _):
@@ -740,7 +752,7 @@
                 ).astype(BF16)
             return 0
 
-        lax.fori_loop(0, D // 256, body, 0)
+        lax.fori_loop(0, D // 256, body, 0, unroll=3)
 
     dx_send = pltpu.make_async_remote_copy(hid, dx_far, xs.at[0], xs.at[1], sibling, MESH)
 
@@ -756,18 +768,8 @@
             acc[:, cols(i)] += product_nt(qs[...], wproj[0, w]) + both(side, w)
             return 0
 
-        lax.fori_loop(0, D // 256, body, 0)
+        lax.fori_loop(0, D // 256, body, 0, unroll=3)
         dx_send.start()
-
-    bits = small_bits(plan.dp_size, seq_size)
-
-    def small_copy(i):
-        axis, bit = bits[i]
-        if axis == "dp":
-            tgt = (dp + bit * (1 - 2 * ((dp // bit) % 2)), sq)
-        else:
-            tgt = (dp, sq + bit * (1 - 2 * ((sq // bit) % 2)))
-        return pltpu.make_async_remote_copy(small.at[i], small.at[len(bits) + 1 + i], ms.at[i], mr.at[i], tgt, MESH)
 
     def input_end():
         dx_send.wait_recv()
@@ -779,7 +781,6 @@
 
         lax.fori_loop(0, tokens // step, body, 0)
         send_home(gout, dx_out, 1)
-        small_copy(0).start()
 
     def small_part(n):
         for i in range(n, n + 1 if n < SMALL_PARTS - 1 else len(bits)):
@@ -789,23 +790,23 @@
                 small_copy(i + 1).start()
 
     parts = (
-        [functools.partial(outer_part, n) for n in range(2)]
+        [functools.partial(outer_part, n) for n in range(6)]
         + [functools.partial(inner_part, j) for j in range(4)]
         + [norm_one_part, branch_part]
         + [functools.partial(attention_part, n) for n in range(3)]
         + [query_part, key_part, input_part, input_end]
         + [functools.partial(small_part, n) for n in range(SMALL_PARTS)]
     )
-    ready = {0: (0,), 1: (1,), 3: (2,), 5: (3,), 11: (4,), 12: (5,)}
+    ready = {n: (n,) for n in range(6)}
+    ready.update({6: (6,), 7: (7, 8), 8: (9,), 9: (10, 11), 11: (12,), 15: (13, 14), 16: (15, 16, 17)})
     scripts = [iter(plan.script(p)) for p in plan.pieces]
     for entry in ORDER:
         if entry >= 0:
             next(scripts[entry])[1]()
             continue
         parts[-entry - 1]()
-        for g in ready.get(-entry - 1, ()):
-            for p in plan.pieces[3 * g : 3 * g + 3]:
-                plan.rs_start(p, 0)
+        for n in ready.get(-entry - 1, ()):
+            plan.rs_start(plan.pieces[n], 0)
     small_out[...] = small[len(bits)]
     for i in range(len(bits)):
         small_copy(i).wait_send()
@@ -846,7 +847,7 @@
             pltpu.VMEM((tokens, D), BF16),
             pltpu.VMEM((2 * tokens, D), BF16),
             pltpu.VMEM((2 * tokens, D), BF16),
-            pltpu.VMEM((D // HD, 2 * tokens, tokens), BF16),
+            pltpu.VMEM((D // HD, tokens, 2 * tokens), BF16),
             pltpu.VMEM((tokens, D), BF16),
             pltpu.VMEM((tokens, D), F32),
             pltpu.VMEM((tokens, 128), F32),
@@ -858,7 +859,7 @@
             pltpu.VMEM((tokens, D), BF16),
             pltpu.VMEM((tokens, D), BF16),
             pltpu.VMEM((tokens, D), F32),
-            pltpu.VMEM((2 * tokens, tokens), F32),
+            pltpu.VMEM((tokens, 2 * tokens), F32),
             pltpu.VMEM((seq_size, 1, length), jnp.int32),
             pltpu.VMEM((tokens, D), BF16),
             pltpu.VMEM((2 * nbits + 1, 16, D), F32),

time: 169 us -> 158 us (0.935)
  Pallas kernels: 168 us -> 157 us
    pallas_call x1, Pallas kernels: 158 us -> 147 us  [whole_layer(): pl.pallas_call(functools.partial(layer_kernel, plan, seq_size), out_shape...]
where the time goes in v5:
time: 158 us
  Pallas kernels  157 us (99%)
    pallas_call x1, Pallas kernels, whole_layer(): pl.pallas_call(functools.partial(layer_kernel, plan, seq_size), out_shape...  147 us
    pallas_call x1, Pallas kernels, widen(): pl.pallas_call(widen_kernel, out_shape=shapes, in_specs=[vmem] * 4, out_s...  10.2 us

profile of v5, /device:TPU:0, one launch (start us, length us, event | category | flops | bytes accessed | tf_op | source)
XLA Modules:
  0.0 157.6 jit_solution(8766701597892492822)
XLA Ops:
  0.7 146.6 %layer.1 = (bf16[9216,768]{1,0:T(8,128)(2,1)S(1)}, f32[16,768]{1,0:T(8,128)S(1)}, bf16[2,128,768]{2,1,0:T(8,128)(2,1)S(1)}, bf16[2,128,768]{2,1,0:T(8,128)(2,1)S(1)}) custom-call(bf16[2,128,768]{2,1,0:T(8,128)(2,1)} %refs_0_.1, bf16[2,128,768]{2,1,0:T(8,128)(2,1)} %refs_1_.1, s32[2,1,128]{2,1,0:T(1,128)} %bitcast.1, bf16[768,768]{1,0:T(8,128)(2,1)} %refs_3_.1, ...), custom_call_target="tpu_custom_call" | custom-call | tf_op jit(solution)/shard_map/layer/pallas_call | solution.py:837
  147.3 10.2 %widen.1 = (bf16[2,128,768]{2,1,0:T(8,128)(2,1)}, bf16[2,128,768]{2,1,0:T(8,128)(2,1)}, f32[768,768]{1,0:T(8,128)}, f32[768]{0:T(1024)}, f32[768,768]{1,0:T(8,12...) custom-call(bf16[9216,768]{1,0:T(8,128)(2,1)S(1)} %get-tuple-element, ...), custom_call_target="tpu_custom_call" | custom-call | tf_op jit(solution)/shard_map/widen/pallas_call | solution.py:929

commit v6 on v5

--- a/solution.py
+++ b/solution.py
@@ -37,7 +37,7 @@
 
 GROUP = 1536
 PIECE = 512
-ORDERS = (("yxz", "xyz", "zyx"), ("zxy", "xyz", "yxz"), ("xyz", "yxz", "zxy"), ("zxy", "yxz", "yxz"), ("xyz", "xyz", "yzx"), ("xyz", "yxz", "yxz"))
+ORDERS = (("yxz", "yxz", "zxy"), ("zyx", "xyz", "xyz"), ("yxz", "xzy", "yxz"), ("zxy", "xyz", "xyz"), ("yzx", "xyz", "yxz"), ("yzx", "xyz", "yxz"))
 SUBS = 1
 LANES = "cxyz"
 
@@ -326,16 +326,16 @@
 FF = 3072
 OUTER, INNER, PROJ = 0, 3072, 6144
 ORDER = (
-    -1, -2, -3, -4, 0, -5, 1, -6, 2, -7, 3, 5, 4, -8, 0, 6, 1, -9, 2, 7, 8, 5, -10, 0,
-    1, 3, 9, 4, -11, 10, -12, 11, 2, -13, 0, 6, 7, 12, 1, 5, 4, 8, 3, -14, 0, 2, 10, 1,
-    7, 9, -15, 5, 4, -16, 3, 0, 7, 11, 12, 8, -17, 6, 14, 0, 13, 2, 10, 1, 9, 3, -18, 15,
-    6, 11, 12, 5, 4, 7, 16, 10, 8, -19, -20, 0, 1, 17, 6, 11, 14, 10, 13, 12, 3, 9, 2, 5,
-    4, 7, 16, 15, 8, -21, 14, 17, 1, 5, 9, 4, 11, 13, 0, 2, 7, 12, 3, 6, 10, 16, 14, 15,
-    13, 1, 5, 8, 11, 6, 4, 17, -22, 12, 10, 7, 9, 16, 0, 13, 14, 15, 6, 2, 5, 11, 3, 10,
-    4, 17, 16, 1, -23, 15, 14, 8, 7, 12, 11, 9, 13, 5, 17, 6, 10, 12, 16, 2, 0, 15, 1, 11,
-    14, 0, 4, 1, 17, 12, 3, 8, -24, 13, 2, 7, 5, 16, 15, 5, 9, 6, 14, 3, 10, 12, 17, 13,
-    11, 16, 2, 15, 2, 7, 8, 14, 4, 7, 3, 17, 13, 4, 16, 3, 10, 9, 15, 6, 10, 8, 14, 6,
-    17, 11, 12, 11, 13, 9, 12, 16, 15, 8, 17, 8, 14, 9, 13, 14, 9, 13, 16, 15, 16, 15, 17, 17,
+    -1, -2, -3, -4, 0, -5, -6, 1, -7, 3, 2, 4, -8, 6, 5, 0, -9, 7, 8, -10, 1, 3, 4, 9,
+    -11, -12, 10, 11, -13, 6, 5, 2, 0, 12, -14, 3, 9, 8, -15, 4, 7, 0, -16, 1, 5, 2, -17, 13,
+    4, 3, 14, -18, 7, 9, 15, 12, 16, 0, 1, 10, 17, 4, 5, -19, -20, 3, 2, 11, 7, 12, 1, 6,
+    5, 9, 14, 0, 8, 4, 15, 13, 6, 10, 0, 8, 4, 16, 12, 7, -21, 17, 15, 6, 1, 3, 10, 0,
+    5, 11, 8, 2, 4, 12, 13, 1, 6, 9, 5, 15, 0, 16, 11, 10, 8, 7, 13, 14, 1, 4, -22, 6,
+    5, 2, 17, 16, 11, 15, 3, 8, 9, 13, 10, 7, 14, 12, 6, 1, 16, -23, 17, 4, 0, 8, 5, 15,
+    10, 2, 14, 11, 12, 13, 3, 7, 6, 9, -24, 1, 17, 16, 10, 11, 8, 14, 12, 7, 17, 4, 0, 13,
+    11, 10, 15, 4, 5, 0, 2, 12, 7, 3, 13, 11, 6, 16, 1, 14, 9, 17, 12, 1, 10, 13, 8, 15,
+    11, 3, 16, 14, 5, 2, 17, 6, 5, 15, 6, 3, 7, 9, 16, 3, 12, 14, 7, 17, 2, 12, 13, 10,
+    15, 10, 9, 8, 11, 2, 8, 16, 11, 14, 2, 17, 9, 15, 9, 15, 13, 14, 13, 14, 16, 17, 16, 17,
 )
 
 
@@ -400,7 +400,8 @@
 
     pl.semaphore_wait(barrier, len(column) - 1 + len(across))
 
-    half, spot = sq // spread, sq % spread
+    half, spot = sq % 2, sq // 2
+    near = sq // 2
 
     def block(i):
         return pl.ds(pl.multiple_of(i * length, length), length)
@@ -423,7 +424,7 @@
         pl.when(jnp.logical_not(local))(remote)
 
     stays = [jnp.logical_and(half == side, sq == rows * side + r) for r in range(rows)]
-    comes = [jnp.logical_and(sq // rows == side, side * spread + b == sq) for b in range(spread)]
+    comes = [jnp.logical_and(sq // rows == side, 2 * b + side == sq) for b in range(spread)]
 
     def x_local(r, at):
         return pltpu.make_async_copy(x_ref.at[r], xf.at[block(at)], gl.at[0])
@@ -450,42 +451,40 @@
             lambda r=r, at=at: x_copy(r, spot, (pair + half, rows * side + r), at).start(),
         )
 
-    for b in range(spread):
+    def token_block(which):
+        return pl.ds(pl.multiple_of(which, tokens), tokens)
+
+    def cols(i, n=256):
+        return pl.ds(pl.multiple_of(i * n, 128), n)
+
+    def arrive(b):
         split(
-            comes[b],
-            lambda b=b: x_local(b, side * spread + b).wait(),
-            lambda b=b: x_copy(0, b, sibling, side * spread + b).wait_recv(),
+            jnp.logical_and(sq // rows == side, 2 * b + side == sq),
+            lambda: x_local(0, side * spread + b).wait(),
+            lambda: x_copy(0, b, sibling, side * spread + b).wait_recv(),
         )
         forward(b, side * spread).start()
-    for r in range(rows):
-        split(
-            stays[r],
-            lambda r=r: c_local(r, spot).start(),
-            lambda r=r: c_copy(r, spot, (pair + half, rows * side + r)).start(),
-        )
-
-    def token_block(which):
-        return pl.ds(pl.multiple_of(which, tokens), tokens)
-
-    def cols(i, n=256):
-        return pl.ds(pl.multiple_of(i * n, 128), n)
-
+
+    def project(b, of, also_query):
+        at = block(of * spread + b)
+
+        def body(i, _):
+            xb = xf[at]
+            c = cols(i)
+            if also_query:
+                qs[block(b), c] = (product(xb, wproj[0, :, c]) + bq[:, c]).astype(BF16) * BF16(0.125)
+            key[at, c] = product(xb, wproj[1, :, c]).astype(BF16)
+            val[at, c] = (product(xb, wproj[2, :, c]) + bv[:, c]).astype(BF16)
+            return 0
+
+        lax.fori_loop(0, D // 256, body, 0, unroll=3)
+
+    arrive(near)
     for name in ("vectors", "q", "k", "v"):
         loaded(name)
-
-    def project(which, also_query):
-        def body(i, _):
-            xb = xf[token_block(which)]
-            c = cols(i)
-            if also_query:
-                qs[:, c] = (product(xb, wproj[0, :, c]) + bq[:, c]).astype(BF16) * BF16(0.125)
-            key[token_block(which), c] = product(xb, wproj[1, :, c]).astype(BF16)
-            val[token_block(which), c] = (product(xb, wproj[2, :, c]) + bv[:, c]).astype(BF16)
-            return 0
-
-        lax.fori_loop(0, D // 256, body, 0, unroll=3)
-
-    project(own, True)
+    project(near, side, True)
+    forward(near, (1 - side) * spread).wait_recv()
+    project(near, 1 - side, False)
 
     for p in range(seq_size):
         split(
@@ -497,15 +496,23 @@
         jnp.int32, (length, length), 1
     )
     for b in range(spread):
-        mine_seg = jnp.broadcast_to(sg[side * spread + b], (length, length))
+        mine_seg = jnp.broadcast_to(sg[2 * b + side], (length, length))
         column = jnp.sum(jnp.where(diagonal, mine_seg, 0), axis=1, keepdims=True)
         for p in range(seq_size):
+            at = (p % 2) * spread + p // 2
             seen = jnp.broadcast_to(column, (length, length)) == jnp.broadcast_to(sg[p], (length, length))
-            mask[b * length : (b + 1) * length, p * length : (p + 1) * length] = jnp.where(seen, 0.0, MASKED)
-
-    for b in range(spread):
-        forward(b, (1 - side) * spread).wait_recv()
-    project(far, False)
+            mask[b * length : (b + 1) * length, at * length : (at + 1) * length] = jnp.where(seen, 0.0, MASKED)
+
+    arrive(1 - near)
+    for r in range(rows):
+        split(
+            stays[r],
+            lambda r=r: c_local(r, spot).start(),
+            lambda r=r: c_copy(r, spot, (pair + half, rows * side + r)).start(),
+        )
+    project(1 - near, side, True)
+    forward(1 - near, (1 - side) * spread).wait_recv()
+    project(1 - near, 1 - side, False)
 
     lane = lax.broadcasted_iota(jnp.int32, (1, 128), 1)
     first = (lane < HD).astype(BF16)
@@ -551,7 +558,7 @@
         hid[r] = (n * g1[...] + s1[...]).astype(BF16)
         return 0
 
-    lax.fori_loop(0, tokens // step, norm_one, 0, unroll=2)
+    lax.fori_loop(0, tokens // step, norm_one, 0, unroll=4)
 
     loaded("in")
     loaded("out")
@@ -566,7 +573,7 @@
             v = product(hid[...], inner_cols(j, i)[...]) + bi[:, c]
             cdf = 0.5 * (1.0 + lax.erf(v * INV_ROOT_TWO))
             active[:, c] = (v * cdf).astype(BF16)
-            slope[:, c] = cdf + v * DENSITY * jnp.exp(-0.5 * v * v)
+            slope[:, c] = v
             return 0
 
         lax.fori_loop(0, 3, expand, 0, unroll=3)
@@ -601,11 +608,11 @@
         return d_gain + fold(g * n), d_shift + fold(g), d_bias + fold(grad_low.astype(F32))
 
     zero = jnp.zeros((8, D), F32)
-    sums = lax.fori_loop(0, tokens // step, norm_two, (zero, zero, zero), unroll=2)
+    sums = lax.fori_loop(0, tokens // step, norm_two, (zero, zero, zero), unroll=4)
     for at, v in zip((6, 7, 5), sums):
         small[0, at : at + 1] = jnp.sum(v, axis=0, keepdims=True)
 
-    homes = [(pair + sq // rows, side * spread + b) for b in range(spread)]
+    homes = [(pair + sq // rows, 2 * b + side) for b in range(spread)]
     at_home = [jnp.logical_and(h[0] == dp, h[1] == sq) for h in homes]
 
     def back(src, dst, b, lane_, to, slot):
@@ -667,7 +674,9 @@
         def body(i, _):
             t = j * 3 + i
             up = product_nt(gout[...], total[pl.ds(pl.multiple_of(PROJ + t * 256, 256), 256)])
-            gi = (up * slope[:, cols(t)]).astype(BF16)
+            v = slope[:, cols(t)]
+            cdf = 0.5 * (1.0 + lax.erf(v * INV_ROOT_TWO))
+            gi = (up * (cdf + v * DENSITY * jnp.exp(-0.5 * v * v))).astype(BF16)
             small[0, 8 + j : 9 + j, cols(i)] = jnp.sum(fold(gi.astype(F32)), axis=0, keepdims=True)
             view = inner_cols(j, i)
             acc[...] += product_nt(gi, view[...])
@@ -910,7 +919,7 @@
             wide[slot, pl.ds(pl.multiple_of(i * 32, 32), 32)] = sums[pl.ds(pl.multiple_of(at + i * 32, 32), 32)].astype(F32)
             return 0
 
-        lax.fori_loop(0, step // 32, body, 0)
+        lax.fori_loop(0, step // 32, body, 0, unroll=4)
         copies.append(pltpu.make_async_copy(wide.at[slot], view, sem.at[slot]))
         copies[-1].start()
     for c in copies[-4:] + rows:

time: 158 us -> 153 us (0.968)
  Pallas kernels: 157 us -> 152 us
    pallas_call x1, Pallas kernels: 147 us -> 142 us  [whole_layer(): pl.pallas_call(functools.partial(layer_kernel, plan, seq_size), out_shape...]
where the time goes in v6:
time: 153 us
  Pallas kernels  152 us (99%)
    pallas_call x1, Pallas kernels, whole_layer(): pl.pallas_call(functools.partial(layer_kernel, plan, seq_size), out_shape...  142 us
    pallas_call x1, Pallas kernels, widen(): pl.pallas_call(widen_kernel, out_shape=shapes, in_specs=[vmem] * 4, out_s...  10.2 us

profile of v6, /device:TPU:0, one launch (start us, length us, event | category | flops | bytes accessed | tf_op | source)
XLA Modules:
  0.0 152.6 jit_solution(14929088329463745645)
XLA Ops:
  0.7 141.5 %layer.1 = (bf16[9216,768]{1,0:T(8,128)(2,1)S(1)}, f32[16,768]{1,0:T(8,128)S(1)}, bf16[2,128,768]{2,1,0:T(8,128)(2,1)S(1)}, bf16[2,128,768]{2,1,0:T(8,128)(2,1)S(1)}) custom-call(bf16[2,128,768]{2,1,0:T(8,128)(2,1)} %refs_0_.1, bf16[2,128,768]{2,1,0:T(8,128)(2,1)} %refs_1_.1, s32[2,1,128]{2,1,0:T(1,128)} %bitcast.1, bf16[768,768]{1,0:T(8,128)(2,1)} %refs_3_.1, ...), custom_call_target="tpu_custom_call" | custom-call | tf_op jit(solution)/shard_map/layer/pallas_call | solution.py:846
  142.2 10.2 %widen.1 = (bf16[2,128,768]{2,1,0:T(8,128)(2,1)}, bf16[2,128,768]{2,1,0:T(8,128)(2,1)}, f32[768,768]{1,0:T(8,128)}, f32[768]{0:T(1024)}, f32[768,768]{1,0:T(8,12...) custom-call(bf16[9216,768]{1,0:T(8,128)(2,1)S(1)} %get-tuple-element, ...), custom_call_target="tpu_custom_call" | custom-call | tf_op jit(solution)/shard_map/widen/pallas_call | solution.py:938

commit v7 on v6

--- a/solution.py
+++ b/solution.py
@@ -522,14 +522,16 @@
     def attend(i, _):
         c = cols(i, 128)
         qp, kp, vp = qs[:, c], key[:, c], val[:, c]
-        outs = []
+        both = jnp.concatenate([qp * picks[0], qp * picks[1]], axis=0)
+        s = product_nt(both, kp)
         for n in range(2):
-            s = product_nt(qp * picks[n], kp) + mask[...]
-            e = jnp.exp(s - jnp.max(s, axis=-1, keepdims=True))
-            p = (e * (1.0 / jnp.sum(e, axis=-1, keepdims=True))).astype(BF16)
-            probs[2 * i + n] = p
-            outs.append(product(p, vp))
-        attn[:, c] = jnp.where(low_lanes, outs[0], outs[1]).astype(BF16)
+            t = s[n * tokens : (n + 1) * tokens] + mask[...]
+            e = jnp.exp(t - jnp.max(t, axis=-1, keepdims=True))
+            probs[pl.ds(pl.multiple_of((2 * i + n) * tokens, tokens), tokens)] = (
+                e * (1.0 / jnp.sum(e, axis=-1, keepdims=True))
+            ).astype(BF16)
+        out = product(probs[pl.ds(pl.multiple_of(2 * i * tokens, 2 * tokens), 2 * tokens)], vp)
+        attn[:, c] = jnp.where(low_lanes, out[:tokens], out[tokens:]).astype(BF16)
         return 0
 
     lax.fori_loop(0, D // 128, attend, 0, unroll=3)
@@ -716,19 +718,16 @@
             i = n * 2 + m
             c = cols(i, 128)
             qp, kp, vp, gp = qs[:, c], key[:, c], val[:, c], cot[:, c]
-            dq, dk, dv = [], [], []
-            for h in range(2):
-                p = probs[2 * i + h]
-                pf = p.astype(F32)
-                weighted = pf * product_nt(gp * picks[h], vp)
-                delta = jnp.sum(weighted, axis=-1, keepdims=True)
-                gs = (weighted - pf * delta).astype(BF16)
-                dq.append(product(gs, kp))
-                dk.append(product_tn(gs, qp))
-                dv.append(product_tn(p, gp))
-            gq = (jnp.where(low_lanes, dq[0], dq[1]) * 0.125).astype(BF16)
-            gk = jnp.where(low_lanes, dk[0], dk[1]).astype(BF16)
-            gv = jnp.where(low_lanes, dv[0], dv[1]).astype(BF16)
+            queries = jnp.concatenate([qp * picks[0], qp * picks[1]], axis=0)
+            grads = jnp.concatenate([gp * picks[0], gp * picks[1]], axis=0)
+            p = probs[pl.ds(pl.multiple_of(2 * i * tokens, 2 * tokens), 2 * tokens)]
+            pf = p.astype(F32)
+            weighted = pf * product_nt(grads, vp)
+            gs = (weighted - pf * jnp.sum(weighted, axis=-1, keepdims=True)).astype(BF16)
+            dq = product(gs, kp)
+            gq = (jnp.where(low_lanes, dq[:tokens], dq[tokens:]) * 0.125).astype(BF16)
+            gk = product_tn(gs, queries).astype(BF16)
+            gv = product_tn(p, grads).astype(BF16)
             qs[:, c] = gq
             small[0, 0:1, c] = jnp.sum(fold(gq.astype(F32)), axis=0, keepdims=True)
             small[0, 1:2, c] = jnp.sum(fold(gv.astype(F32)), axis=0, keepdims=True)
@@ -856,7 +855,7 @@
             pltpu.VMEM((tokens, D), BF16),
             pltpu.VMEM((2 * tokens, D), BF16),
             pltpu.VMEM((2 * tokens, D), BF16),
-            pltpu.VMEM((D // HD, tokens, 2 * tokens), BF16),
+            pltpu.VMEM((D // HD * tokens, 2 * tokens), BF16),
             pltpu.VMEM((tokens, D), BF16),
             pltpu.VMEM((tokens, D), F32),
             pltpu.VMEM((tokens, 128), F32),

time: 153 us -> 151 us (0.987)
  Pallas kernels: 152 us -> 150 us
    pallas_call x1, Pallas kernels: 142 us -> 140 us  [whole_layer(): pl.pallas_call(functools.partial(layer_kernel, plan, seq_size), out_shape...]
where the time goes in v7:
time: 151 us
  Pallas kernels  150 us (99%)
    pallas_call x1, Pallas kernels, whole_layer(): pl.pallas_call(functools.partial(layer_kernel, plan, seq_size), out_shape...  140 us
    pallas_call x1, Pallas kernels, widen(): pl.pallas_call(widen_kernel, out_shape=shapes, in_specs=[vmem] * 4, out_s...  10.2 us

profile of v7, /device:TPU:0, one launch (start us, length us, event | category | flops | bytes accessed | tf_op | source)
XLA Modules:
  0.0 150.7 jit_solution(6494410782111666517)
XLA Ops:
  0.7 139.6 %layer.1 = (bf16[9216,768]{1,0:T(8,128)(2,1)S(1)}, f32[16,768]{1,0:T(8,128)S(1)}, bf16[2,128,768]{2,1,0:T(8,128)(2,1)S(1)}, bf16[2,128,768]{2,1,0:T(8,128)(2,1)S(1)}) custom-call(bf16[2,128,768]{2,1,0:T(8,128)(2,1)} %refs_0_.1, bf16[2,128,768]{2,1,0:T(8,128)(2,1)} %refs_1_.1, s32[2,1,128]{2,1,0:T(1,128)} %bitcast.1, bf16[768,768]{1,0:T(8,128)(2,1)} %refs_3_.1, ...), custom_call_target="tpu_custom_call" | custom-call | tf_op jit(solution)/shard_map/layer/pallas_call | solution.py:845
  140.3 10.2 %widen.1 = (bf16[2,128,768]{2,1,0:T(8,128)(2,1)}, bf16[2,128,768]{2,1,0:T(8,128)(2,1)}, f32[768,768]{1,0:T(8,128)}, f32[768]{0:T(1024)}, f32[768,768]{1,0:T(8,12...) custom-call(bf16[9216,768]{1,0:T(8,128)(2,1)S(1)} %get-tuple-element, ...), custom_call_target="tpu_custom_call" | custom-call | tf_op jit(solution)/shard_map/widen/pallas_call | solution.py:937

commit v8 on v7

--- a/solution.py
+++ b/solution.py
@@ -534,7 +534,7 @@
         attn[:, c] = jnp.where(low_lanes, out[:tokens], out[tokens:]).astype(BF16)
         return 0
 
-    lax.fori_loop(0, D // 128, attend, 0, unroll=3)
+    lax.fori_loop(0, D // 128, attend, 0, unroll=6)
 
     loaded("o")
 

time: 151 us -> 151 us (level)
  no operation moved by 1% of the time
where the time goes in v8:
time: 151 us; the launch traced here: 150 us
  Pallas kernels  150 us (99%)
    pallas_call x1, Pallas kernels, whole_layer(): pl.pallas_call(functools.partial(layer_kernel, plan, seq_size), out_shape...  139 us
    pallas_call x1, Pallas kernels, widen(): pl.pallas_call(widen_kernel, out_shape=shapes, in_specs=[vmem] * 4, out_s...  10.2 us

profile of v8, /device:TPU:0, one launch (start us, length us, event | category | flops | bytes accessed | tf_op | source)
XLA Modules:
  0.0 150.5 jit_solution(7019433681155701062)
XLA Ops:
  0.7 139.4 %layer.1 = (bf16[9216,768]{1,0:T(8,128)(2,1)S(1)}, f32[16,768]{1,0:T(8,128)S(1)}, bf16[2,128,768]{2,1,0:T(8,128)(2,1)S(1)}, bf16[2,128,768]{2,1,0:T(8,128)(2,1)S(1)}) custom-call(bf16[2,128,768]{2,1,0:T(8,128)(2,1)} %refs_0_.1, bf16[2,128,768]{2,1,0:T(8,128)(2,1)} %refs_1_.1, s32[2,1,128]{2,1,0:T(1,128)} %bitcast.1, bf16[768,768]{1,0:T(8,128)(2,1)} %refs_3_.1, ...), custom_call_target="tpu_custom_call" | custom-call | tf_op jit(solution)/shard_map/layer/pallas_call | solution.py:845
  140.1 10.2 %widen.1 = (bf16[2,128,768]{2,1,0:T(8,128)(2,1)}, bf16[2,128,768]{2,1,0:T(8,128)(2,1)}, f32[768,768]{1,0:T(8,128)}, f32[768]{0:T(1024)}, f32[768,768]{1,0:T(8,12...) custom-call(bf16[9216,768]{1,0:T(8,128)(2,1)S(1)} %get-tuple-element, ...), custom_call_target="tpu_custom_call" | custom-call | tf_op jit(solution)/shard_map/widen/pallas_call | solution.py:937
